TPU v7x, 256 devices: a whole 4x4x8 slice. The times are simulated.
256 devices in a mesh: blk: 64 (over z, y, core), rep: 4 (over x).
Axes of the slice: x: 4, y: 4, z: 8, core: 2. Of those that a mesh axis runs over, the one named last changes fastest.
Arguments:
- saved_inputs: bfloat16 [2, 65536, 256], P(None, ('rep', 'blk')), parts along dimension 1, may hold values from -6 to 6
- output_grads: bfloat16 [65536, 256], P(('rep', 'blk')), parts along dimension 0, may hold values from -6 to 6
- owner_ids: int32 [2, 65536, 1], P(None, 'rep'), parts along dimension 1, may hold values from 0 to 63; in each aligned block of 256 rows (0 to 255, 256 to 511, ..., all dimensions but the last counted through in order) at most 8 rows name the same one
- attend_weight: bfloat16 [2, 256, 768], replicated, may hold values from -8 to 8
- output_weight: bfloat16 [2, 256, 256], replicated, may hold values from -0.375 to 0.375
- up_weight: bfloat16 [2, 256, 1024], replicated, may hold values from -0.375 to 0.375
- down_weight: bfloat16 [2, 1024, 256], replicated, may hold values from -0.1875 to 0.1875
Outputs:
- input_grads: bfloat16 [65536, 256], P(('rep', 'blk')), parts along dimension 0
There are 4 independent parts, one for each index of `rep`. A program takes and returns all parts, laid end to end along the dimension named above; an argument that names none is the same for every part. Nothing has to cross between parts.
Inputs may be any that keep to these rules, and one draw needn't show every extreme that they name: `owner_ids`: in each layer, at most 8 of the points of one device have the same owner, and in every draw some device's points name one owner exactly 8 times.
All inputs are finite; a program needn't handle non-finite values.
Results may differ from a plain program's by a relative error of at most 0.02.
The roundings to bfloat16 on the way count: a program that leaves them out, or rounds other values in their place, can miss the bound.
Values may be sent and summed in bfloat16 or wider, within the bound.
No kernel may reach another device: no remote copies, remote signals or barrier semaphores. Data moves between devices by JAX's collectives and lax.ppermute only.
A program may use at most 64 MiB of HBM per device.

v0:
```python
import jax
import jax.numpy as jnp
from jax import lax
from jax.experimental import pallas as pl
from jax.experimental.pallas import tpu as pltpu
from jax.sharding import PartitionSpec as P

D = 256
HEADS = 8
HD = D // HEADS
EPSILON = 1e-05
MASKED = -1e30
SCALE = HD ** (-0.5)
LOG2E = 1.4426950408889634
BF = jnp.bfloat16
F32 = jnp.float32


def mm(left, right):
    return lax.dot_general(left, right, (((1,), (0,)), ((), ())), preferred_element_type=F32)


def mm_t(left, right):
    return lax.dot_general(left, right, (((1,), (1,)), ((), ())), preferred_element_type=F32)


def iota(shape, axis):
    return lax.broadcasted_iota(jnp.int32, shape, axis)


def vmem_call(kernel, outs, name, limit=40 << 20):
    return pl.pallas_call(
        kernel,
        out_shape=outs,
        name=name,
        compiler_params=pltpu.CompilerParams(vmem_limit_bytes=limit),
    )


def destination_row(own_row):
    points = own_row.shape[1]
    rows, cols = iota((points, points), 0), iota((points, points), 1)
    wide = jnp.broadcast_to(own_row, (points, points))
    own_col = jnp.sum(jnp.where(rows == cols, wide, 0.0), axis=1, keepdims=True)
    same = jnp.where((own_col == wide) & (rows < cols), 1.0, 0.0)
    rank = jnp.sum(same, axis=0, keepdims=True)
    return own_row * 8.0 + rank


def one_hot(dest_row, slots):
    shape = (slots, dest_row.shape[1])
    return jnp.where(iota(shape, 0).astype(F32) == dest_row, 1.0, 0.0).astype(BF)


def key_bias(owners, my_index):
    devices = owners.shape[0]
    count = jnp.sum(jnp.where(owners == my_index, 1.0, 0.0), axis=1, keepdims=True)
    shape = (devices * 8, devices)
    spread = jnp.where(iota(shape, 0) // 8 == iota(shape, 1), 1.0, 0.0).astype(BF)
    slot_count = mm(spread, jnp.broadcast_to(count, (devices, 128)).astype(BF))
    rank = (iota(slot_count.shape, 0) % 8).astype(F32)
    return jnp.where(rank < slot_count, 0.0, MASKED).astype(BF)


def route_first_kernel(index_ref, owners_ref, x_ref, dest_ref, out_ref):
    my = index_ref[0]
    dest = destination_row(owners_ref[pl.ds(my, 1), :].astype(F32))
    dest_ref[...] = jnp.broadcast_to(dest, dest_ref.shape)
    out_ref[...] = mm(one_hot(dest, out_ref.shape[0]), x_ref[...]).astype(BF)


def route_second_kernel(
    index_ref, owners_one_ref, owners_zero_ref, dest_one_ref, g_ref, x_ref, dest_ref, out_ref, bias_ref
):
    my = index_ref[0]
    slots = out_ref.shape[0]
    out_ref[:, :D] = mm(one_hot(dest_one_ref[0:1, :], slots), g_ref[...]).astype(BF)
    dest = destination_row(owners_zero_ref[pl.ds(my, 1), :].astype(F32))
    dest_ref[...] = jnp.broadcast_to(dest, dest_ref.shape)
    out_ref[:, D:] = mm(one_hot(dest, slots), x_ref[...]).astype(BF)
    bias_ref[1] = key_bias(owners_one_ref[...], my)
    bias_ref[0] = key_bias(owners_zero_ref[...], my)


def unpack(dest_row, rows):
    hot = one_hot(dest_row, rows.shape[0])
    return lax.dot_general(hot, rows, (((0,), (0,)), ((), ())), preferred_element_type=F32).astype(BF)


def repack_kernel(dest_one_ref, dest_zero_ref, rows_ref, out_ref):
    gradient = unpack(dest_one_ref[0:1, :], rows_ref[...])
    out_ref[...] = mm(one_hot(dest_zero_ref[0:1, :], out_ref.shape[0]), gradient).astype(BF)


def unpack_kernel(dest_ref, rows_ref, out_ref):
    out_ref[...] = unpack(dest_ref[0:1, :], rows_ref[...])


def normalized(values):
    centered = values - jnp.mean(values, axis=1, keepdims=True)
    inverse = lax.rsqrt(jnp.mean(centered * centered, axis=1, keepdims=True) + EPSILON)
    return centered * inverse, inverse


def norm_gradient(upstream, hat, inverse):
    mean_one = jnp.mean(upstream, axis=1, keepdims=True)
    mean_two = jnp.mean(upstream * hat, axis=1, keepdims=True)
    return inverse * (upstream - mean_one - hat * mean_two)


def head_lanes(shape, head):
    lane = iota(shape, 1)
    return (lane >= head * HD) & (lane < head * HD + HD)


def gelu_slope(pre):
    root, cubic = 0.7978845608028654, 0.044715
    square = pre * pre
    bend = jnp.tanh(root * (pre + cubic * (pre * square)))
    return 0.5 * (1.0 + bend) + 0.5 * pre * (1.0 - bend * bend) * (root * (1.0 + 3.0 * cubic * square))


def forward_kernel(
    x_ref, bias_ref, attend_ref, output_ref, up_ref,
    qkv_ref, probs_ref, hat_ref, inverse_ref, slope_ref,
    value_t_ref, mixed_t_ref,
):
    x = x_ref[...].astype(F32)
    normed, _ = normalized(x)
    qkv = mm(normed.astype(BF), attend_ref[...]).astype(BF)
    qkv_ref[...] = qkv
    value_t_ref[...] = qkv[:, 2 * D :].T
    slots = x.shape[0]

    def one_head(head, carry):
        spare = jnp.where(head == 0, D - 1, 0)
        lane = iota((slots, D), 1)
        bias = jnp.concatenate([bias_ref[...], bias_ref[...]], axis=1)
        keys = jnp.where(
            head_lanes((slots, D), head),
            qkv_ref[:, D : 2 * D],
            jnp.where(lane == spare, bias, jnp.zeros_like(bias)),
        )
        queries = jnp.where(lane == spare, jnp.ones((slots, D), BF), qkv_ref[:, :D])
        scores = mm_t(keys, queries)
        largest = jnp.max(scores, axis=0, keepdims=True)
        exponent = jnp.exp2((scores - largest) * (SCALE * LOG2E))
        total = jnp.sum(exponent, axis=0, keepdims=True)
        probs = (exponent * (1.0 / total)).astype(BF)
        probs_ref[head] = probs
        at = pl.multiple_of(head * HD, HD)
        mixed_t_ref[pl.ds(at, HD), :] = mm(value_t_ref[pl.ds(at, HD), :], probs)
        return carry

    lax.fori_loop(0, HEADS, one_head, 0)
    attended = mixed_t_ref[...].astype(BF).T
    mixed = mm(attended, output_ref[...]).astype(BF).astype(F32)
    hat, inverse = normalized(x + mixed)
    hat_ref[...] = hat
    inverse_ref[...] = inverse
    slope_ref[...] = gelu_slope(mm(hat.astype(BF), up_ref[...]))


def backward_kernel(
    x_ref, g_ref, qkv_ref, probs_ref, hat_ref, inverse_ref, slope_ref,
    attend_ref, output_ref, up_ref, down_ref,
    out_ref,
    key_t_ref, query_grad_ref, key_grad_ref, value_grad_ref, up_grad_ref,
):
    g = g_ref[...]
    slots = g.shape[0]
    pre_grad = (slope_ref[...] * mm_t(g, down_ref[...])).astype(BF)
    grad_mid = (
        g.astype(F32) + norm_gradient(mm_t(pre_grad, up_ref[...]), hat_ref[...], inverse_ref[...])
    ).astype(BF)
    up_grad_ref[...] = mm_t(grad_mid, output_ref[...]).astype(BF)
    key_t_ref[...] = qkv_ref[:, D : 2 * D].T
    key_grad_ref[...] = jnp.zeros_like(key_grad_ref)
    value_grad_ref[...] = jnp.zeros_like(value_grad_ref)

    def one_head(head, carry):
        inside = head_lanes((slots, D), head)
        zero = jnp.zeros((slots, D), BF)
        values = jnp.where(inside, qkv_ref[:, 2 * D :], zero)
        prob_grads = mm_t(values, up_grad_ref[...])
        rounded = probs_ref[head]
        probs = rounded.astype(F32)
        total = jnp.sum(prob_grads * probs, axis=0, keepdims=True)
        score_grads = (probs * (prob_grads - total)).astype(BF)
        value_grad_ref[...] += mm(rounded, jnp.where(inside, up_grad_ref[...], zero))
        key_grad_ref[...] += mm(score_grads, jnp.where(inside, qkv_ref[:, :D], zero))
        at = pl.multiple_of(head * HD, HD)
        query_grad_ref[pl.ds(at, HD), :] = mm(key_t_ref[pl.ds(at, HD), :], score_grads)
        return carry

    lax.fori_loop(0, HEADS, one_head, 0)
    query_grads = (query_grad_ref[...] * SCALE).astype(BF).T
    key_grads = (key_grad_ref[...] * SCALE).astype(BF)
    value_grads = value_grad_ref[...].astype(BF)
    normed_grads = (
        mm_t(query_grads, attend_ref[:, :D])
        + mm_t(key_grads, attend_ref[:, D : 2 * D])
        + mm_t(value_grads, attend_ref[:, 2 * D :])
    )
    hat, inverse = normalized(x_ref[...].astype(F32))
    branch = norm_gradient(normed_grads, hat, inverse).astype(BF)
    out_ref[...] = (grad_mid.astype(F32) + branch.astype(F32)).astype(BF)


def forward(x, bias, attend, output, up):
    slots = x.shape[0]
    hidden = up.shape[1]
    return pl.pallas_call(
        forward_kernel,
        out_shape=(
            jax.ShapeDtypeStruct((slots, 3 * D), BF),
            jax.ShapeDtypeStruct((HEADS, slots, slots), BF),
            jax.ShapeDtypeStruct((slots, D), F32),
            jax.ShapeDtypeStruct((slots, 1), F32),
            jax.ShapeDtypeStruct((slots, hidden), F32),
        ),
        scratch_shapes=[pltpu.VMEM((D, slots), BF), pltpu.VMEM((D, slots), F32)],
        name="layer_forward",
        compiler_params=pltpu.CompilerParams(vmem_limit_bytes=40 << 20),
    )(x, bias, attend, output, up)


def backward(x, g, saved, attend, output, up, down):
    slots = x.shape[0]
    return pl.pallas_call(
        backward_kernel,
        out_shape=jax.ShapeDtypeStruct((slots, D), BF),
        scratch_shapes=[
            pltpu.VMEM((D, slots), BF),
            pltpu.VMEM((D, slots), F32),
            pltpu.VMEM((slots, D), F32),
            pltpu.VMEM((slots, D), F32),
            pltpu.VMEM((slots, D), BF),
        ],
        name="layer_backward",
        compiler_params=pltpu.CompilerParams(vmem_limit_bytes=40 << 20),
    )(x, g, *saved, attend, output, up, down)


def per_device(saved_inputs, output_grads, owner_ids, attend, output, up, down):
    devices = lax.axis_size("blk")
    points = saved_inputs.shape[1]
    slots = devices * 8
    my_index = lax.axis_index("blk").astype(jnp.int32).reshape(1)
    owners = owner_ids.reshape(2, devices, points)

    def exchange(rows):
        width = rows.shape[1]
        moved = lax.all_to_all(
            rows.reshape(devices, 8, width), "blk", split_axis=0, concat_axis=0, tiled=True
        )
        return moved.reshape(slots, width)

    smem = pl.BlockSpec(memory_space=pltpu.SMEM)
    vmem = pl.BlockSpec(memory_space=pltpu.VMEM)
    dest_shape = jax.ShapeDtypeStruct((8, points), F32)
    dest_one, packed_x = pl.pallas_call(
        route_first_kernel,
        out_shape=(dest_shape, jax.ShapeDtypeStruct((slots, D), BF)),
        in_specs=[smem, vmem, vmem],
        name="route_first",
    )(my_index, owners[1], saved_inputs[1])
    x_one = exchange(packed_x)
    dest_zero, packed_gx, bias = pl.pallas_call(
        route_second_kernel,
        out_shape=(
            dest_shape,
            jax.ShapeDtypeStruct((slots, 2 * D), BF),
            jax.ShapeDtypeStruct((2, slots, 128), BF),
        ),
        in_specs=[smem] + [vmem] * 5,
        name="route_second",
    )(my_index, owners[1], owners[0], dest_one, output_grads, saved_inputs[0])
    gx = exchange(packed_gx)
    saved_one = forward(x_one, bias[1], attend[1], output[1], up[1])
    result = backward(x_one, gx[:, :D], saved_one, attend[1], output[1], up[1], down[1])
    returned = exchange(result)
    x_zero = gx[:, D:]
    saved_zero = forward(x_zero, bias[0], attend[0], output[0], up[0])
    packed_g = vmem_call(repack_kernel, jax.ShapeDtypeStruct((slots, D), BF), "repack")(
        dest_one, dest_zero, returned
    )
    g_zero = exchange(packed_g)
    result = backward(x_zero, g_zero, saved_zero, attend[0], output[0], up[0], down[0])
    returned = exchange(result)
    return vmem_call(unpack_kernel, jax.ShapeDtypeStruct((points, D), BF), "unpack")(
        dest_zero, returned
    )


def solution(mesh):
    placed = (
        P(None, ("rep", "blk"), None),
        P(("rep", "blk"), None),
        P(None, "rep", None),
        P(),
        P(),
        P(),
        P(),
    )
    return jax.shard_map(
        per_device, mesh=mesh, in_specs=placed, out_specs=P(("rep", "blk"), None), check_vma=False
    )
```

profile of v0, /device:TPU:1, one launch (start us, length us, event | category | flops | bytes accessed | tf_op | source)
XLA Modules:
  0.0 153.8 jit_solution(14049092486000157968)
XLA Ops:
  0.0 1.3 slice_reduce_fusion
  1.9 1.7 %slice_bitcast_fusion.10 = (bf16[256,256]{1,0:T(8,128)(2,1)}, bf16[256,256]{1,0:T(8,128)(2,1)}) fusion(bf16[2,256,256]{2,1,0:T(8,128)(2,1)} %param.7), kind=kLoop, calls=%fused_computation.10 | loop fusion | bytes 524288 | tf_op jit(solution)/shard_map/squeeze | solution.py:278
  3.6 2.0 %route_first.1 = (f32[8,256]{1,0:T(8,128)}, bf16[512,256]{1,0:T(8,128)(2,1)}) custom-call(s32[1]{0:T(128)} %bitcast.index_ref, s32[64,256]{1,0:T(8,128)} %squeeze.49.owners_ref.owners_one_ref, bf16[256,256]{1,0:T(8,128)(2,1)} %get-tuple-element.50.x_ref), custom_call_target="tpu_custom_call" | custom-call | tf_op jit(solution)/shard_map/route_first/pallas_call | solution.py:262
  5.5 13.1 %all-to-all-start.1 = ((bf16[64,8,256]{2,1,0:T(8,128)(2,1)}), bf16[64,8,256]{2,1,0:T(8,128)(2,1)S(1)}, u32[]{:S(2)}, u32[]{:S(2)}) async-start(bf16[64,8,256]{2,1,0:T(8,128)(2,1)} %bitcast.43), calls=%async_computation.1 | async-start | bytes 524288 | tf_op jit(solution)/shard_map/all_to_all | solution.py:254
  19.3 2.3 %route_second.1 = (f32[8,256]{1,0:T(8,128)}, bf16[512,512]{1,0:T(8,128)(2,1)}, bf16[2,512,128]{2,1,0:T(8,128)(2,1)}) custom-call(s32[1]{0:T(128)} %bitcast.index_ref, s32[64,256]{1,0:T(8,128)} %squeeze.49.owners_ref.owners_one_ref, s32[64,256]{1,0:T(8,128)} %squeeze.50.owners_zero_ref, f32[8,256]{1,0:T(8,128)} %get-tuple-element.20.dest_one_ref, ...), custom_call_target="tpu_custom_call" | custom-call | tf_op jit(solution)/shard_map/route_second/pallas_call | solution.py:269
  21.7 10.1 %all-to-all-done.1 = bf16[64,8,256]{2,1,0:T(8,128)(2,1)S(1)} async-done(((bf16[64,8,256]{2,1,0:T(8,128)(2,1)}), bf16[64,8,256]{2,1,0:T(8,128)(2,1)S(1)}, u32[]{:S(2)}, u32[]{:S(2)}) %all-to-all-start.1) | async-done | bytes 262176 | tf_op jit(solution)/shard_map/all_to_all | solution.py:254
  31.8 5.1 %all-to-all-start = ((bf16[64,8,512]{2,1,0:T(8,128)(2,1)}), bf16[64,8,512]{2,1,0:T(8,128)(2,1)}, u32[]{:S(2)}, u32[]{:S(2)}) async-start(bf16[64,8,512]{2,1,0:T(8,128)(2,1)} %bitcast.42), calls=%async_computation | async-start | bytes 1048576 | tf_op jit(solution)/shard_map/all_to_all | solution.py:254
  36.9 1.7 %slice_bitcast_fusion.7 = (bf16[512,128]{1,0:T(8,128)(2,1)}, bf16[512,128]{1,0:T(8,128)(2,1)S(1)}) fusion(bf16[2,512,128]{2,1,0:T(8,128)(2,1)} %get-tuple-element.24), kind=kLoop, calls=%fused_computation.7 | loop fusion | bytes 524288 | tf_op jit(solution)/shard_map/squeeze | solution.py:284
  38.6 1.0 slice_bitcast_fusion.6
  40.3 8.4 %layer_forward.2 = (bf16[512,768]{1,0:T(8,128)(2,1)S(1)}, bf16[8,512,512]{2,1,0:T(8,128)(2,1)S(1)}, f32[512,256]{1,0:T(8,128)S(1)}, f32[512,1]{1,0:T(8,128)S(1)}, f32[512,1024]{1,0:T(8,128)S(1)}) custom-call(bf16[512,256]{1,0:T(8,128)(2,1)S(1)} %bitcast.35, bf16[512,128]{1,0:T(8,128)(2,1)S(1)} %get-tuple-element.48.bias_ref, ...), custom_call_target="tpu_custom_call" | custom-call | tf_op jit(solution)/shard_map/layer_forward/pallas_call | solution.py:213
  48.7 2.0 %copy-done = bf16[8,512,512]{2,1,0:T(8,128)(2,1)} copy-done((bf16[8,512,512]{2,1,0:T(8,128)(2,1)}, bf16[8,512,512]{2,1,0:T(8,128)(2,1)S(1)}, u32[]{:S(2)}) %copy-start) | copy-done | bytes 4194328
  50.7 1.4 copy-done.4
  54.6 1.1 fusion
  55.7 2.2 %copy-done.1 = bf16[8,512,512]{2,1,0:T(8,128)(2,1)S(1)} copy-done((bf16[8,512,512]{2,1,0:T(8,128)(2,1)S(1)}, bf16[8,512,512]{2,1,0:T(8,128)(2,1)}, u32[]{:S(2)}) %copy-start.1) | copy-done | bytes 4194328
  57.9 1.6 %copy-done.5 = f32[512,1024]{1,0:T(8,128)S(1)} copy-done((f32[512,1024]{1,0:T(8,128)S(1)}, f32[512,1024]{1,0:T(8,128)}, u32[]{:S(2)}) %copy-start.5) | copy-done | bytes 2097176
  59.5 0.9 copy-done.9
  60.4 1.1 copy-done.11
  61.5 1.0 copy-done.15
  62.5 0.9 copy-done.18
  63.5 9.3 %layer_backward.2 = bf16[512,256]{1,0:T(8,128)(2,1)S(1)} custom-call(bf16[512,256]{1,0:T(8,128)(2,1)S(1)} %bitcast.36, bf16[512,256]{1,0:T(8,128)(2,1)S(1)} %get-tuple-element.43.g_ref, bf16[512,768]{1,0:T(8,128)(2,1)S(1)} %copy-done.11, bf16[8,512,512]{2,1,0:T(8,128)(2,1)S(1)} %copy-done.1, f32[512,256]{1,0:T(8,128)S(1)} %copy-done.15, ...), custom_call_target="tpu_custom_call" | custom-call | tf_op jit(solution)/shard_map/layer_backward/pallas_call | solution.py:230
  72.8 23.2 %all_to_all.25 = bf16[64,8,256]{2,1,0:T(8,128)(2,1)S(1)} all-to-all(bf16[64,8,256]{2,1,0:T(8,128)(2,1)S(1)} %bitcast.38), channel_id=1, replica_groups=mesh['blk'=64,'rep'=4] {'blk'}, dimensions={0} | all-to-all | bytes 524288 | tf_op jit(solution)/shard_map/all_to_all | solution.py:254
  95.9 1.3 repack.1
  97.2 4.8 %all-to-all-start.3 = ((bf16[64,8,256]{2,1,0:T(8,128)(2,1)}), bf16[64,8,256]{2,1,0:T(8,128)(2,1)S(1)}, u32[]{:S(2)}, u32[]{:S(2)}) async-start(bf16[64,8,256]{2,1,0:T(8,128)(2,1)} %bitcast.14), calls=%async_computation.3 | async-start | bytes 524288 | tf_op jit(solution)/shard_map/all_to_all | solution.py:254
  102.9 8.4 %layer_forward.3 = (bf16[512,768]{1,0:T(8,128)(2,1)S(1)}, bf16[8,512,512]{2,1,0:T(8,128)(2,1)S(1)}, f32[512,256]{1,0:T(8,128)S(1)}, f32[512,1]{1,0:T(8,128)S(1)}, f32[512,1024]{1,0:T(8,128)S(1)}) custom-call(bf16[512,256]{1,0:T(8,128)(2,1)S(1)} %get-tuple-element.44.x_ref, bf16[512,128]{1,0:T(8,128)(2,1)S(1)} %copy-done.16, ...), custom_call_target="tpu_custom_call" | custom-call | tf_op jit(solution)/shard_map/layer_forward/pallas_call | solution.py:213
  111.3 2.0 %copy-done.2 = bf16[8,512,512]{2,1,0:T(8,128)(2,1)} copy-done((bf16[8,512,512]{2,1,0:T(8,128)(2,1)}, bf16[8,512,512]{2,1,0:T(8,128)(2,1)S(1)}, u32[]{:S(2)}) %copy-start.2) | copy-done | bytes 4194328
  113.3 1.4 copy-done.6
  115.6 2.2 %copy-done.3 = bf16[8,512,512]{2,1,0:T(8,128)(2,1)S(1)} copy-done((bf16[8,512,512]{2,1,0:T(8,128)(2,1)S(1)}, bf16[8,512,512]{2,1,0:T(8,128)(2,1)}, u32[]{:S(2)}) %copy-start.3) | copy-done | bytes 4194328
  117.7 1.6 %copy-done.7 = f32[512,1024]{1,0:T(8,128)S(1)} copy-done((f32[512,1024]{1,0:T(8,128)S(1)}, f32[512,1024]{1,0:T(8,128)}, u32[]{:S(2)}) %copy-start.7) | copy-done | bytes 2097176
  119.3 1.1 copy-done.13
  120.5 9.3 %layer_backward.3 = bf16[512,256]{1,0:T(8,128)(2,1)S(1)} custom-call(bf16[512,256]{1,0:T(8,128)(2,1)S(1)} %get-tuple-element.44.x_ref, bf16[512,256]{1,0:T(8,128)(2,1)S(1)} %bitcast.37, bf16[512,768]{1,0:T(8,128)(2,1)S(1)} %copy-done.13, bf16[8,512,512]{2,1,0:T(8,128)(2,1)S(1)} %copy-done.3, f32[512,256]{1,0:T(8,128)S(1)} %get-tuple-element.32.hat_ref, ...), custom_call_target="tpu_custom_call" | custom-call | tf_op jit(solution)/shard_map/layer_backward/pallas_call | solution.py:230
  129.7 23.2 %all_to_all.26 = bf16[64,8,256]{2,1,0:T(8,128)(2,1)S(1)} all-to-all(bf16[64,8,256]{2,1,0:T(8,128)(2,1)S(1)} %bitcast.39), channel_id=1, replica_groups=mesh['blk'=64,'rep'=4] {'blk'}, dimensions={0} | all-to-all | bytes 524288 | tf_op jit(solution)/shard_map/all_to_all | solution.py:254
  152.9 0.9 unpack.1
  (42 shorter events, 6.3 us)
Async XLA Ops:
  0.0 39.6 %copy-start.23 = (bf16[2,256,768]{2,1,0:T(8,128)(2,1)S(1)}, bf16[2,256,768]{2,1,0:T(8,128)(2,1)}, u32[]{:S(2)}) copy-start(bf16[2,256,768]{2,1,0:T(8,128)(2,1)} %param.10) | copy-start | bytes 2359300
  0.0 39.7 %copy-start.21 = (bf16[2,256,1024]{2,1,0:T(8,128)(2,1)S(1)}, bf16[2,256,1024]{2,1,0:T(8,128)(2,1)}, u32[]{:S(2)}) copy-start(bf16[2,256,1024]{2,1,0:T(8,128)(2,1)} %param.12) | copy-start | bytes 3145732
  5.5 26.2 %all-to-all-start.1 = ((bf16[64,8,256]{2,1,0:T(8,128)(2,1)}), bf16[64,8,256]{2,1,0:T(8,128)(2,1)S(1)}, u32[]{:S(2)}, u32[]{:S(2)}) async-start(bf16[64,8,256]{2,1,0:T(8,128)(2,1)} %bitcast.43), calls=%async_computation.1 | async-start | bytes 524288 | tf_op jit(solution)/shard_map/all_to_all | solution.py:254
  31.8 22.8 %all-to-all-start = ((bf16[64,8,512]{2,1,0:T(8,128)(2,1)}), bf16[64,8,512]{2,1,0:T(8,128)(2,1)}, u32[]{:S(2)}, u32[]{:S(2)}) async-start(bf16[64,8,512]{2,1,0:T(8,128)(2,1)} %bitcast.42), calls=%async_computation | async-start | bytes 1048576 | tf_op jit(solution)/shard_map/all_to_all | solution.py:254
  36.9 2.9 %copy-start.22 = (bf16[2,1024,256]{2,1,0:T(8,128)(2,1)S(1)}, bf16[2,1024,256]{2,1,0:T(8,128)(2,1)}, u32[]{:S(2)}) copy-start(bf16[2,1024,256]{2,1,0:T(8,128)(2,1)} %param.13) | copy-start | bytes 3145732
  39.6 0.7 copy-start.8
  48.7 2.0 %copy-start = (bf16[8,512,512]{2,1,0:T(8,128)(2,1)}, bf16[8,512,512]{2,1,0:T(8,128)(2,1)S(1)}, u32[]{:S(2)}) copy-start(bf16[8,512,512]{2,1,0:T(8,128)(2,1)S(1)} %get-tuple-element.26.probs_ref) | copy-start | bytes 12582916
  50.7 1.4 copy-start.4
  52.0 0.9 copy-start.10
  52.9 0.9 copy-start.14
  53.8 0.7 copy-start.17
  55.7 2.2 %copy-start.1 = (bf16[8,512,512]{2,1,0:T(8,128)(2,1)S(1)}, bf16[8,512,512]{2,1,0:T(8,128)(2,1)}, u32[]{:S(2)}) copy-start(bf16[8,512,512]{2,1,0:T(8,128)(2,1)} %copy-done) | copy-start | bytes 12582916
  57.9 1.6 %copy-start.5 = (f32[512,1024]{1,0:T(8,128)S(1)}, f32[512,1024]{1,0:T(8,128)}, u32[]{:S(2)}) copy-start(f32[512,1024]{1,0:T(8,128)} %copy-done.4) | copy-start | bytes 6291460
  59.5 0.9 copy-start.9
  60.4 1.1 copy-start.11
  61.5 1.0 copy-start.15
  62.5 0.9 copy-start.18
  63.5 32.5 %copy-start.19 = (f32[8,256]{1,0:T(8,128)S(1)}, f32[8,256]{1,0:T(8,128)}, u32[]{:S(2)}) copy-start(f32[8,256]{1,0:T(8,128)} %get-tuple-element.21.dest_zero_ref.dest_ref) | copy-start | bytes 24580
  63.5 32.5 %copy-start.20 = (f32[8,256]{1,0:T(8,128)S(1)}, f32[8,256]{1,0:T(8,128)}, u32[]{:S(2)}) copy-start(f32[8,256]{1,0:T(8,128)} %get-tuple-element.20.dest_one_ref) | copy-start | bytes 24580
  97.2 18.3 %all-to-all-start.3 = ((bf16[64,8,256]{2,1,0:T(8,128)(2,1)}), bf16[64,8,256]{2,1,0:T(8,128)(2,1)S(1)}, u32[]{:S(2)}, u32[]{:S(2)}) async-start(bf16[64,8,256]{2,1,0:T(8,128)(2,1)} %bitcast.14), calls=%async_computation.3 | async-start | bytes 524288 | tf_op jit(solution)/shard_map/all_to_all | solution.py:254
  102.0 0.9 copy-start.16
  111.3 2.0 %copy-start.2 = (bf16[8,512,512]{2,1,0:T(8,128)(2,1)}, bf16[8,512,512]{2,1,0:T(8,128)(2,1)S(1)}, u32[]{:S(2)}) copy-start(bf16[8,512,512]{2,1,0:T(8,128)(2,1)S(1)} %get-tuple-element.31.probs_ref) | copy-start | bytes 12582916
  113.3 1.4 copy-start.6
  114.7 0.9 copy-start.12
  115.6 2.2 %copy-start.3 = (bf16[8,512,512]{2,1,0:T(8,128)(2,1)S(1)}, bf16[8,512,512]{2,1,0:T(8,128)(2,1)}, u32[]{:S(2)}) copy-start(bf16[8,512,512]{2,1,0:T(8,128)(2,1)} %copy-done.2) | copy-start | bytes 12582916
  117.7 1.6 %copy-start.7 = (f32[512,1024]{1,0:T(8,128)S(1)}, f32[512,1024]{1,0:T(8,128)}, u32[]{:S(2)}) copy-start(f32[512,1024]{1,0:T(8,128)} %copy-done.6) | copy-start | bytes 6291460
  119.3 1.1 copy-start.13
where the time goes:
time: 155 us; the launch traced here: 154 us
  blocking collectives  46.4 us (30%)
  Pallas kernels  41.8 us (27%)
  local copies, waits for them, and re-layouts  32.2 us (21%)
  starting transfers between devices  23 us (15%)
  waiting for transfers between devices  10.2 us (7%)
    all_to_all x2, blocking collectives, exchange(): lax.all_to_all(rows.reshape(devices, 8, width), 'blk', split_axis=0, conc...  46.4 us
    unnamed x48, local copies, waits for them, and re-layouts  24 us
    all_to_all x3, starting transfers between devices, exchange(): lax.all_to_all(rows.reshape(devices, 8, width), 'blk', split_axis=0, conc...  23 us
    pallas_call x2, Pallas kernels, backward(): pl.pallas_call(backward_kernel, out_shape=jax.ShapeDtypeStruct((slots, D)...  18.5 us
    pallas_call x2, Pallas kernels, forward(): pl.pallas_call(forward_kernel, out_shape=(jax.ShapeDtypeStruct((slots, 3...  16.8 us
    all_to_all x3, waiting for transfers between devices, exchange(): lax.all_to_all(rows.reshape(devices, 8, width), 'blk', split_axis=0, conc...  10.2 us
  transfers between devices with their start and end apart: 3, of which 2 were waited for; matrix products, arithmetic and copies ran while one was open for 2% of the time, Pallas kernels for 12%

commit v1 on v0

--- a/solution.py
+++ b/solution.py
@@ -62,24 +62,12 @@
     return jnp.where(rank < slot_count, 0.0, MASKED).astype(BF)
 
 
-def route_first_kernel(index_ref, owners_ref, x_ref, dest_ref, out_ref):
-    my = index_ref[0]
-    dest = destination_row(owners_ref[pl.ds(my, 1), :].astype(F32))
+def route_kernel(index_ref, owners_ref, x_ref, g_ref, dest_ref, out_ref):
+    dest = destination_row(owners_ref[pl.ds(index_ref[0], 1), :].astype(F32))
     dest_ref[...] = jnp.broadcast_to(dest, dest_ref.shape)
-    out_ref[...] = mm(one_hot(dest, out_ref.shape[0]), x_ref[...]).astype(BF)
-
-
-def route_second_kernel(
-    index_ref, owners_one_ref, owners_zero_ref, dest_one_ref, g_ref, x_ref, dest_ref, out_ref, bias_ref
-):
-    my = index_ref[0]
-    slots = out_ref.shape[0]
-    out_ref[:, :D] = mm(one_hot(dest_one_ref[0:1, :], slots), g_ref[...]).astype(BF)
-    dest = destination_row(owners_zero_ref[pl.ds(my, 1), :].astype(F32))
-    dest_ref[...] = jnp.broadcast_to(dest, dest_ref.shape)
-    out_ref[:, D:] = mm(one_hot(dest, slots), x_ref[...]).astype(BF)
-    bias_ref[1] = key_bias(owners_one_ref[...], my)
-    bias_ref[0] = key_bias(owners_zero_ref[...], my)
+    hot = one_hot(dest, out_ref.shape[0])
+    out_ref[:, :D] = mm(hot, x_ref[...]).astype(BF)
+    out_ref[:, D:] = mm(hot, g_ref[...]).astype(BF)
 
 
 def unpack(dest_row, rows):
@@ -88,7 +76,7 @@
 
 
 def repack_kernel(dest_one_ref, dest_zero_ref, rows_ref, out_ref):
-    gradient = unpack(dest_one_ref[0:1, :], rows_ref[...])
+    gradient = unpack(dest_one_ref[0:1, :], rows_ref[:, :D])
     out_ref[...] = mm(one_hot(dest_zero_ref[0:1, :], out_ref.shape[0]), gradient).astype(BF)
 
 
@@ -120,12 +108,10 @@
     return 0.5 * (1.0 + bend) + 0.5 * pre * (1.0 - bend * bend) * (root * (1.0 + 3.0 * cubic * square))
 
 
-def forward_kernel(
-    x_ref, bias_ref, attend_ref, output_ref, up_ref,
-    qkv_ref, probs_ref, hat_ref, inverse_ref, slope_ref,
-    value_t_ref, mixed_t_ref,
+def forward_part(
+    x, bias_ref, attend_ref, output_ref, up_ref,
+    qkv_ref, probs_ref, rest_ref, value_t_ref, mixed_t_ref, after_head,
 ):
-    x = x_ref[...].astype(F32)
     normed, _ = normalized(x)
     qkv = mm(normed.astype(BF), attend_ref[...]).astype(BF)
     qkv_ref[...] = qkv
@@ -148,6 +134,7 @@
         total = jnp.sum(exponent, axis=0, keepdims=True)
         probs = (exponent * (1.0 / total)).astype(BF)
         probs_ref[head] = probs
+        after_head(head)
         at = pl.multiple_of(head * HD, HD)
         mixed_t_ref[pl.ds(at, HD), :] = mm(value_t_ref[pl.ds(at, HD), :], probs)
         return carry
@@ -156,22 +143,25 @@
     attended = mixed_t_ref[...].astype(BF).T
     mixed = mm(attended, output_ref[...]).astype(BF).astype(F32)
     hat, inverse = normalized(x + mixed)
-    hat_ref[...] = hat
-    inverse_ref[...] = inverse
-    slope_ref[...] = gelu_slope(mm(hat.astype(BF), up_ref[...]))
-
-
-def backward_kernel(
-    x_ref, g_ref, qkv_ref, probs_ref, hat_ref, inverse_ref, slope_ref,
+    hidden = up_ref.shape[1]
+    rest_ref[:, hidden : hidden + D] = hat
+    rest_ref[:, hidden + D :] = jnp.broadcast_to(inverse, (slots, 128))
+    rest_ref[:, :hidden] = gelu_slope(mm(hat.astype(BF), up_ref[...]))
+
+
+def backward_part(
+    x, g, qkv_ref, probs_ref, rest_ref,
     attend_ref, output_ref, up_ref, down_ref,
-    out_ref,
-    key_t_ref, query_grad_ref, key_grad_ref, value_grad_ref, up_grad_ref,
+    key_t_ref, query_grad_ref, key_grad_ref, value_grad_ref, up_grad_ref, before_rest, before_head,
 ):
-    g = g_ref[...]
     slots = g.shape[0]
-    pre_grad = (slope_ref[...] * mm_t(g, down_ref[...])).astype(BF)
+    hidden_grad = mm_t(g, down_ref[...])
+    before_rest()
+    hidden = up_ref.shape[1]
+    pre_grad = (rest_ref[:, :hidden] * hidden_grad).astype(BF)
+    hat, inverse = rest_ref[:, hidden : hidden + D], rest_ref[:, hidden + D : hidden + D + 1]
     grad_mid = (
-        g.astype(F32) + norm_gradient(mm_t(pre_grad, up_ref[...]), hat_ref[...], inverse_ref[...])
+        g.astype(F32) + norm_gradient(mm_t(pre_grad, up_ref[...]), hat, inverse)
     ).astype(BF)
     up_grad_ref[...] = mm_t(grad_mid, output_ref[...]).astype(BF)
     key_t_ref[...] = qkv_ref[:, D : 2 * D].T
@@ -183,6 +173,7 @@
         zero = jnp.zeros((slots, D), BF)
         values = jnp.where(inside, qkv_ref[:, 2 * D :], zero)
         prob_grads = mm_t(values, up_grad_ref[...])
+        before_head(head)
         rounded = probs_ref[head]
         probs = rounded.astype(F32)
         total = jnp.sum(prob_grads * probs, axis=0, keepdims=True)
@@ -202,44 +193,171 @@
         + mm_t(key_grads, attend_ref[:, D : 2 * D])
         + mm_t(value_grads, attend_ref[:, 2 * D :])
     )
-    hat, inverse = normalized(x_ref[...].astype(F32))
+    hat, inverse = normalized(x)
     branch = norm_gradient(normed_grads, hat, inverse).astype(BF)
-    out_ref[...] = (grad_mid.astype(F32) + branch.astype(F32)).astype(BF)
-
-
-def forward(x, bias, attend, output, up):
-    slots = x.shape[0]
-    hidden = up.shape[1]
+    return (grad_mid.astype(F32) + branch.astype(F32)).astype(BF)
+
+
+def nothing(*_):
+    return None
+
+
+def whole_layer_kernel(
+    index_ref, owners_one_ref, owners_zero_ref, xg_ref, next_x_ref,
+    attend_ref, output_ref, up_ref, down_ref,
+    out_ref, dest_ref, next_bias_ref,
+    bias_ref, qkv_ref, probs_ref, rest_ref,
+    value_t_ref, mixed_t_ref, query_grad_ref, key_grad_ref, value_grad_ref, up_grad_ref,
+):
+    my = index_ref[0]
+    bias_ref[...] = key_bias(owners_one_ref[...], my)
+    next_bias_ref[...] = key_bias(owners_zero_ref[...], my)
+    dest = destination_row(owners_zero_ref[pl.ds(my, 1), :].astype(F32))
+    dest_ref[...] = jnp.broadcast_to(dest, dest_ref.shape)
+    out_ref[:, D:] = mm(one_hot(dest, out_ref.shape[0]), next_x_ref[...]).astype(BF)
+    saved = (qkv_ref, probs_ref, rest_ref)
+    forward_part(
+        xg_ref[:, :D].astype(F32), bias_ref, attend_ref, output_ref, up_ref,
+        *saved, value_t_ref, mixed_t_ref, nothing,
+    )
+    out_ref[:, :D] = backward_part(
+        xg_ref[:, :D].astype(F32), xg_ref[:, D:], *saved,
+        attend_ref, output_ref, up_ref, down_ref,
+        value_t_ref, query_grad_ref, key_grad_ref, value_grad_ref, up_grad_ref, nothing, nothing,
+    )
+
+
+def forward_kernel(
+    rx_ref, bias_ref, attend_ref, output_ref, up_ref,
+    qkv_ref, probs_out_ref, rest_out_ref,
+    probs_ref, rest_ref, value_t_ref, mixed_t_ref, probs_sem, rest_sem,
+):
+    def probs_copy(head):
+        return pltpu.make_async_copy(probs_ref.at[head], probs_out_ref.at[head], probs_sem.at[head])
+
+    forward_part(
+        rx_ref[:, D:].astype(F32), bias_ref, attend_ref, output_ref, up_ref,
+        qkv_ref, probs_ref, rest_ref,
+        value_t_ref, mixed_t_ref, lambda head: probs_copy(head).start(),
+    )
+    rest_copy = pltpu.make_async_copy(rest_ref, rest_out_ref, rest_sem)
+    rest_copy.start()
+    for head in range(HEADS):
+        probs_copy(head).wait()
+    rest_copy.wait()
+
+
+def backward_kernel(
+    rx_ref, g_ref, qkv_ref, probs_in_ref, rest_in_ref,
+    attend_ref, output_ref, up_ref, down_ref,
+    out_ref,
+    probs_ref, rest_ref, key_t_ref, query_grad_ref, key_grad_ref, value_grad_ref, up_grad_ref,
+    probs_sem, rest_sem,
+):
+    def probs_copy(head):
+        return pltpu.make_async_copy(probs_in_ref.at[head], probs_ref.at[head], probs_sem.at[head])
+
+    rest_copy = pltpu.make_async_copy(rest_in_ref, rest_ref, rest_sem)
+    rest_copy.start()
+    for head in range(HEADS):
+        probs_copy(head).start()
+    out_ref[...] = backward_part(
+        rx_ref[:, D:].astype(F32), g_ref[...], qkv_ref, probs_ref, rest_ref,
+        attend_ref, output_ref, up_ref, down_ref,
+        key_t_ref, query_grad_ref, key_grad_ref, value_grad_ref, up_grad_ref,
+        rest_copy.wait, lambda head: probs_copy(head).wait(),
+    )
+
+
+SMEM_SPEC = pl.BlockSpec(memory_space=pltpu.SMEM)
+VMEM_SPEC = pl.BlockSpec(memory_space=pltpu.VMEM)
+HBM_SPEC = pl.BlockSpec(memory_space=pltpu.HBM)
+
+
+def saved_shapes(slots, hidden):
+    return dict(
+        qkv=((slots, 3 * D), BF),
+        probs=((HEADS, slots, slots), BF),
+        rest=((slots, hidden + D + 128), F32),
+    )
+
+
+def gradient_scratch(slots):
+    return [
+        pltpu.VMEM((D, slots), BF),
+        pltpu.VMEM((D, slots), F32),
+        pltpu.VMEM((slots, D), F32),
+        pltpu.VMEM((slots, D), F32),
+        pltpu.VMEM((slots, D), BF),
+    ]
+
+
+def params():
+    return pltpu.CompilerParams(vmem_limit_bytes=40 << 20)
+
+
+def whole_layer(my_index, owners_one, owners_zero, xg, next_x, attend, output, up, down):
+    slots, hidden = xg.shape[0], up.shape[1]
+    shape = saved_shapes(slots, hidden)
+    gradients = gradient_scratch(slots)
+    return pl.pallas_call(
+        whole_layer_kernel,
+        out_shape=(
+            jax.ShapeDtypeStruct((slots, 2 * D), BF),
+            jax.ShapeDtypeStruct((8, next_x.shape[0]), F32),
+            jax.ShapeDtypeStruct((slots, 128), BF),
+        ),
+        in_specs=[SMEM_SPEC] + [VMEM_SPEC] * 8,
+        scratch_shapes=[pltpu.VMEM((slots, 128), BF)]
+        + [pltpu.VMEM(*shape[n]) for n in ("qkv", "probs", "rest")]
+        + [gradients[0], pltpu.VMEM((D, slots), F32)]
+        + gradients[1:],
+        name="whole_layer",
+        compiler_params=params(),
+    )(my_index, owners_one, owners_zero, xg, next_x, attend, output, up, down)
+
+
+def forward(rx, bias, attend, output, up):
+    slots, hidden = rx.shape[0], up.shape[1]
+    shape = saved_shapes(slots, hidden)
     return pl.pallas_call(
         forward_kernel,
         out_shape=(
-            jax.ShapeDtypeStruct((slots, 3 * D), BF),
-            jax.ShapeDtypeStruct((HEADS, slots, slots), BF),
-            jax.ShapeDtypeStruct((slots, D), F32),
-            jax.ShapeDtypeStruct((slots, 1), F32),
-            jax.ShapeDtypeStruct((slots, hidden), F32),
+            jax.ShapeDtypeStruct(*shape["qkv"]),
+            pltpu.HBM(*shape["probs"]),
+            pltpu.HBM(*shape["rest"]),
         ),
-        scratch_shapes=[pltpu.VMEM((D, slots), BF), pltpu.VMEM((D, slots), F32)],
+        out_specs=(VMEM_SPEC, HBM_SPEC, HBM_SPEC),
+        scratch_shapes=[
+            pltpu.VMEM(*shape["probs"]),
+            pltpu.VMEM(*shape["rest"]),
+            pltpu.VMEM((D, slots), BF),
+            pltpu.VMEM((D, slots), F32),
+            pltpu.SemaphoreType.DMA((HEADS,)),
+            pltpu.SemaphoreType.DMA,
+        ],
         name="layer_forward",
-        compiler_params=pltpu.CompilerParams(vmem_limit_bytes=40 << 20),
-    )(x, bias, attend, output, up)
-
-
-def backward(x, g, saved, attend, output, up, down):
-    slots = x.shape[0]
+        compiler_params=params(),
+    )(rx, bias, attend, output, up)
+
+
+def backward(rx, g, saved, attend, output, up, down):
+    slots, hidden = g.shape[0], up.shape[1]
+    shape = saved_shapes(slots, hidden)
     return pl.pallas_call(
         backward_kernel,
         out_shape=jax.ShapeDtypeStruct((slots, D), BF),
-        scratch_shapes=[
-            pltpu.VMEM((D, slots), BF),
-            pltpu.VMEM((D, slots), F32),
-            pltpu.VMEM((slots, D), F32),
-            pltpu.VMEM((slots, D), F32),
-            pltpu.VMEM((slots, D), BF),
-        ],
+        in_specs=[VMEM_SPEC] * 3 + [HBM_SPEC] * 2 + [VMEM_SPEC] * 4,
+        scratch_shapes=[pltpu.VMEM(*shape["probs"]), pltpu.VMEM(*shape["rest"])]
+        + gradient_scratch(slots)
+        + [pltpu.SemaphoreType.DMA((HEADS,)), pltpu.SemaphoreType.DMA],
         name="layer_backward",
-        compiler_params=pltpu.CompilerParams(vmem_limit_bytes=40 << 20),
-    )(x, g, *saved, attend, output, up, down)
+        compiler_params=params(),
+    )(
+        rx, g, saved[0],
+        *(pltpu.with_memory_space_constraint(s, pltpu.HBM) for s in saved[1:]),
+        attend, output, up, down,
+    )
 
 
 def per_device(saved_inputs, output_grads, owner_ids, attend, output, up, down):
@@ -256,40 +374,28 @@
         )
         return moved.reshape(slots, width)
 
-    smem = pl.BlockSpec(memory_space=pltpu.SMEM)
-    vmem = pl.BlockSpec(memory_space=pltpu.VMEM)
-    dest_shape = jax.ShapeDtypeStruct((8, points), F32)
-    dest_one, packed_x = pl.pallas_call(
-        route_first_kernel,
-        out_shape=(dest_shape, jax.ShapeDtypeStruct((slots, D), BF)),
-        in_specs=[smem, vmem, vmem],
-        name="route_first",
-    )(my_index, owners[1], saved_inputs[1])
-    x_one = exchange(packed_x)
-    dest_zero, packed_gx, bias = pl.pallas_call(
-        route_second_kernel,
+    dest_one, packed = pl.pallas_call(
+        route_kernel,
         out_shape=(
-            dest_shape,
+            jax.ShapeDtypeStruct((8, points), F32),
             jax.ShapeDtypeStruct((slots, 2 * D), BF),
-            jax.ShapeDtypeStruct((2, slots, 128), BF),
         ),
-        in_specs=[smem] + [vmem] * 5,
-        name="route_second",
-    )(my_index, owners[1], owners[0], dest_one, output_grads, saved_inputs[0])
-    gx = exchange(packed_gx)
-    saved_one = forward(x_one, bias[1], attend[1], output[1], up[1])
-    result = backward(x_one, gx[:, :D], saved_one, attend[1], output[1], up[1], down[1])
-    returned = exchange(result)
-    x_zero = gx[:, D:]
-    saved_zero = forward(x_zero, bias[0], attend[0], output[0], up[0])
-    packed_g = vmem_call(repack_kernel, jax.ShapeDtypeStruct((slots, D), BF), "repack")(
-        dest_one, dest_zero, returned
-    )
-    g_zero = exchange(packed_g)
-    result = backward(x_zero, g_zero, saved_zero, attend[0], output[0], up[0], down[0])
-    returned = exchange(result)
+        in_specs=[SMEM_SPEC] + [VMEM_SPEC] * 3,
+        name="route",
+    )(my_index, owners[1], saved_inputs[1], output_grads)
+    xg = exchange(packed)
+    result, dest_zero, bias = whole_layer(
+        my_index, owners[1], owners[0], xg, saved_inputs[0], attend[1], output[1], up[1], down[1]
+    )
+    rx = exchange(result)
+    packed = vmem_call(repack_kernel, jax.ShapeDtypeStruct((slots, D), BF), "repack")(
+        dest_one, dest_zero, rx
+    )
+    g_zero = exchange(packed)
+    saved = forward(rx, bias, attend[0], output[0], up[0])
+    result = backward(rx, g_zero, saved, attend[0], output[0], up[0], down[0])
     return vmem_call(unpack_kernel, jax.ShapeDtypeStruct((points, D), BF), "unpack")(
-        dest_zero, returned
+        dest_zero, exchange(result)
     )
 
 

time: 155 us -> 135 us (0.87)
  local copies, waits for them, and re-layouts: 32.2 us -> 12.7 us
  waiting for transfers between devices: 10.2 us -> 14.8 us
  starting transfers between devices: 23 us -> 18.8 us
  Pallas kernels: 41.8 us -> 44.1 us
  blocking collectives: 46.4 us -> 44.3 us
    unnamed x48 -> x16, local copies, waits for them, and re-layouts: 24 us -> 4.4 us
    pallas_call x4 -> x3, Pallas kernels: 21.1 us -> 29.5 us  [the longest x1 17.2 us: whole_layer(): pl.pallas_call(whole_layer_kernel, out_shape=(jax.ShapeDtypeStruct((slots...]
    pallas_call x2 -> x1, Pallas kernels: 18.5 us -> 12.4 us  [backward(): pl.pallas_call(backward_kernel, out_shape=jax.ShapeDtypeStruct((slots, D)...]
    all_to_all x3 -> x2, waiting for transfers between devices: 10.2 us -> 14.8 us  [exchange(): lax.all_to_all(rows.reshape(devices, 8, width), 'blk', split_axis=0, conc...]
    all_to_all x3 -> x2, starting transfers between devices: 23 us -> 18.8 us  [exchange(): lax.all_to_all(rows.reshape(devices, 8, width), 'blk', split_axis=0, conc...]
    all_to_all x2, blocking collectives: 46.4 us -> 44.3 us  [exchange(): lax.all_to_all(rows.reshape(devices, 8, width), 'blk', split_axis=0, conc...]
    squeeze x5 -> x4, local copies, waits for them, and re-layouts: 2.91 us -> 4.23 us  [the longest x3 4.16 us: per_device(): saved = forward(rx, bias, attend[0], output[0], up[0])]
  transfers between devices with their start and end apart: 3 -> 2, of which waited for: 2 -> 2; matrix products, arithmetic and copies ran while one was open for 2% -> 4% of each run, Pallas kernels for 12% -> 7%
where the time goes in v1:
time: 135 us
  blocking collectives  44.3 us (33%)
  Pallas kernels  44.1 us (33%)
  starting transfers between devices  18.8 us (14%)
  waiting for transfers between devices  14.8 us (11%)
  local copies, waits for them, and re-layouts  12.7 us (9%)
    all_to_all x2, blocking collectives, exchange(): lax.all_to_all(rows.reshape(devices, 8, width), 'blk', split_axis=0, conc...  44.3 us
    all_to_all x2, starting transfers between devices, exchange(): lax.all_to_all(rows.reshape(devices, 8, width), 'blk', split_axis=0, conc...  18.8 us
    pallas_call x1, Pallas kernels, whole_layer(): pl.pallas_call(whole_layer_kernel, out_shape=(jax.ShapeDtypeStruct((slots...  17.2 us
    all_to_all x2, waiting for transfers between devices, exchange(): lax.all_to_all(rows.reshape(devices, 8, width), 'blk', split_axis=0, conc...  14.8 us
    pallas_call x1, Pallas kernels, backward(): pl.pallas_call(backward_kernel, out_shape=jax.ShapeDtypeStruct((slots, D)...  12.4 us
    pallas_call x1, Pallas kernels, forward(): pl.pallas_call(forward_kernel, out_shape=(jax.ShapeDtypeStruct(*shape['qk...  10.1 us
    unnamed x16, local copies, waits for them, and re-layouts  4.4 us
    squeeze x3, local copies, waits for them, and re-layouts, per_device(): saved = forward(rx, bias, attend[0], output[0], up[0])  4.16 us
  transfers between devices with their start and end apart: 2, of which 2 were waited for; matrix products, arithmetic and copies ran while one was open for 4% of the time, Pallas kernels for 7%

profile of v1, /device:TPU:1, one launch (start us, length us, event | category | flops | bytes accessed | tf_op | source)
XLA Modules:
  0.0 134.9 jit_solution(17871573261275806241)
XLA Ops:
  0.0 1.1 slice_reduce_fusion
  1.1 0.6 squeeze.40.owners_ref.owners_one_ref
  1.8 1.7 %slice_bitcast_fusion.8 = (bf16[256,256]{1,0:T(8,128)(2,1)}, bf16[256,256]{1,0:T(8,128)(2,1)}) fusion(bf16[2,256,256]{2,1,0:T(8,128)(2,1)} %param.7), kind=kLoop, calls=%fused_computation.8 | loop fusion | bytes 524288 | tf_op jit(solution)/shard_map/squeeze | solution.py:388
  3.4 2.2 %route.1 = (f32[8,256]{1,0:T(8,128)}, bf16[512,512]{1,0:T(8,128)(2,1)}) custom-call(s32[1]{0:T(128)} %bitcast.index_ref, s32[64,256]{1,0:T(8,128)} %squeeze.40.owners_ref.owners_one_ref, bf16[256,256]{1,0:T(8,128)(2,1)} %get-tuple-element.32.x_ref, bf16[256,256]{1,0:T(8,128)(2,1)} %g_ref.1), custom_call_target="tpu_custom_call" | custom-call | tf_op jit(solution)/shard_map/route/pallas_call | solution.py:377
  5.6 13.1 %all-to-all-start = ((bf16[64,8,512]{2,1,0:T(8,128)(2,1)}), bf16[64,8,512]{2,1,0:T(8,128)(2,1)S(1)}, u32[]{:S(2)}, u32[]{:S(2)}) async-start(bf16[64,8,512]{2,1,0:T(8,128)(2,1)} %bitcast.37), calls=%async_computation | async-start | bytes 1048576 | tf_op jit(solution)/shard_map/all_to_all | solution.py:372
  18.8 0.7 squeeze.41.owners_zero_ref
  19.4 0.0 copy-start.7
  19.4 1.7 %slice_bitcast_fusion.6 = (bf16[256,256]{1,0:T(8,128)(2,1)S(1)}, bf16[256,256]{1,0:T(8,128)(2,1)}) fusion(bf16[2,256,256]{2,1,0:T(8,128)(2,1)} %param.11), kind=kLoop, calls=%fused_computation.6 | loop fusion | bytes 524288 | tf_op jit(solution)/shard_map/squeeze | solution.py:395
  21.2 1.2 slice_bitcast_fusion.4
  22.3 0.0 copy-start.6
  22.3 1.3 slice_bitcast_fusion.1
  23.6 0.0 copy-done.7
  23.6 0.1 slice_bitcast_fusion
  23.7 12.8 %all-to-all-done = bf16[64,8,512]{2,1,0:T(8,128)(2,1)S(1)} async-done(((bf16[64,8,512]{2,1,0:T(8,128)(2,1)}), bf16[64,8,512]{2,1,0:T(8,128)(2,1)S(1)}, u32[]{:S(2)}, u32[]{:S(2)}) %all-to-all-start) | async-done | bytes 524320 | tf_op jit(solution)/shard_map/all_to_all | solution.py:372
  36.5 0.8 copy-done
  37.3 0.9 copy-done.1
  38.2 0.9 copy-done.2
  39.1 0.8 copy-done.3
  40.0 17.2 %whole_layer.1 = (bf16[512,512]{1,0:T(8,128)(2,1)S(1)}, f32[8,256]{1,0:T(8,128)S(1)}, bf16[512,128]{1,0:T(8,128)(2,1)S(1)}) custom-call(s32[1]{0:T(128)} %bitcast.index_ref, s32[64,256]{1,0:T(8,128)S(1)} %copy-done, s32[64,256]{1,0:T(8,128)S(1)} %copy-done.3, bf16[512,512]{1,0:T(8,128)(2,1)S(1)} %bitcast.32, bf16[256,256]{1,0:T(8,128)(2,1)S(1)} %copy-done.1, ...), custom_call_target="tpu_custom_call" | custom-call | tf_op jit(solution)/shard_map/whole_layer/pallas_call | solution.py:303
  57.2 0.0 copy-start.4
  57.2 23.2 %all_to_all.20 = bf16[64,8,512]{2,1,0:T(8,128)(2,1)S(1)} all-to-all(bf16[64,8,512]{2,1,0:T(8,128)(2,1)S(1)} %bitcast.36), channel_id=1, replica_groups=mesh['blk'=64,'rep'=4] {'blk'}, dimensions={0} | all-to-all | bytes 1048576 | tf_op jit(solution)/shard_map/all_to_all | solution.py:372
  80.4 0.0 copy-done.4
  80.4 0.0 copy-done.6
  80.4 1.3 repack.1
  81.6 5.7 %all-to-all-start.2 = ((bf16[64,8,256]{2,1,0:T(8,128)(2,1)}), bf16[64,8,256]{2,1,0:T(8,128)(2,1)S(1)}, u32[]{:S(2)}, u32[]{:S(2)}) async-start(bf16[64,8,256]{2,1,0:T(8,128)(2,1)} %bitcast.11), calls=%async_computation.2 | async-start | bytes 524288 | tf_op jit(solution)/shard_map/all_to_all | solution.py:372
  87.3 0.0 copy-start.5
  87.4 0.9 copy-done.5
  88.3 10.1 %layer_forward.1 = (bf16[512,768]{1,0:T(8,128)(2,1)S(1)}, bf16[8,512,512]{2,1,0:T(8,128)(2,1)}, f32[512,1408]{1,0:T(8,128)}) custom-call(bf16[512,512]{1,0:T(8,128)(2,1)S(1)} %bitcast.30, bf16[512,128]{1,0:T(8,128)(2,1)S(1)} %copy-done.5, bf16[256,768]{1,0:T(8,128)(2,1)S(1)} %get-tuple-element.27.attend_ref, ...), custom_call_target="tpu_custom_call" | custom-call | tf_op jit(solution)/shard_map/layer_forward/pallas_call | solution.py:323
  98.3 2.1 %all-to-all-done.2 = bf16[64,8,256]{2,1,0:T(8,128)(2,1)S(1)} async-done(((bf16[64,8,256]{2,1,0:T(8,128)(2,1)}), bf16[64,8,256]{2,1,0:T(8,128)(2,1)S(1)}, u32[]{:S(2)}, u32[]{:S(2)}) %all-to-all-start.2) | async-done | bytes 262176 | tf_op jit(solution)/shard_map/all_to_all | solution.py:372
  100.4 12.4 %layer_backward.1 = bf16[512,256]{1,0:T(8,128)(2,1)S(1)} custom-call(bf16[512,512]{1,0:T(8,128)(2,1)S(1)} %bitcast.31, bf16[512,256]{1,0:T(8,128)(2,1)S(1)} %bitcast.33, bf16[512,768]{1,0:T(8,128)(2,1)S(1)} %get-tuple-element.18.qkv_ref, bf16[8,512,512]{2,1,0:T(8,128)(2,1)} %get-tuple-element.19.probs_in_ref, f32[512,1408]{1,0:T(8,128)} %get-tuple-element.20.rest_in_ref, ...), custom_call_target="tpu_custom_call" | custom-call | tf_op jit(solution)/shard_map/layer_backward/pallas_call | solution.py:347
  112.8 21.1 %all_to_all.21 = bf16[64,8,256]{2,1,0:T(8,128)(2,1)S(1)} all-to-all(bf16[64,8,256]{2,1,0:T(8,128)(2,1)S(1)} %bitcast.34), channel_id=1, replica_groups=mesh['blk'=64,'rep'=4] {'blk'}, dimensions={0} | all-to-all | bytes 524288 | tf_op jit(solution)/shard_map/all_to_all | solution.py:372
  133.9 0.9 unpack.1
  (4 shorter events, 0.0 us)
Async XLA Ops:
  5.6 30.8 %all-to-all-start = ((bf16[64,8,512]{2,1,0:T(8,128)(2,1)}), bf16[64,8,512]{2,1,0:T(8,128)(2,1)S(1)}, u32[]{:S(2)}, u32[]{:S(2)}) async-start(bf16[64,8,512]{2,1,0:T(8,128)(2,1)} %bitcast.37), calls=%async_computation | async-start | bytes 1048576 | tf_op jit(solution)/shard_map/all_to_all | solution.py:372
  19.4 4.2 %copy-start.7 = (bf16[2,1024,256]{2,1,0:T(8,128)(2,1)S(1)}, bf16[2,1024,256]{2,1,0:T(8,128)(2,1)}, u32[]{:S(2)}) copy-start(bf16[2,1024,256]{2,1,0:T(8,128)(2,1)} %param.13) | copy-start | bytes 3145732
  22.3 58.1 %copy-start.6 = (f32[8,256]{1,0:T(8,128)S(1)}, f32[8,256]{1,0:T(8,128)}, u32[]{:S(2)}) copy-start(f32[8,256]{1,0:T(8,128)} %get-tuple-element.16.dest_one_ref) | copy-start | bytes 24580
  36.5 0.8 copy-start
  37.3 0.9 copy-start.1
  38.2 0.9 copy-start.2
  39.1 0.8 copy-start.3
  57.2 23.2 %copy-start.4 = (bf16[512,128]{1,0:T(8,128)(2,1)}, bf16[512,128]{1,0:T(8,128)(2,1)S(1)}, u32[]{:S(2)}) copy-start(bf16[512,128]{1,0:T(8,128)(2,1)S(1)} %get-tuple-element.17.bias_ref) | copy-start | bytes 393220
  81.6 18.8 %all-to-all-start.2 = ((bf16[64,8,256]{2,1,0:T(8,128)(2,1)}), bf16[64,8,256]{2,1,0:T(8,128)(2,1)S(1)}, u32[]{:S(2)}, u32[]{:S(2)}) async-start(bf16[64,8,256]{2,1,0:T(8,128)(2,1)} %bitcast.11), calls=%async_computation.2 | async-start | bytes 524288 | tf_op jit(solution)/shard_map/all_to_all | solution.py:372
  87.3 0.9 copy-start.5

commit v2 on v0

v2 whole, which is shorter than its diff:
```python
import jax
import jax.numpy as jnp
from jax import lax
from jax.experimental import pallas as pl
from jax.experimental.pallas import tpu as pltpu
from jax.sharding import PartitionSpec as P

D = 256
HEADS = 8
HD = D // HEADS
EPSILON = 1e-05
MASKED = -1e30
SCALE = HD ** (-0.5)
LOG2E = 1.4426950408889634
BF = jnp.bfloat16
F32 = jnp.float32


def mm(left, right):
    return lax.dot_general(left, right, (((1,), (0,)), ((), ())), preferred_element_type=F32)


def mm_t(left, right):
    return lax.dot_general(left, right, (((1,), (1,)), ((), ())), preferred_element_type=F32)


def iota(shape, axis):
    return lax.broadcasted_iota(jnp.int32, shape, axis)


def destination_row(owners, my_index, points):
    wide_rows = points // LANES
    own_row = jnp.concatenate(
        [owners[pl.ds(my_index * wide_rows + i, 1), :] for i in range(wide_rows)], axis=1
    ).astype(F32)
    rows, cols = iota((points, points), 0), iota((points, points), 1)
    wide = jnp.broadcast_to(own_row, (points, points))
    own_col = jnp.sum(jnp.where(rows == cols, wide, 0.0), axis=1, keepdims=True)
    same = jnp.where((own_col == wide) & (rows < cols), 1.0, 0.0)
    rank = jnp.sum(same, axis=0, keepdims=True)
    return own_row * 8.0 + rank


def one_hot(dest_row, slots):
    shape = (slots, dest_row.shape[1])
    return jnp.where(iota(shape, 0).astype(F32) == dest_row, 1.0, 0.0).astype(BF)


def key_bias(owners, my_index, slots):
    rows = owners.shape[0]
    per_source = rows * 8 // slots
    count = jnp.sum(jnp.where(owners == my_index, 1.0, 0.0), axis=1, keepdims=True)
    shape = (slots, rows)
    spread = jnp.where(iota(shape, 0) // 8 == iota(shape, 1) // per_source, 1.0, 0.0).astype(BF)
    slot_count = mm(spread, jnp.broadcast_to(count, (rows, D)).astype(BF))
    rank = (iota(slot_count.shape, 0) % 8).astype(F32)
    return jnp.where(rank < slot_count, 0.0, MASKED).astype(BF)


def unpack(dest_row, rows):
    hot = one_hot(dest_row, rows.shape[0])
    return lax.dot_general(hot, rows, (((0,), (0,)), ((), ())), preferred_element_type=F32).astype(BF)


def fetch(sem, pairs):
    copies = [pltpu.make_async_copy(a, b, sem.at[i]) for i, (a, b) in enumerate(pairs)]
    for copy in copies:
        copy.start()
    return copies


def route_kernel(
    index_ref, owners_hbm, saved_hbm, g_hbm, dest_ref, out_ref, owners_ref, x_ref, g_ref, sem
):
    slots, points = out_ref.shape[0], g_hbm.shape[0]
    owners_in, x_in, g_in = fetch(
        sem, [(owners_hbm.at[1], owners_ref), (saved_hbm.at[1], x_ref), (g_hbm, g_ref)]
    )
    owners_in.wait()
    dest = destination_row(owners_ref, index_ref[0], points)
    dest_ref[...] = jnp.broadcast_to(dest, dest_ref.shape)
    hot = one_hot(dest, slots)
    x_in.wait()
    out_ref[:, :D] = mm(hot, x_ref[...]).astype(BF)
    g_in.wait()
    out_ref[:, D:] = mm(hot, g_ref[...]).astype(BF)


def repack_kernel(dest_one_ref, dest_zero_ref, rows_ref, out_ref):
    gradient = unpack(dest_one_ref[0:1, :], rows_ref[:, :D])
    out_ref[...] = mm(one_hot(dest_zero_ref[0:1, :], out_ref.shape[0]), gradient).astype(BF)


def unpack_kernel(dest_ref, rows_ref, out_ref):
    out_ref[...] = unpack(dest_ref[0:1, :], rows_ref[...])


def normalized(values):
    centered = values - jnp.mean(values, axis=1, keepdims=True)
    inverse = lax.rsqrt(jnp.mean(centered * centered, axis=1, keepdims=True) + EPSILON)
    return centered * inverse, inverse


def norm_gradient(upstream, hat, inverse):
    mean_one = jnp.mean(upstream, axis=1, keepdims=True)
    mean_two = jnp.mean(upstream * hat, axis=1, keepdims=True)
    return inverse * (upstream - mean_one - hat * mean_two)


def head_lanes(shape, head):
    lane = iota(shape, 1)
    return (lane >= head * HD) & (lane < head * HD + HD)


def gelu_slope(pre):
    root, cubic = 0.7978845608028654, 0.044715
    square = pre * pre
    bend = jnp.tanh(pre * (root + (root * cubic) * square))
    rise = pre * (root + (3.0 * root * cubic) * square)
    return (0.5 + 0.5 * bend) * (1.0 + (1.0 - bend) * rise)


HALVES = 2
LANES = 128


def forward_part(x, weights, kept, work, wait, after_head):
    attend_ref, output_ref, up_ref, _ = weights
    qkv_ref, probs_ref, slope_ref, norm_ref, mixed_t_ref = kept
    bias_ref, query_ref, value_t_ref, even_ref, odd_ref, even_max_ref, odd_max_ref = work
    slots = x.shape[0]
    half = slots // HALVES
    normed, _ = normalized(x)
    wait("attend")
    qkv = mm(normed.astype(BF), attend_ref[...]).astype(BF)
    qkv_ref[...] = qkv
    value_t_ref[...] = qkv[:, 2 * D :].T
    lane = iota((slots, D), 1)
    query_ref[...] = jnp.where(lane == 0, jnp.ones((slots, D), BF), qkv[:, :D])
    wait("owners")

    def score_half(keys, queries, part, scores_ref, max_ref):
        cols = slice(part * half, (part + 1) * half)
        scores = mm_t(keys, queries)
        scores_ref[:, cols] = scores
        max_ref[:, cols] = jnp.broadcast_to(jnp.max(scores, axis=0, keepdims=True), (8, half))

    def soft_half(head, part, scores_ref, max_ref):
        cols = slice(part * half, (part + 1) * half)
        largest = max_ref[0:1, cols]
        exponent = jnp.exp2((scores_ref[:, cols] - largest) * (SCALE * LOG2E))
        total = jnp.sum(exponent, axis=0, keepdims=True)
        probs = (exponent * (1.0 / total)).astype(BF)
        probs_ref[head, :, cols] = probs
        at = pl.multiple_of(head * HD, HD)
        mixed_t_ref[pl.ds(at, HD), cols] = mm(value_t_ref[pl.ds(at, HD), :], probs)

    bias = bias_ref[...]
    first_keys = jnp.where(
        head_lanes((slots, D), 0),
        qkv[:, D : 2 * D],
        jnp.where(lane == D - 1, bias, jnp.zeros_like(bias)),
    )
    first_queries = jnp.where(lane == D - 1, jnp.ones((slots, D), BF), qkv[:, :D])
    bias_ref[...] = jnp.where(lane == 0, bias, jnp.zeros_like(bias))
    for part in range(HALVES):
        rows = slice(part * half, (part + 1) * half)
        score_half(first_keys, first_queries[rows], part, even_ref, even_max_ref)

    def step(head, following, here, here_max, there, there_max):
        keys = jnp.where(head_lanes((slots, D), following), qkv_ref[:, D : 2 * D], bias_ref[...])
        for part in range(HALVES):
            rows = slice(part * half, (part + 1) * half)
            score_half(keys, query_ref[rows, :], part, there, there_max)
            soft_half(head, part, here, here_max)
        after_head(head)

    def pair(index, carry):
        step(2 * index, 2 * index + 1, even_ref, even_max_ref, odd_ref, odd_max_ref)
        following = jnp.minimum(2 * index + 2, HEADS - 1)
        step(2 * index + 1, following, odd_ref, odd_max_ref, even_ref, even_max_ref)
        return carry

    lax.fori_loop(0, HEADS // 2, pair, 0)
    attended = mixed_t_ref[...].astype(BF).T
    wait("output")
    mixed = mm(attended, output_ref[...]).astype(BF).astype(F32)
    hat, inverse = normalized(x + mixed)
    norm_ref[:, :D] = hat
    norm_ref[:, D:] = jnp.broadcast_to(inverse, (slots, LANES))
    rounded = hat.astype(BF)
    wait("up")
    for part in range(slope_ref.shape[0]):
        slope_ref[part] = gelu_slope(mm(rounded, up_ref[:, part * D : (part + 1) * D]))


def backward_part(x, g, weights, kept, work, wait, before_head):
    attend_ref, output_ref, up_ref, down_ref = weights
    qkv_ref, probs_ref, slope_ref, norm_ref, mixed_t_ref = kept
    pre_grad_ref, up_grad_ref, up_grad_t_ref, query_t_ref, key_t_ref, delta_ref, grads_t_ref = work
    slots = g.shape[0]
    half = slots // HALVES
    query_t_ref[...] = qkv_ref[:, :D].T
    key_t_ref[...] = qkv_ref[:, D : 2 * D].T
    wait("down")
    for part in range(slope_ref.shape[0]):
        rows = slice(part * D, (part + 1) * D)
        hidden_grad = mm_t(g, down_ref[rows, :])
        wait("slope", part)
        pre_grad_ref[:, rows] = (slope_ref[part] * hidden_grad).astype(BF)
    wait("up")
    normed_grad = mm_t(pre_grad_ref[...], up_ref[...])
    wait("norm")
    grad_mid = (
        g.astype(F32) + norm_gradient(normed_grad, norm_ref[:, :D], norm_ref[:, D : D + 1])
    ).astype(BF)
    wait("output")
    up_grad_ref[...] = mm_t(grad_mid, output_ref[...]).astype(BF)
    up_grad_t = mm_t(output_ref[...], grad_mid).astype(BF)
    up_grad_t_ref[...] = up_grad_t
    wait("mixed")
    weighted = mixed_t_ref[...] * up_grad_t.astype(F32)
    for head in range(HEADS):
        delta_ref[head : head + 1, :] = jnp.sum(
            weighted[head * HD : (head + 1) * HD], axis=0, keepdims=True
        )

    def one_head(head, carry):
        values = jnp.where(
            head_lanes((slots, D), head), qkv_ref[:, 2 * D :], jnp.zeros((slots, D), BF)
        )
        at = pl.multiple_of(head * HD, HD)
        key_grad = value_grad = 0.0
        before_head(head)
        for part in range(HALVES):
            cols = slice(part * half, (part + 1) * half)
            prob_grads = mm_t(values, up_grad_ref[cols, :])
            probs = probs_ref[head, :, cols]
            delta = delta_ref[pl.ds(head, 1), cols]
            score_grads = (probs.astype(F32) * (prob_grads - delta)).astype(BF)
            value_grad += mm_t(up_grad_t_ref[pl.ds(at, HD), cols], probs)
            key_grad += mm_t(query_t_ref[pl.ds(at, HD), cols], score_grads)
            grads_t_ref[pl.ds(at, HD), cols] = (
                mm(key_t_ref[pl.ds(at, HD), :], score_grads) * SCALE
            ).astype(BF)
        grads_t_ref[pl.ds(pl.multiple_of(D + at, HD), HD), :] = (key_grad * SCALE).astype(BF)
        grads_t_ref[pl.ds(pl.multiple_of(2 * D + at, HD), HD), :] = value_grad.astype(BF)
        return carry

    lax.fori_loop(0, HEADS, one_head, 0, unroll=BACK_UNROLL)
    wait("attend")
    normed_grads = mm(attend_ref[...], grads_t_ref[...]).T
    hat, inverse = normalized(x)
    branch = norm_gradient(normed_grads, hat, inverse).astype(BF)
    return (grad_mid.astype(F32) + branch.astype(F32)).astype(BF)


BACK_UNROLL = 1


def whole_layer_kernel(
    index_ref, xg_ref, owners_hbm, saved_hbm, *rest
):
    weights_hbm, (out_ref, dest_ref), rest = rest[:4], rest[4:6], rest[6:]
    weights, kept, forward_work, backward_work = rest[:4], rest[4:9], rest[9:16], rest[16:23]
    owners_ref, next_x_ref, sem = rest[23:]
    my = index_ref[0]
    slots = out_ref.shape[0]
    copies = fetch(
        sem,
        [(weights_hbm[0].at[1], weights[0]), (owners_hbm, owners_ref)]
        + [(weights_hbm[i].at[1], weights[i]) for i in (1, 2, 3)]
        + [(saved_hbm.at[0], next_x_ref)],
    )
    order = dict(attend=0, owners=1, output=2, up=3, down=4)
    waited = set()

    def wait(name, part=0):
        if name in order and name not in waited:
            waited.add(name)
            copies[order[name]].wait()
            if name == "owners":
                forward_work[0][...] = key_bias(owners_ref[1], my, slots)

    forward_part(
        xg_ref[:, :D].astype(F32), weights, kept, forward_work, wait, lambda head: None
    )
    dest = destination_row(owners_ref.at[0], my, next_x_ref.shape[0])
    dest_ref[...] = jnp.broadcast_to(dest, dest_ref.shape)
    copies[5].wait()
    out_ref[:, D:] = mm(one_hot(dest, slots), next_x_ref[...]).astype(BF)
    out_ref[:, :D] = backward_part(
        xg_ref[:, :D].astype(F32), xg_ref[:, D:], weights, kept, backward_work, wait,
        lambda head: None,
    )


def forward_kernel(index_ref, rx_ref, owners_hbm, *rest):
    weights_hbm, rest = rest[:3], rest[3:]
    qkv_ref, probs_out, slope_out, norm_out, mixed_out = rest[:5]
    weights, kept, work = rest[5:8], (qkv_ref,) + rest[8:12], rest[12:19]
    owners_ref, in_sem, out_sem, probs_sem = rest[19:]
    my = index_ref[0]
    slots = rx_ref.shape[0]
    copies = fetch(
        in_sem,
        [(weights_hbm[0].at[0], weights[0]), (owners_hbm.at[0], owners_ref)]
        + [(weights_hbm[i].at[0], weights[i]) for i in (1, 2)],
    )
    order = dict(attend=0, owners=1, output=2, up=3)

    def wait(name, part=0):
        copies[order[name]].wait()
        if name == "owners":
            work[0][...] = key_bias(owners_ref[...], my, slots)

    def probs_copy(head):
        return pltpu.make_async_copy(kept[1].at[head], probs_out.at[head], probs_sem.at[head])

    forward_part(
        rx_ref[:, D:].astype(F32), tuple(weights) + (None,), kept, work, wait,
        lambda head: probs_copy(head).start(),
    )
    leaving = fetch(
        out_sem, [(kept[2], slope_out), (kept[3], norm_out), (kept[4], mixed_out)]
    )
    for head in range(HEADS):
        probs_copy(head).wait()
    for copy in leaving:
        copy.wait()


def backward_kernel(rx_ref, g_ref, qkv_ref, *rest):
    probs_hbm, slope_hbm, norm_hbm, mixed_hbm = rest[:4]
    weights_hbm, out_ref, rest = rest[4:8], rest[8], rest[9:]
    weights, kept, work = rest[:4], (qkv_ref,) + rest[4:8], rest[8:15]
    sem, probs_sem = rest[15:]
    parts = slope_hbm.shape[0]
    names = ["down"] + ["slope"] * parts + ["up", "norm", "output", "mixed", "attend"]

    def probs_copy(head):
        return pltpu.make_async_copy(probs_hbm.at[head], kept[1].at[head], probs_sem.at[head])

    copies = fetch(
        sem,
        [(weights_hbm[3].at[0], weights[3])]
        + [(slope_hbm.at[i], kept[2].at[i]) for i in range(parts)]
        + [
            (weights_hbm[2].at[0], weights[2]),
            (norm_hbm, kept[3]),
            (weights_hbm[1].at[0], weights[1]),
            (mixed_hbm, kept[4]),
            (weights_hbm[0].at[0], weights[0]),
        ],
    )
    for head in range(HEADS):
        probs_copy(head).start()

    def wait(name, part=0):
        copies[names.index(name) + part].wait()

    out_ref[...] = backward_part(
        rx_ref[:, D:].astype(F32), g_ref[...], weights, kept, work, wait,
        lambda head: probs_copy(head).wait(),
    )


SMEM_SPEC = pl.BlockSpec(memory_space=pltpu.SMEM)
VMEM_SPEC = pl.BlockSpec(memory_space=pltpu.VMEM)
HBM_SPEC = pl.BlockSpec(memory_space=pltpu.HBM)


def in_hbm(array):
    return pltpu.with_memory_space_constraint(array, pltpu.HBM)


def kept_shapes(slots, hidden):
    return [
        ((slots, 3 * D), BF),
        ((HEADS, slots, slots), BF),
        ((hidden // D, slots, D), F32),
        ((slots, D + LANES), F32),
        ((D, slots), F32),
    ]


def weight_scratch(weights):
    return [pltpu.VMEM(w.shape[1:], BF) for w in weights]


def forward_scratch(slots):
    return [
        pltpu.VMEM((slots, D), BF),
        pltpu.VMEM((slots, D), BF),
        pltpu.VMEM((D, slots), BF),
        pltpu.VMEM((slots, slots), F32),
        pltpu.VMEM((slots, slots), F32),
        pltpu.VMEM((8, slots), F32),
        pltpu.VMEM((8, slots), F32),
    ]


def backward_scratch(slots, hidden):
    return [
        pltpu.VMEM((slots, hidden), BF),
        pltpu.VMEM((slots, D), BF),
        pltpu.VMEM((D, slots), BF),
        pltpu.VMEM((D, slots), BF),
        pltpu.VMEM((D, slots), BF),
        pltpu.VMEM((HEADS, slots), F32),
        pltpu.VMEM((3 * D, slots), BF),
    ]


def call(kernel, outs, in_specs, out_specs, scratch, name):
    return pl.pallas_call(
        kernel,
        out_shape=outs,
        in_specs=in_specs,
        out_specs=out_specs,
        scratch_shapes=scratch,
        name=name,
        compiler_params=pltpu.CompilerParams(vmem_limit_bytes=40 << 20),
    )


def whole_layer(my_index, xg, owners, saved_inputs, weights):
    slots, hidden = xg.shape[0], weights[2].shape[2]
    points = saved_inputs.shape[1]
    return call(
        whole_layer_kernel,
        (jax.ShapeDtypeStruct((slots, 2 * D), BF), jax.ShapeDtypeStruct((8, points), F32)),
        [SMEM_SPEC, VMEM_SPEC] + [HBM_SPEC] * 6,
        (VMEM_SPEC, VMEM_SPEC),
        weight_scratch(weights)
        + [pltpu.VMEM(*k) for k in kept_shapes(slots, hidden)]
        + forward_scratch(slots)
        + backward_scratch(slots, hidden)
        + [
            pltpu.VMEM(owners.shape, jnp.int32),
            pltpu.VMEM((points, D), BF),
            pltpu.SemaphoreType.DMA((6,)),
        ],
        "whole_layer",
    )(my_index, xg, owners, saved_inputs, *weights)


def forward(my_index, rx, owners, weights):
    slots, hidden = rx.shape[0], weights[2].shape[2]
    shapes = kept_shapes(slots, hidden)
    return call(
        forward_kernel,
        (jax.ShapeDtypeStruct(*shapes[0]),) + tuple(pltpu.HBM(*k) for k in shapes[1:]),
        [SMEM_SPEC, VMEM_SPEC] + [HBM_SPEC] * 4,
        (VMEM_SPEC,) + (HBM_SPEC,) * 4,
        weight_scratch(weights[:3])
        + [pltpu.VMEM(*k) for k in shapes[1:]]
        + forward_scratch(slots)
        + [
            pltpu.VMEM(owners.shape[1:], jnp.int32),
            pltpu.SemaphoreType.DMA((4,)),
            pltpu.SemaphoreType.DMA((3,)),
            pltpu.SemaphoreType.DMA((HEADS,)),
        ],
        "layer_forward",
    )(my_index, rx, owners, *weights[:3])


def backward(rx, g, kept, weights):
    slots, hidden = g.shape[0], weights[2].shape[2]
    return call(
        backward_kernel,
        jax.ShapeDtypeStruct((slots, D), BF),
        [VMEM_SPEC] * 3 + [HBM_SPEC] * 8,
        VMEM_SPEC,
        weight_scratch(weights)
        + [pltpu.VMEM(*k) for k in kept_shapes(slots, hidden)[1:]]
        + backward_scratch(slots, hidden)
        + [
            pltpu.SemaphoreType.DMA((6 + hidden // D,)),
            pltpu.SemaphoreType.DMA((HEADS,)),
        ],
        "layer_backward",
    )(rx, g, kept[0], *(in_hbm(k) for k in kept[1:]), *weights)


def per_device(saved_inputs, output_grads, owner_ids, attend, output, up, down):
    devices = lax.axis_size("blk")
    points = saved_inputs.shape[1]
    slots = devices * 8
    my_index = lax.axis_index("blk").astype(jnp.int32).reshape(1)
    owners = in_hbm(owner_ids.reshape(2, devices * points // LANES, LANES))
    saved_inputs, output_grads = in_hbm(saved_inputs), in_hbm(output_grads)
    weights = tuple(in_hbm(w) for w in (attend, output, up, down))

    def exchange(rows):
        width = rows.shape[1]
        moved = lax.all_to_all(
            rows.reshape(devices, 8, width), "blk", split_axis=0, concat_axis=0, tiled=True
        )
        return moved.reshape(slots, width)

    dest_one, packed = call(
        route_kernel,
        (jax.ShapeDtypeStruct((8, points), F32), jax.ShapeDtypeStruct((slots, 2 * D), BF)),
        [SMEM_SPEC] + [HBM_SPEC] * 3,
        (VMEM_SPEC, VMEM_SPEC),
        [
            pltpu.VMEM(owners.shape[1:], jnp.int32),
            pltpu.VMEM((points, D), BF),
            pltpu.VMEM((points, D), BF),
            pltpu.SemaphoreType.DMA((3,)),
        ],
        "route",
    )(my_index, owners, saved_inputs, output_grads)
    xg = exchange(packed)
    result, dest_zero = whole_layer(my_index, xg, owners, saved_inputs, weights)
    rx = exchange(result)
    packed = call(
        repack_kernel, jax.ShapeDtypeStruct((slots, D), BF), [VMEM_SPEC] * 3, VMEM_SPEC, [], "repack"
    )(dest_one, dest_zero, rx)
    g_zero = exchange(packed)
    kept = forward(my_index, rx, owners, weights)
    result = backward(rx, g_zero, kept, weights)
    return call(
        unpack_kernel, jax.ShapeDtypeStruct((points, D), BF), [VMEM_SPEC] * 2, VMEM_SPEC, [], "unpack"
    )(dest_zero, exchange(result))


def solution(mesh):
    placed = (
        P(None, ("rep", "blk"), None),
        P(("rep", "blk"), None),
        P(None, "rep", None),
        P(),
        P(),
        P(),
        P(),
    )
    return jax.shard_map(
        per_device, mesh=mesh, in_specs=placed, out_specs=P(("rep", "blk"), None), check_vma=False
    )
```

time: 155 us -> 126 us (0.81)
  local copies, waits for them, and re-layouts: 32.2 us -> 0 us
  blocking collectives: 46.4 us -> 73.3 us
  starting transfers between devices: 23 us -> 5.7 us
  waiting for transfers between devices: 10.2 us -> 3.71 us
    all_to_all x2 -> x3, blocking collectives: 46.4 us -> 73.3 us  [exchange(): lax.all_to_all(rows.reshape(devices, 8, width), 'blk', split_axis=0, conc...]
    unnamed x48 -> x0, local copies, waits for them, and re-layouts: 24 us -> none
    all_to_all x3 -> x1, starting transfers between devices: 23 us -> 5.7 us  [exchange(): lax.all_to_all(rows.reshape(devices, 8, width), 'blk', split_axis=0, conc...]
    all_to_all x3 -> x1, waiting for transfers between devices: 10.2 us -> 3.71 us  [exchange(): lax.all_to_all(rows.reshape(devices, 8, width), 'blk', split_axis=0, conc...]
    squeeze x8 -> x0, local copies, waits for them, and re-layouts: 5.87 us -> none  [the longest x4 2.84 us: per_device(): saved_zero = forward(x_zero, bias[0], attend[0], output[0], up[0])]
    slice x2 -> x0, local copies, waits for them, and re-layouts: 2.31 us -> none  [the longest x1 1.25 us: per_device(): owners[0]]
    pallas_call x8 -> x6, Pallas kernels: 41.8 us -> 42.8 us  [the longest x1 17.2 us: whole_layer(): call(whole_layer_kernel, (jax.ShapeDtypeStruct((slots, 2 * D), BF), jax.S...]
  transfers between devices with their start and end apart: 3 -> 1, of which waited for: 2 -> 1; matrix products, arithmetic and copies ran while one was open for 2% -> 0% of each run, Pallas kernels for 12% -> 7%
where the time goes in v2:
time: 126 us
  blocking collectives  73.3 us (58%)
  Pallas kernels  42.8 us (34%)
  starting transfers between devices  5.7 us (5%)
  waiting for transfers between devices  3.71 us (3%)
    all_to_all x3, blocking collectives, exchange(): lax.all_to_all(rows.reshape(devices, 8, width), 'blk', split_axis=0, conc...  73.3 us
    pallas_call x1, Pallas kernels, whole_layer(): call(whole_layer_kernel, (jax.ShapeDtypeStruct((slots, 2 * D), BF), jax.S...  17.2 us
    pallas_call x1, Pallas kernels, backward(): call(backward_kernel, jax.ShapeDtypeStruct((slots, D), BF), [VMEM_SPEC] *...  12.4 us
    pallas_call x1, Pallas kernels, forward(): call(forward_kernel, (jax.ShapeDtypeStruct(*shapes[0]),) + tuple((pltpu.H...  9.35 us
    all_to_all x1, starting transfers between devices, exchange(): lax.all_to_all(rows.reshape(devices, 8, width), 'blk', split_axis=0, conc...  5.7 us
    all_to_all x1, waiting for transfers between devices, exchange(): lax.all_to_all(rows.reshape(devices, 8, width), 'blk', split_axis=0, conc...  3.71 us
  transfers between devices with their start and end apart: 1, of which 1 were waited for; matrix products, arithmetic and copies ran while one was open for 0% of the time, Pallas kernels for 7%

profile of v2, /device:TPU:1, one launch (start us, length us, event | category | flops | bytes accessed | tf_op | source)
XLA Modules:
  0.0 125.5 jit_solution(5311983249716226467)
XLA Ops:
  0.0 1.6 %route.1 = (f32[8,256]{1,0:T(8,128)S(1)}, bf16[512,512]{1,0:T(8,128)(2,1)S(1)}) custom-call(s32[1]{0:T(128)} %bitcast.index_ref, s32[2,128,128]{2,1,0:T(8,128)} %bitcast.19, bf16[2,256,256]{2,1,0:T(8,128)(2,1)} %saved_hbm.3, bf16[256,256]{1,0:T(8,128)(2,1)} %g_hbm.1), custom_call_target="tpu_custom_call" | custom-call | tf_op jit(solution)/shard_map/route/pallas_call | solution.py:503
  1.6 30.6 %all_to_all.20 = bf16[64,8,512]{2,1,0:T(8,128)(2,1)S(1)} all-to-all(bf16[64,8,512]{2,1,0:T(8,128)(2,1)S(1)} %bitcast.18), channel_id=1, replica_groups=mesh['blk'=64,'rep'=4] {'blk'}, dimensions={0} | all-to-all | bytes 1048576 | tf_op jit(solution)/shard_map/all_to_all | solution.py:498
  32.2 17.2 %whole_layer.1 = (bf16[512,512]{1,0:T(8,128)(2,1)S(1)}, f32[8,256]{1,0:T(8,128)S(1)}) custom-call(s32[1]{0:T(128)} %bitcast.index_ref, bf16[512,512]{1,0:T(8,128)(2,1)S(1)} %bitcast.13, s32[2,128,128]{2,1,0:T(8,128)} %bitcast.20, bf16[2,256,256]{2,1,0:T(8,128)(2,1)} %saved_hbm.3, bf16[2,256,768]{2,1,0:T(8,128)(2,1)} %rest_4_.1, ...), custom_call_target="tpu_custom_call" | custom-call | tf_op jit(solution)/shard_map/whole_layer/pallas_call | solution.py:430
  49.5 23.2 %all_to_all.21 = bf16[64,8,512]{2,1,0:T(8,128)(2,1)S(1)} all-to-all(bf16[64,8,512]{2,1,0:T(8,128)(2,1)S(1)} %bitcast.17), channel_id=1, replica_groups=mesh['blk'=64,'rep'=4] {'blk'}, dimensions={0} | all-to-all | bytes 1048576 | tf_op jit(solution)/shard_map/all_to_all | solution.py:498
  72.6 1.3 %repack.1 = bf16[512,256]{1,0:T(8,128)(2,1)} custom-call(f32[8,256]{1,0:T(8,128)S(1)} %get-tuple-element.17.dest_one_ref, f32[8,256]{1,0:T(8,128)S(1)} %get-tuple-element.15.dest_zero_ref.dest_ref, bf16[512,512]{1,0:T(8,128)(2,1)S(1)} %bitcast.10), custom_call_target="tpu_custom_call" | custom-call | tf_op jit(solution)/shard_map/repack/pallas_call | solution.py:519
  73.9 5.7 %all-to-all-start.2 = ((bf16[64,8,256]{2,1,0:T(8,128)(2,1)}), bf16[64,8,256]{2,1,0:T(8,128)(2,1)S(1)}, u32[]{:S(2)}, u32[]{:S(2)}) async-start(bf16[64,8,256]{2,1,0:T(8,128)(2,1)} %bitcast.6), calls=%async_computation.2 | async-start | bytes 524288 | tf_op jit(solution)/shard_map/all_to_all | solution.py:498
  79.6 9.3 %layer_forward.1 = (bf16[512,768]{1,0:T(8,128)(2,1)S(1)}, bf16[8,512,512]{2,1,0:T(8,128)(2,1)}, f32[4,512,256]{2,1,0:T(8,128)}, f32[512,384]{1,0:T(8,128)}, f32[256,512]{1,0:T(8,128)}) custom-call(s32[1]{0:T(128)} %bitcast.index_ref, bf16[512,512]{1,0:T(8,128)(2,1)S(1)} %bitcast.11, s32[2,128,128]{2,1,0:T(8,128)} %bitcast.21, bf16[2,256,768]{2,1,0:T(8,128)(2,1)} %rest_4_.1, ...), custom_call_target="tpu_custom_call" | custom-call | tf_op jit(solution)/shard_map/layer_forward/pallas_call | solution.py:451
  89.0 3.7 %all-to-all-done.2 = bf16[64,8,256]{2,1,0:T(8,128)(2,1)S(1)} async-done(((bf16[64,8,256]{2,1,0:T(8,128)(2,1)}), bf16[64,8,256]{2,1,0:T(8,128)(2,1)S(1)}, u32[]{:S(2)}, u32[]{:S(2)}) %all-to-all-start.2) | async-done | bytes 262176 | tf_op jit(solution)/shard_map/all_to_all | solution.py:498
  92.7 12.4 %layer_backward.1 = bf16[512,256]{1,0:T(8,128)(2,1)S(1)} custom-call(bf16[512,512]{1,0:T(8,128)(2,1)S(1)} %bitcast.12, bf16[512,256]{1,0:T(8,128)(2,1)S(1)} %bitcast.14, bf16[512,768]{1,0:T(8,128)(2,1)S(1)} %get-tuple-element.18.qkv_ref, bf16[8,512,512]{2,1,0:T(8,128)(2,1)} %get-tuple-element.19.rest_0_, f32[4,512,256]{2,1,0:T(8,128)} %get-tuple-element.20.rest_1_, ...), custom_call_target="tpu_custom_call" | custom-call | tf_op jit(solution)/shard_map/layer_backward/pallas_call | solution.py:471
  105.1 19.5 %all_to_all.22 = bf16[64,8,256]{2,1,0:T(8,128)(2,1)S(1)} all-to-all(bf16[64,8,256]{2,1,0:T(8,128)(2,1)S(1)} %bitcast.15), channel_id=1, replica_groups=mesh['blk'=64,'rep'=4] {'blk'}, dimensions={0} | all-to-all | bytes 524288 | tf_op jit(solution)/shard_map/all_to_all | solution.py:498
  124.6 0.9 unpack.1
Async XLA Ops:
  73.9 18.8 %all-to-all-start.2 = ((bf16[64,8,256]{2,1,0:T(8,128)(2,1)}), bf16[64,8,256]{2,1,0:T(8,128)(2,1)S(1)}, u32[]{:S(2)}, u32[]{:S(2)}) async-start(bf16[64,8,256]{2,1,0:T(8,128)(2,1)} %bitcast.6), calls=%async_computation.2 | async-start | bytes 524288 | tf_op jit(solution)/shard_map/all_to_all | solution.py:498

commit v3 on v2

--- a/solution.py
+++ b/solution.py
@@ -120,16 +120,14 @@
     return (0.5 + 0.5 * bend) * (1.0 + (1.0 - bend) * rise)
 
 
-HALVES = 2
 LANES = 128
 
 
-def forward_part(x, weights, kept, work, wait, after_head):
+def forward_part(x, weights, kept, work, wait, after_head, unroll):
     attend_ref, output_ref, up_ref, _ = weights
     qkv_ref, probs_ref, slope_ref, norm_ref, mixed_t_ref = kept
     bias_ref, query_ref, value_t_ref, even_ref, odd_ref, even_max_ref, odd_max_ref = work
     slots = x.shape[0]
-    half = slots // HALVES
     normed, _ = normalized(x)
     wait("attend")
     qkv = mm(normed.astype(BF), attend_ref[...]).astype(BF)
@@ -139,21 +137,18 @@
     query_ref[...] = jnp.where(lane == 0, jnp.ones((slots, D), BF), qkv[:, :D])
     wait("owners")
 
-    def score_half(keys, queries, part, scores_ref, max_ref):
-        cols = slice(part * half, (part + 1) * half)
+    def score(keys, queries, scores_ref, max_ref):
         scores = mm_t(keys, queries)
-        scores_ref[:, cols] = scores
-        max_ref[:, cols] = jnp.broadcast_to(jnp.max(scores, axis=0, keepdims=True), (8, half))
-
-    def soft_half(head, part, scores_ref, max_ref):
-        cols = slice(part * half, (part + 1) * half)
-        largest = max_ref[0:1, cols]
-        exponent = jnp.exp2((scores_ref[:, cols] - largest) * (SCALE * LOG2E))
+        scores_ref[...] = scores
+        max_ref[...] = jnp.broadcast_to(jnp.max(scores, axis=0, keepdims=True), (8, slots))
+
+    def soften(head, scores_ref, max_ref):
+        exponent = jnp.exp2((scores_ref[...] - max_ref[0:1, :]) * (SCALE * LOG2E))
         total = jnp.sum(exponent, axis=0, keepdims=True)
         probs = (exponent * (1.0 / total)).astype(BF)
-        probs_ref[head, :, cols] = probs
+        probs_ref[head] = probs
         at = pl.multiple_of(head * HD, HD)
-        mixed_t_ref[pl.ds(at, HD), cols] = mm(value_t_ref[pl.ds(at, HD), :], probs)
+        mixed_t_ref[pl.ds(at, HD), :] = mm(value_t_ref[pl.ds(at, HD), :], probs)
 
     bias = bias_ref[...]
     first_keys = jnp.where(
@@ -163,16 +158,12 @@
     )
     first_queries = jnp.where(lane == D - 1, jnp.ones((slots, D), BF), qkv[:, :D])
     bias_ref[...] = jnp.where(lane == 0, bias, jnp.zeros_like(bias))
-    for part in range(HALVES):
-        rows = slice(part * half, (part + 1) * half)
-        score_half(first_keys, first_queries[rows], part, even_ref, even_max_ref)
+    score(first_keys, first_queries, even_ref, even_max_ref)
 
     def step(head, following, here, here_max, there, there_max):
         keys = jnp.where(head_lanes((slots, D), following), qkv_ref[:, D : 2 * D], bias_ref[...])
-        for part in range(HALVES):
-            rows = slice(part * half, (part + 1) * half)
-            score_half(keys, query_ref[rows, :], part, there, there_max)
-            soft_half(head, part, here, here_max)
+        score(keys, query_ref[...], there, there_max)
+        soften(head, here, here_max)
         after_head(head)
 
     def pair(index, carry):
@@ -181,7 +172,7 @@
         step(2 * index + 1, following, odd_ref, odd_max_ref, even_ref, even_max_ref)
         return carry
 
-    lax.fori_loop(0, HEADS // 2, pair, 0)
+    lax.fori_loop(0, HEADS // 2, pair, 0, unroll=unroll)
     attended = mixed_t_ref[...].astype(BF).T
     wait("output")
     mixed = mm(attended, output_ref[...]).astype(BF).astype(F32)
@@ -194,12 +185,11 @@
         slope_ref[part] = gelu_slope(mm(rounded, up_ref[:, part * D : (part + 1) * D]))
 
 
-def backward_part(x, g, weights, kept, work, wait, before_head):
+def backward_part(x, g, weights, kept, work, wait, before_heads):
     attend_ref, output_ref, up_ref, down_ref = weights
     qkv_ref, probs_ref, slope_ref, norm_ref, mixed_t_ref = kept
     pre_grad_ref, up_grad_ref, up_grad_t_ref, query_t_ref, key_t_ref, delta_ref, grads_t_ref = work
     slots = g.shape[0]
-    half = slots // HALVES
     query_t_ref[...] = qkv_ref[:, :D].T
     key_t_ref[...] = qkv_ref[:, D : 2 * D].T
     wait("down")
@@ -225,37 +215,30 @@
             weighted[head * HD : (head + 1) * HD], axis=0, keepdims=True
         )
 
+    before_heads()
+
     def one_head(head, carry):
         values = jnp.where(
             head_lanes((slots, D), head), qkv_ref[:, 2 * D :], jnp.zeros((slots, D), BF)
         )
         at = pl.multiple_of(head * HD, HD)
-        key_grad = value_grad = 0.0
-        before_head(head)
-        for part in range(HALVES):
-            cols = slice(part * half, (part + 1) * half)
-            prob_grads = mm_t(values, up_grad_ref[cols, :])
-            probs = probs_ref[head, :, cols]
-            delta = delta_ref[pl.ds(head, 1), cols]
-            score_grads = (probs.astype(F32) * (prob_grads - delta)).astype(BF)
-            value_grad += mm_t(up_grad_t_ref[pl.ds(at, HD), cols], probs)
-            key_grad += mm_t(query_t_ref[pl.ds(at, HD), cols], score_grads)
-            grads_t_ref[pl.ds(at, HD), cols] = (
-                mm(key_t_ref[pl.ds(at, HD), :], score_grads) * SCALE
-            ).astype(BF)
+        prob_grads = mm_t(values, up_grad_ref[...])
+        probs = probs_ref[head]
+        delta = delta_ref[pl.ds(head, 1), :]
+        score_grads = (probs.astype(F32) * (prob_grads - delta)).astype(BF)
+        value_grad = mm_t(up_grad_t_ref[pl.ds(at, HD), :], probs)
+        key_grad = mm_t(query_t_ref[pl.ds(at, HD), :], score_grads)
+        grads_t_ref[pl.ds(at, HD), :] = (mm(key_t_ref[pl.ds(at, HD), :], score_grads) * SCALE).astype(BF)
         grads_t_ref[pl.ds(pl.multiple_of(D + at, HD), HD), :] = (key_grad * SCALE).astype(BF)
         grads_t_ref[pl.ds(pl.multiple_of(2 * D + at, HD), HD), :] = value_grad.astype(BF)
         return carry
 
-    lax.fori_loop(0, HEADS, one_head, 0, unroll=BACK_UNROLL)
+    lax.fori_loop(0, HEADS, one_head, 0, unroll=HEADS)
     wait("attend")
     normed_grads = mm(attend_ref[...], grads_t_ref[...]).T
     hat, inverse = normalized(x)
     branch = norm_gradient(normed_grads, hat, inverse).astype(BF)
     return (grad_mid.astype(F32) + branch.astype(F32)).astype(BF)
-
-
-BACK_UNROLL = 1
 
 
 def whole_layer_kernel(
@@ -283,7 +266,7 @@
                 forward_work[0][...] = key_bias(owners_ref[1], my, slots)
 
     forward_part(
-        xg_ref[:, :D].astype(F32), weights, kept, forward_work, wait, lambda head: None
+        xg_ref[:, :D].astype(F32), weights, kept, forward_work, wait, lambda head: None, HEADS // 2
     )
     dest = destination_row(owners_ref.at[0], my, next_x_ref.shape[0])
     dest_ref[...] = jnp.broadcast_to(dest, dest_ref.shape)
@@ -291,15 +274,15 @@
     out_ref[:, D:] = mm(one_hot(dest, slots), next_x_ref[...]).astype(BF)
     out_ref[:, :D] = backward_part(
         xg_ref[:, :D].astype(F32), xg_ref[:, D:], weights, kept, backward_work, wait,
-        lambda head: None,
+        lambda: None,
     )
 
 
 def forward_kernel(index_ref, rx_ref, owners_hbm, *rest):
     weights_hbm, rest = rest[:3], rest[3:]
-    qkv_ref, probs_out, slope_out, norm_out, mixed_out = rest[:5]
-    weights, kept, work = rest[5:8], (qkv_ref,) + rest[8:12], rest[12:19]
-    owners_ref, in_sem, out_sem, probs_sem = rest[19:]
+    qkv_ref, norm_ref, mixed_ref, probs_out, slope_out = rest[:5]
+    weights, kept, work = rest[5:8], (qkv_ref,) + rest[8:10] + (norm_ref, mixed_ref), rest[10:17]
+    owners_ref, in_sem, out_sem, probs_sem = rest[17:]
     my = index_ref[0]
     slots = rx_ref.shape[0]
     copies = fetch(
@@ -319,10 +302,10 @@
 
     forward_part(
         rx_ref[:, D:].astype(F32), tuple(weights) + (None,), kept, work, wait,
-        lambda head: probs_copy(head).start(),
+        lambda head: probs_copy(head).start(), 1,
     )
     leaving = fetch(
-        out_sem, [(kept[2], slope_out), (kept[3], norm_out), (kept[4], mixed_out)]
+        out_sem, [(kept[2].at[i], slope_out.at[i]) for i in range(slope_out.shape[0])]
     )
     for head in range(HEADS):
         probs_copy(head).wait()
@@ -330,38 +313,39 @@
         copy.wait()
 
 
-def backward_kernel(rx_ref, g_ref, qkv_ref, *rest):
-    probs_hbm, slope_hbm, norm_hbm, mixed_hbm = rest[:4]
-    weights_hbm, out_ref, rest = rest[4:8], rest[8], rest[9:]
-    weights, kept, work = rest[:4], (qkv_ref,) + rest[4:8], rest[8:15]
-    sem, probs_sem = rest[15:]
+def backward_kernel(rx_ref, g_ref, qkv_ref, norm_ref, mixed_ref, probs_hbm, slope_hbm, *rest):
+    weights_hbm, out_ref, rest = rest[:4], rest[4], rest[5:]
+    weights, kept, work = rest[:4], (qkv_ref,) + rest[4:6] + (norm_ref, mixed_ref), rest[6:13]
+    sem, probs_sem = rest[13:]
     parts = slope_hbm.shape[0]
-    names = ["down"] + ["slope"] * parts + ["up", "norm", "output", "mixed", "attend"]
+    pairs = [(weights_hbm[3].at[0], weights[3])]
+    pairs += [(slope_hbm.at[i], kept[2].at[i]) for i in range(parts)]
+    pairs += [(weights_hbm[i].at[0], weights[i]) for i in (2, 1, 0)]
+    copies = [pltpu.make_async_copy(x, y, sem.at[i]) for i, (x, y) in enumerate(pairs)]
+    names = ["down"] + ["slope"] * parts + ["up", "output", "attend"]
 
     def probs_copy(head):
         return pltpu.make_async_copy(probs_hbm.at[head], kept[1].at[head], probs_sem.at[head])
 
-    copies = fetch(
-        sem,
-        [(weights_hbm[3].at[0], weights[3])]
-        + [(slope_hbm.at[i], kept[2].at[i]) for i in range(parts)]
-        + [
-            (weights_hbm[2].at[0], weights[2]),
-            (norm_hbm, kept[3]),
-            (weights_hbm[1].at[0], weights[1]),
-            (mixed_hbm, kept[4]),
-            (weights_hbm[0].at[0], weights[0]),
-        ],
-    )
-    for head in range(HEADS):
-        probs_copy(head).start()
+    for copy in copies[: 1 + parts]:
+        copy.start()
 
     def wait(name, part=0):
-        copies[names.index(name) + part].wait()
+        if name in names:
+            copies[names.index(name) + part].wait()
+        if name == "down":
+            for copy in copies[1 + parts :]:
+                copy.start()
+        if name == "slope":
+            for head in (2 * part, 2 * part + 1):
+                probs_copy(head).start()
+
+    def before_heads():
+        for head in range(HEADS):
+            probs_copy(head).wait()
 
     out_ref[...] = backward_part(
-        rx_ref[:, D:].astype(F32), g_ref[...], weights, kept, work, wait,
-        lambda head: probs_copy(head).wait(),
+        rx_ref[:, D:].astype(F32), g_ref[...], weights, kept, work, wait, before_heads
     )
 
 
@@ -450,16 +434,17 @@
     shapes = kept_shapes(slots, hidden)
     return call(
         forward_kernel,
-        (jax.ShapeDtypeStruct(*shapes[0]),) + tuple(pltpu.HBM(*k) for k in shapes[1:]),
+        tuple(jax.ShapeDtypeStruct(*shapes[i]) for i in (0, 3, 4))
+        + tuple(pltpu.HBM(*k) for k in shapes[1:3]),
         [SMEM_SPEC, VMEM_SPEC] + [HBM_SPEC] * 4,
-        (VMEM_SPEC,) + (HBM_SPEC,) * 4,
+        (VMEM_SPEC,) * 3 + (HBM_SPEC,) * 2,
         weight_scratch(weights[:3])
-        + [pltpu.VMEM(*k) for k in shapes[1:]]
+        + [pltpu.VMEM(*k) for k in shapes[1:3]]
         + forward_scratch(slots)
         + [
             pltpu.VMEM(owners.shape[1:], jnp.int32),
             pltpu.SemaphoreType.DMA((4,)),
-            pltpu.SemaphoreType.DMA((3,)),
+            pltpu.SemaphoreType.DMA((hidden // D,)),
             pltpu.SemaphoreType.DMA((HEADS,)),
         ],
         "layer_forward",
@@ -471,17 +456,17 @@
     return call(
         backward_kernel,
         jax.ShapeDtypeStruct((slots, D), BF),
-        [VMEM_SPEC] * 3 + [HBM_SPEC] * 8,
+        [VMEM_SPEC] * 5 + [HBM_SPEC] * 6,
         VMEM_SPEC,
         weight_scratch(weights)
-        + [pltpu.VMEM(*k) for k in kept_shapes(slots, hidden)[1:]]
+        + [pltpu.VMEM(*k) for k in kept_shapes(slots, hidden)[1:3]]
         + backward_scratch(slots, hidden)
         + [
-            pltpu.SemaphoreType.DMA((6 + hidden // D,)),
+            pltpu.SemaphoreType.DMA((4 + hidden // D,)),
             pltpu.SemaphoreType.DMA((HEADS,)),
         ],
         "layer_backward",
-    )(rx, g, kept[0], *(in_hbm(k) for k in kept[1:]), *weights)
+    )(rx, g, *kept[:3], *(in_hbm(k) for k in kept[3:]), *weights)
 
 
 def per_device(saved_inputs, output_grads, owner_ids, attend, output, up, down):

time: 126 us -> 118 us (0.937)
  Pallas kernels: 42.8 us -> 35 us
    pallas_call x1, Pallas kernels: 17.2 us -> 13.5 us  [whole_layer(): call(whole_layer_kernel, (jax.ShapeDtypeStruct((slots, 2 * D), BF), jax.S...]
    pallas_call x1, Pallas kernels: 12.4 us -> 8.86 us  [backward(): call(backward_kernel, jax.ShapeDtypeStruct((slots, D), BF), [VMEM_SPEC] *...]
where the time goes in v3:
time: 118 us
  blocking collectives  72.7 us (62%)
  Pallas kernels  35 us (30%)
  starting transfers between devices  5.69 us (5%)
  waiting for transfers between devices  4.29 us (4%)
    all_to_all x3, blocking collectives, exchange(): lax.all_to_all(rows.reshape(devices, 8, width), 'blk', split_axis=0, conc...  72.7 us
    pallas_call x1, Pallas kernels, whole_layer(): call(whole_layer_kernel, (jax.ShapeDtypeStruct((slots, 2 * D), BF), jax.S...  13.5 us
    pallas_call x1, Pallas kernels, backward(): call(backward_kernel, jax.ShapeDtypeStruct((slots, D), BF), [VMEM_SPEC] *...  8.86 us
    pallas_call x1, Pallas kernels, forward(): call(forward_kernel, tuple((jax.ShapeDtypeStruct(*shapes[i]) for i in (0,...  8.78 us
    all_to_all x1, starting transfers between devices, exchange(): lax.all_to_all(rows.reshape(devices, 8, width), 'blk', split_axis=0, conc...  5.69 us
    all_to_all x1, waiting for transfers between devices, exchange(): lax.all_to_all(rows.reshape(devices, 8, width), 'blk', split_axis=0, conc...  4.29 us
  transfers between devices with their start and end apart: 1, of which 1 were waited for; matrix products, arithmetic and copies ran while one was open for 0% of the time, Pallas kernels for 7%

profile of v3, /device:TPU:1, one launch (start us, length us, event | category | flops | bytes accessed | tf_op | source)
XLA Modules:
  0.0 117.7 jit_solution(6895228920733829796)
XLA Ops:
  0.0 1.6 %route.1 = (f32[8,256]{1,0:T(8,128)S(1)}, bf16[512,512]{1,0:T(8,128)(2,1)S(1)}) custom-call(s32[1]{0:T(128)} %bitcast.index_ref, s32[2,128,128]{2,1,0:T(8,128)} %bitcast.19, bf16[2,256,256]{2,1,0:T(8,128)(2,1)} %saved_hbm.3, bf16[256,256]{1,0:T(8,128)(2,1)} %g_hbm.1), custom_call_target="tpu_custom_call" | custom-call | tf_op jit(solution)/shard_map/route/pallas_call | solution.py:488
  1.6 30.6 %all_to_all.20 = bf16[64,8,512]{2,1,0:T(8,128)(2,1)S(1)} all-to-all(bf16[64,8,512]{2,1,0:T(8,128)(2,1)S(1)} %bitcast.18), channel_id=1, replica_groups=mesh['blk'=64,'rep'=4] {'blk'}, dimensions={0} | all-to-all | bytes 1048576 | tf_op jit(solution)/shard_map/all_to_all | solution.py:483
  32.2 13.5 %whole_layer.1 = (bf16[512,512]{1,0:T(8,128)(2,1)S(1)}, f32[8,256]{1,0:T(8,128)S(1)}) custom-call(s32[1]{0:T(128)} %bitcast.index_ref, bf16[512,512]{1,0:T(8,128)(2,1)S(1)} %bitcast.13, s32[2,128,128]{2,1,0:T(8,128)} %bitcast.20, bf16[2,256,256]{2,1,0:T(8,128)(2,1)} %saved_hbm.3, bf16[2,256,768]{2,1,0:T(8,128)(2,1)} %rest_0_.5, ...), custom_call_target="tpu_custom_call" | custom-call | tf_op jit(solution)/shard_map/whole_layer/pallas_call | solution.py:414
  45.8 23.2 %all_to_all.21 = bf16[64,8,512]{2,1,0:T(8,128)(2,1)S(1)} all-to-all(bf16[64,8,512]{2,1,0:T(8,128)(2,1)S(1)} %bitcast.17), channel_id=1, replica_groups=mesh['blk'=64,'rep'=4] {'blk'}, dimensions={0} | all-to-all | bytes 1048576 | tf_op jit(solution)/shard_map/all_to_all | solution.py:483
  68.9 1.3 %repack.1 = bf16[512,256]{1,0:T(8,128)(2,1)} custom-call(f32[8,256]{1,0:T(8,128)S(1)} %get-tuple-element.17.dest_one_ref, f32[8,256]{1,0:T(8,128)S(1)} %get-tuple-element.15.dest_zero_ref.dest_ref, bf16[512,512]{1,0:T(8,128)(2,1)S(1)} %bitcast.10), custom_call_target="tpu_custom_call" | custom-call | tf_op jit(solution)/shard_map/repack/pallas_call | solution.py:504
  70.2 5.7 %all-to-all-start.2 = ((bf16[64,8,256]{2,1,0:T(8,128)(2,1)}), bf16[64,8,256]{2,1,0:T(8,128)(2,1)S(1)}, u32[]{:S(2)}, u32[]{:S(2)}) async-start(bf16[64,8,256]{2,1,0:T(8,128)(2,1)} %bitcast.6), calls=%async_computation.2 | async-start | bytes 524288 | tf_op jit(solution)/shard_map/all_to_all | solution.py:483
  75.9 8.8 %layer_forward.1 = (bf16[512,768]{1,0:T(8,128)(2,1)S(1)}, f32[512,384]{1,0:T(8,128)S(1)}, f32[256,512]{1,0:T(8,128)S(1)}, bf16[8,512,512]{2,1,0:T(8,128)(2,1)}, f32[4,512,256]{2,1,0:T(8,128)}) custom-call(s32[1]{0:T(128)} %bitcast.index_ref, bf16[512,512]{1,0:T(8,128)(2,1)S(1)} %bitcast.11, s32[2,128,128]{2,1,0:T(8,128)} %bitcast.21, ...), custom_call_target="tpu_custom_call" | custom-call | tf_op jit(solution)/shard_map/layer_forward/pallas_call | solution.py:435
  84.7 4.3 %all-to-all-done.2 = bf16[64,8,256]{2,1,0:T(8,128)(2,1)S(1)} async-done(((bf16[64,8,256]{2,1,0:T(8,128)(2,1)}), bf16[64,8,256]{2,1,0:T(8,128)(2,1)S(1)}, u32[]{:S(2)}, u32[]{:S(2)}) %all-to-all-start.2) | async-done | bytes 262176 | tf_op jit(solution)/shard_map/all_to_all | solution.py:483
  89.0 8.9 %layer_backward.1 = bf16[512,256]{1,0:T(8,128)(2,1)S(1)} custom-call(bf16[512,512]{1,0:T(8,128)(2,1)S(1)} %bitcast.12, bf16[512,256]{1,0:T(8,128)(2,1)S(1)} %bitcast.14, bf16[512,768]{1,0:T(8,128)(2,1)S(1)} %get-tuple-element.18.qkv_ref, f32[512,384]{1,0:T(8,128)S(1)} %get-tuple-element.19.norm_ref, f32[256,512]{1,0:T(8,128)S(1)} %get-tuple-element.20.mixed_ref, ...), custom_call_target="tpu_custom_call" | custom-call | tf_op jit(solution)/shard_map/layer_backward/pallas_call | solution.py:456
  97.9 18.9 %all_to_all.22 = bf16[64,8,256]{2,1,0:T(8,128)(2,1)S(1)} all-to-all(bf16[64,8,256]{2,1,0:T(8,128)(2,1)S(1)} %bitcast.15), channel_id=1, replica_groups=mesh['blk'=64,'rep'=4] {'blk'}, dimensions={0} | all-to-all | bytes 524288 | tf_op jit(solution)/shard_map/all_to_all | solution.py:483
  116.8 0.9 unpack.1
Async XLA Ops:
  70.2 18.8 %all-to-all-start.2 = ((bf16[64,8,256]{2,1,0:T(8,128)(2,1)}), bf16[64,8,256]{2,1,0:T(8,128)(2,1)S(1)}, u32[]{:S(2)}, u32[]{:S(2)}) async-start(bf16[64,8,256]{2,1,0:T(8,128)(2,1)} %bitcast.6), calls=%async_computation.2 | async-start | bytes 524288 | tf_op jit(solution)/shard_map/all_to_all | solution.py:483

commit v4 on v3

--- a/solution.py
+++ b/solution.py
@@ -124,15 +124,18 @@
 
 
 def forward_part(x, weights, kept, work, wait, after_head, unroll):
-    attend_ref, output_ref, up_ref, _ = weights
-    qkv_ref, probs_ref, slope_ref, norm_ref, mixed_t_ref = kept
-    bias_ref, query_ref, value_t_ref, even_ref, odd_ref, even_max_ref, odd_max_ref = work
+    attend_ref, output_ref = weights[:2]
+    value_ref, query_t_ref, key_t_ref, probs_ref, norm_ref, mixed_t_ref = kept
+    bias_ref, query_ref, key_ref, value_t_ref, even_ref, odd_ref, even_max_ref, odd_max_ref = work
     slots = x.shape[0]
     normed, _ = normalized(x)
     wait("attend")
     qkv = mm(normed.astype(BF), attend_ref[...]).astype(BF)
-    qkv_ref[...] = qkv
+    key_ref[...] = qkv[:, D : 2 * D]
+    value_ref[...] = qkv[:, 2 * D :]
     value_t_ref[...] = qkv[:, 2 * D :].T
+    query_t_ref[...] = qkv[:, :D].T
+    key_t_ref[...] = qkv[:, D : 2 * D].T
     lane = iota((slots, D), 1)
     query_ref[...] = jnp.where(lane == 0, jnp.ones((slots, D), BF), qkv[:, :D])
     wait("owners")
@@ -161,7 +164,7 @@
     score(first_keys, first_queries, even_ref, even_max_ref)
 
     def step(head, following, here, here_max, there, there_max):
-        keys = jnp.where(head_lanes((slots, D), following), qkv_ref[:, D : 2 * D], bias_ref[...])
+        keys = jnp.where(head_lanes((slots, D), following), key_ref[...], bias_ref[...])
         score(keys, query_ref[...], there, there_max)
         soften(head, here, here_max)
         after_head(head)
@@ -179,28 +182,21 @@
     hat, inverse = normalized(x + mixed)
     norm_ref[:, :D] = hat
     norm_ref[:, D:] = jnp.broadcast_to(inverse, (slots, LANES))
-    rounded = hat.astype(BF)
-    wait("up")
-    for part in range(slope_ref.shape[0]):
-        slope_ref[part] = gelu_slope(mm(rounded, up_ref[:, part * D : (part + 1) * D]))
 
 
 def backward_part(x, g, weights, kept, work, wait, before_heads):
     attend_ref, output_ref, up_ref, down_ref = weights
-    qkv_ref, probs_ref, slope_ref, norm_ref, mixed_t_ref = kept
-    pre_grad_ref, up_grad_ref, up_grad_t_ref, query_t_ref, key_t_ref, delta_ref, grads_t_ref = work
+    value_ref, query_t_ref, key_t_ref, probs_ref, norm_ref, mixed_t_ref = kept
+    pre_grad_ref, up_grad_ref, up_grad_t_ref, delta_ref, grads_t_ref = work
     slots = g.shape[0]
-    query_t_ref[...] = qkv_ref[:, :D].T
-    key_t_ref[...] = qkv_ref[:, D : 2 * D].T
+    rounded = norm_ref[:, :D].astype(BF)
+    wait("up")
     wait("down")
-    for part in range(slope_ref.shape[0]):
-        rows = slice(part * D, (part + 1) * D)
-        hidden_grad = mm_t(g, down_ref[rows, :])
-        wait("slope", part)
-        pre_grad_ref[:, rows] = (slope_ref[part] * hidden_grad).astype(BF)
-    wait("up")
+    for part in range(up_ref.shape[1] // D):
+        cols = slice(part * D, (part + 1) * D)
+        slope = gelu_slope(mm(rounded, up_ref[:, cols]))
+        pre_grad_ref[:, cols] = (slope * mm_t(g, down_ref[cols, :])).astype(BF)
     normed_grad = mm_t(pre_grad_ref[...], up_ref[...])
-    wait("norm")
     grad_mid = (
         g.astype(F32) + norm_gradient(normed_grad, norm_ref[:, :D], norm_ref[:, D : D + 1])
     ).astype(BF)
@@ -208,18 +204,15 @@
     up_grad_ref[...] = mm_t(grad_mid, output_ref[...]).astype(BF)
     up_grad_t = mm_t(output_ref[...], grad_mid).astype(BF)
     up_grad_t_ref[...] = up_grad_t
-    wait("mixed")
     weighted = mixed_t_ref[...] * up_grad_t.astype(F32)
     for head in range(HEADS):
         delta_ref[head : head + 1, :] = jnp.sum(
             weighted[head * HD : (head + 1) * HD], axis=0, keepdims=True
         )
 
-    before_heads()
-
     def one_head(head, carry):
         values = jnp.where(
-            head_lanes((slots, D), head), qkv_ref[:, 2 * D :], jnp.zeros((slots, D), BF)
+            head_lanes((slots, D), head), value_ref[...], jnp.zeros((slots, D), BF)
         )
         at = pl.multiple_of(head * HD, HD)
         prob_grads = mm_t(values, up_grad_ref[...])
@@ -233,6 +226,7 @@
         grads_t_ref[pl.ds(pl.multiple_of(2 * D + at, HD), HD), :] = value_grad.astype(BF)
         return carry
 
+    before_heads()
     lax.fori_loop(0, HEADS, one_head, 0, unroll=HEADS)
     wait("attend")
     normed_grads = mm(attend_ref[...], grads_t_ref[...]).T
@@ -245,7 +239,7 @@
     index_ref, xg_ref, owners_hbm, saved_hbm, *rest
 ):
     weights_hbm, (out_ref, dest_ref), rest = rest[:4], rest[4:6], rest[6:]
-    weights, kept, forward_work, backward_work = rest[:4], rest[4:9], rest[9:16], rest[16:23]
+    weights, kept, forward_work, backward_work = rest[:4], rest[4:10], rest[10:18], rest[18:23]
     owners_ref, next_x_ref, sem = rest[23:]
     my = index_ref[0]
     slots = out_ref.shape[0]
@@ -258,7 +252,7 @@
     order = dict(attend=0, owners=1, output=2, up=3, down=4)
     waited = set()
 
-    def wait(name, part=0):
+    def wait(name):
         if name in order and name not in waited:
             waited.add(name)
             copies[order[name]].wait()
@@ -266,7 +260,8 @@
                 forward_work[0][...] = key_bias(owners_ref[1], my, slots)
 
     forward_part(
-        xg_ref[:, :D].astype(F32), weights, kept, forward_work, wait, lambda head: None, HEADS // 2
+        xg_ref[:, :D].astype(F32), weights, kept, forward_work, wait, lambda head: None,
+        HEADS // 2,
     )
     dest = destination_row(owners_ref.at[0], my, next_x_ref.shape[0])
     dest_ref[...] = jnp.broadcast_to(dest, dest_ref.shape)
@@ -279,65 +274,68 @@
 
 
 def forward_kernel(index_ref, rx_ref, owners_hbm, *rest):
-    weights_hbm, rest = rest[:3], rest[3:]
-    qkv_ref, norm_ref, mixed_ref, probs_out, slope_out = rest[:5]
-    weights, kept, work = rest[5:8], (qkv_ref,) + rest[8:10] + (norm_ref, mixed_ref), rest[10:17]
-    owners_ref, in_sem, out_sem, probs_sem = rest[17:]
+    attend_hbm, output_hbm, up_hbm = rest[:3]
+    value_ref, query_t_ref, key_t_ref, norm_ref, mixed_t_ref, up_ref, probs_out = rest[3:10]
+    attend_ref, output_ref, probs_ref = rest[10:13]
+    work = rest[13:21]
+    owners_ref, in_sem, probs_sem = rest[21:]
     my = index_ref[0]
     slots = rx_ref.shape[0]
     copies = fetch(
         in_sem,
-        [(weights_hbm[0].at[0], weights[0]), (owners_hbm.at[0], owners_ref)]
-        + [(weights_hbm[i].at[0], weights[i]) for i in (1, 2)],
-    )
-    order = dict(attend=0, owners=1, output=2, up=3)
-
-    def wait(name, part=0):
+        [
+            (attend_hbm.at[0], attend_ref),
+            (owners_hbm.at[0], owners_ref),
+            (output_hbm.at[0], output_ref),
+            (up_hbm.at[0], up_ref),
+        ],
+    )
+    order = dict(attend=0, owners=1, output=2)
+
+    def wait(name):
         copies[order[name]].wait()
         if name == "owners":
             work[0][...] = key_bias(owners_ref[...], my, slots)
 
     def probs_copy(head):
-        return pltpu.make_async_copy(kept[1].at[head], probs_out.at[head], probs_sem.at[head])
+        return pltpu.make_async_copy(probs_ref.at[head], probs_out.at[head], probs_sem.at[head])
 
     forward_part(
-        rx_ref[:, D:].astype(F32), tuple(weights) + (None,), kept, work, wait,
-        lambda head: probs_copy(head).start(), 1,
-    )
-    leaving = fetch(
-        out_sem, [(kept[2].at[i], slope_out.at[i]) for i in range(slope_out.shape[0])]
-    )
+        rx_ref[:, D:].astype(F32),
+        (attend_ref, output_ref),
+        (value_ref, query_t_ref, key_t_ref, probs_ref, norm_ref, mixed_t_ref),
+        work, wait, lambda head: probs_copy(head).start(), 1,
+    )
+    copies[3].wait()
     for head in range(HEADS):
         probs_copy(head).wait()
-    for copy in leaving:
-        copy.wait()
-
-
-def backward_kernel(rx_ref, g_ref, qkv_ref, norm_ref, mixed_ref, probs_hbm, slope_hbm, *rest):
-    weights_hbm, out_ref, rest = rest[:4], rest[4], rest[5:]
-    weights, kept, work = rest[:4], (qkv_ref,) + rest[4:6] + (norm_ref, mixed_ref), rest[6:13]
-    sem, probs_sem = rest[13:]
-    parts = slope_hbm.shape[0]
-    pairs = [(weights_hbm[3].at[0], weights[3])]
-    pairs += [(slope_hbm.at[i], kept[2].at[i]) for i in range(parts)]
-    pairs += [(weights_hbm[i].at[0], weights[i]) for i in (2, 1, 0)]
-    copies = [pltpu.make_async_copy(x, y, sem.at[i]) for i, (x, y) in enumerate(pairs)]
-    names = ["down"] + ["slope"] * parts + ["up", "output", "attend"]
+
+
+def backward_kernel(
+    rx_ref, g_ref, value_ref, query_t_ref, key_t_ref, norm_ref, mixed_t_ref, up_ref, probs_hbm,
+    attend_hbm, output_hbm, down_hbm,
+    out_ref,
+    attend_ref, output_ref, down_ref, probs_ref, *rest,
+):
+    work, (sem, probs_sem) = rest[:5], rest[5:]
+    copies = fetch(
+        sem,
+        [
+            (down_hbm.at[0], down_ref),
+            (output_hbm.at[0], output_ref),
+            (attend_hbm.at[0], attend_ref),
+        ],
+    )
+    order = dict(down=0, output=1, attend=2)
 
     def probs_copy(head):
-        return pltpu.make_async_copy(probs_hbm.at[head], kept[1].at[head], probs_sem.at[head])
-
-    for copy in copies[: 1 + parts]:
-        copy.start()
-
-    def wait(name, part=0):
-        if name in names:
-            copies[names.index(name) + part].wait()
+        return pltpu.make_async_copy(probs_hbm.at[head], probs_ref.at[head], probs_sem.at[head])
+
+    def wait(name):
+        if name in order:
+            copies[order[name]].wait()
         if name == "down":
-            for copy in copies[1 + parts :]:
-                copy.start()
-        if name == "slope":
-            for head in (2 * part, 2 * part + 1):
+            for head in range(HEADS):
                 probs_copy(head).start()
 
     def before_heads():
@@ -345,7 +343,9 @@
             probs_copy(head).wait()
 
     out_ref[...] = backward_part(
-        rx_ref[:, D:].astype(F32), g_ref[...], weights, kept, work, wait, before_heads
+        rx_ref[:, D:].astype(F32), g_ref[...], (attend_ref, output_ref, up_ref, down_ref),
+        (value_ref, query_t_ref, key_t_ref, probs_ref, norm_ref, mixed_t_ref),
+        work, wait, before_heads,
     )
 
 
@@ -358,11 +358,12 @@
     return pltpu.with_memory_space_constraint(array, pltpu.HBM)
 
 
-def kept_shapes(slots, hidden):
+def kept_shapes(slots):
     return [
-        ((slots, 3 * D), BF),
+        ((slots, D), BF),
+        ((D, slots), BF),
+        ((D, slots), BF),
         ((HEADS, slots, slots), BF),
-        ((hidden // D, slots, D), F32),
         ((slots, D + LANES), F32),
         ((D, slots), F32),
     ]
@@ -374,6 +375,7 @@
 
 def forward_scratch(slots):
     return [
+        pltpu.VMEM((slots, D), BF),
         pltpu.VMEM((slots, D), BF),
         pltpu.VMEM((slots, D), BF),
         pltpu.VMEM((D, slots), BF),
@@ -388,8 +390,6 @@
     return [
         pltpu.VMEM((slots, hidden), BF),
         pltpu.VMEM((slots, D), BF),
-        pltpu.VMEM((D, slots), BF),
-        pltpu.VMEM((D, slots), BF),
         pltpu.VMEM((D, slots), BF),
         pltpu.VMEM((HEADS, slots), F32),
         pltpu.VMEM((3 * D, slots), BF),
@@ -417,7 +417,7 @@
         [SMEM_SPEC, VMEM_SPEC] + [HBM_SPEC] * 6,
         (VMEM_SPEC, VMEM_SPEC),
         weight_scratch(weights)
-        + [pltpu.VMEM(*k) for k in kept_shapes(slots, hidden)]
+        + [pltpu.VMEM(*k) for k in kept_shapes(slots)]
         + forward_scratch(slots)
         + backward_scratch(slots, hidden)
         + [
@@ -430,43 +430,41 @@
 
 
 def forward(my_index, rx, owners, weights):
-    slots, hidden = rx.shape[0], weights[2].shape[2]
-    shapes = kept_shapes(slots, hidden)
+    slots = rx.shape[0]
+    shapes = kept_shapes(slots)
+    attend, output, up = weights[:3]
     return call(
         forward_kernel,
-        tuple(jax.ShapeDtypeStruct(*shapes[i]) for i in (0, 3, 4))
-        + tuple(pltpu.HBM(*k) for k in shapes[1:3]),
+        tuple(jax.ShapeDtypeStruct(*shapes[i]) for i in (0, 1, 2, 4, 5))
+        + (jax.ShapeDtypeStruct(up.shape[1:], BF), pltpu.HBM(*shapes[3])),
         [SMEM_SPEC, VMEM_SPEC] + [HBM_SPEC] * 4,
-        (VMEM_SPEC,) * 3 + (HBM_SPEC,) * 2,
-        weight_scratch(weights[:3])
-        + [pltpu.VMEM(*k) for k in shapes[1:3]]
+        (VMEM_SPEC,) * 6 + (HBM_SPEC,),
+        weight_scratch((attend, output))
+        + [pltpu.VMEM(*shapes[3])]
         + forward_scratch(slots)
         + [
             pltpu.VMEM(owners.shape[1:], jnp.int32),
             pltpu.SemaphoreType.DMA((4,)),
-            pltpu.SemaphoreType.DMA((hidden // D,)),
             pltpu.SemaphoreType.DMA((HEADS,)),
         ],
         "layer_forward",
-    )(my_index, rx, owners, *weights[:3])
+    )(my_index, rx, owners, attend, output, up)
 
 
 def backward(rx, g, kept, weights):
-    slots, hidden = g.shape[0], weights[2].shape[2]
+    slots = g.shape[0]
+    attend, output, up, down = weights
     return call(
         backward_kernel,
         jax.ShapeDtypeStruct((slots, D), BF),
-        [VMEM_SPEC] * 5 + [HBM_SPEC] * 6,
+        [VMEM_SPEC] * 8 + [HBM_SPEC] * 4,
         VMEM_SPEC,
-        weight_scratch(weights)
-        + [pltpu.VMEM(*k) for k in kept_shapes(slots, hidden)[1:3]]
-        + backward_scratch(slots, hidden)
-        + [
-            pltpu.SemaphoreType.DMA((4 + hidden // D,)),
-            pltpu.SemaphoreType.DMA((HEADS,)),
-        ],
+        weight_scratch((attend, output, down))
+        + [pltpu.VMEM(*kept_shapes(slots)[3])]
+        + backward_scratch(slots, up.shape[2])
+        + [pltpu.SemaphoreType.DMA((3,)), pltpu.SemaphoreType.DMA((HEADS,))],
         "layer_backward",
-    )(rx, g, *kept[:3], *(in_hbm(k) for k in kept[3:]), *weights)
+    )(rx, g, *kept[:6], in_hbm(kept[6]), attend, output, down)
 
 
 def per_device(saved_inputs, output_grads, owner_ids, attend, output, up, down):

time: 118 us -> 117 us (level)
  Pallas kernels: 35 us -> 32.6 us
  waiting for transfers between devices: 4.29 us -> 6.59 us
  blocking collectives: 72.7 us -> 71.5 us
    all_to_all x1, waiting for transfers between devices: 4.29 us -> 6.59 us  [exchange(): lax.all_to_all(rows.reshape(devices, 8, width), 'blk', split_axis=0, conc...]
    pallas_call x1, Pallas kernels: 8.78 us -> 6.48 us  [forward(): call(forward_kernel, tuple((jax.ShapeDtypeStruct(*shapes[i]) for i in (0,...]
    all_to_all x3, blocking collectives: 72.7 us -> 71.5 us  [exchange(): lax.all_to_all(rows.reshape(devices, 8, width), 'blk', split_axis=0, conc...]
  transfers between devices with their start and end apart: 1 -> 1, of which waited for: 1 -> 1; matrix products, arithmetic and copies ran while one was open for 0% -> 0% of each run, Pallas kernels for 7% -> 6%
where the time goes in v4:
time: 117 us; the launch traced here: 116 us
  blocking collectives  71.5 us (61%)
  Pallas kernels  32.6 us (28%)
  waiting for transfers between devices  6.59 us (6%)
  starting transfers between devices  5.69 us (5%)
    all_to_all x3, blocking collectives, exchange(): lax.all_to_all(rows.reshape(devices, 8, width), 'blk', split_axis=0, conc...  71.5 us
    pallas_call x1, Pallas kernels, whole_layer(): call(whole_layer_kernel, (jax.ShapeDtypeStruct((slots, 2 * D), BF), jax.S...  13.2 us
    pallas_call x1, Pallas kernels, backward(): call(backward_kernel, jax.ShapeDtypeStruct((slots, D), BF), [VMEM_SPEC] *...  9.16 us
    all_to_all x1, waiting for transfers between devices, exchange(): lax.all_to_all(rows.reshape(devices, 8, width), 'blk', split_axis=0, conc...  6.59 us
    pallas_call x1, Pallas kernels, forward(): call(forward_kernel, tuple((jax.ShapeDtypeStruct(*shapes[i]) for i in (0,...  6.48 us
    all_to_all x1, starting transfers between devices, exchange(): lax.all_to_all(rows.reshape(devices, 8, width), 'blk', split_axis=0, conc...  5.69 us
  transfers between devices with their start and end apart: 1, of which 1 were waited for; matrix products, arithmetic and copies ran while one was open for 0% of the time, Pallas kernels for 6%

profile of v4, /device:TPU:1, one launch (start us, length us, event | category | flops | bytes accessed | tf_op | source)
XLA Modules:
  0.0 116.4 jit_solution(12484587157187141968)
XLA Ops:
  0.0 1.6 %route.1 = (f32[8,256]{1,0:T(8,128)S(1)}, bf16[512,512]{1,0:T(8,128)(2,1)S(1)}) custom-call(s32[1]{0:T(128)} %bitcast.index_ref, s32[2,128,128]{2,1,0:T(8,128)} %bitcast.19, bf16[2,256,256]{2,1,0:T(8,128)(2,1)} %saved_hbm.3, bf16[256,256]{1,0:T(8,128)(2,1)} %g_hbm.1), custom_call_target="tpu_custom_call" | custom-call | tf_op jit(solution)/shard_map/route/pallas_call | solution.py:486
  1.6 30.6 %all_to_all.20 = bf16[64,8,512]{2,1,0:T(8,128)(2,1)S(1)} all-to-all(bf16[64,8,512]{2,1,0:T(8,128)(2,1)S(1)} %bitcast.18), channel_id=1, replica_groups=mesh['blk'=64,'rep'=4] {'blk'}, dimensions={0} | all-to-all | bytes 1048576 | tf_op jit(solution)/shard_map/all_to_all | solution.py:481
  32.2 13.2 %whole_layer.1 = (bf16[512,512]{1,0:T(8,128)(2,1)S(1)}, f32[8,256]{1,0:T(8,128)S(1)}) custom-call(s32[1]{0:T(128)} %bitcast.index_ref, bf16[512,512]{1,0:T(8,128)(2,1)S(1)} %bitcast.13, s32[2,128,128]{2,1,0:T(8,128)} %bitcast.20, bf16[2,256,256]{2,1,0:T(8,128)(2,1)} %saved_hbm.3, bf16[2,256,768]{2,1,0:T(8,128)(2,1)} %attend_hbm.1, ...), custom_call_target="tpu_custom_call" | custom-call | tf_op jit(solution)/shard_map/whole_layer/pallas_call | solution.py:414
  45.4 23.2 %all_to_all.21 = bf16[64,8,512]{2,1,0:T(8,128)(2,1)S(1)} all-to-all(bf16[64,8,512]{2,1,0:T(8,128)(2,1)S(1)} %bitcast.17), channel_id=1, replica_groups=mesh['blk'=64,'rep'=4] {'blk'}, dimensions={0} | all-to-all | bytes 1048576 | tf_op jit(solution)/shard_map/all_to_all | solution.py:481
  68.6 1.3 %repack.1 = bf16[512,256]{1,0:T(8,128)(2,1)} custom-call(f32[8,256]{1,0:T(8,128)S(1)} %get-tuple-element.19.dest_one_ref, f32[8,256]{1,0:T(8,128)S(1)} %get-tuple-element.17.dest_zero_ref.dest_ref, bf16[512,512]{1,0:T(8,128)(2,1)S(1)} %bitcast.10), custom_call_target="tpu_custom_call" | custom-call | tf_op jit(solution)/shard_map/repack/pallas_call | solution.py:502
  69.9 5.7 %all-to-all-start.2 = ((bf16[64,8,256]{2,1,0:T(8,128)(2,1)}), bf16[64,8,256]{2,1,0:T(8,128)(2,1)S(1)}, u32[]{:S(2)}, u32[]{:S(2)}) async-start(bf16[64,8,256]{2,1,0:T(8,128)(2,1)} %bitcast.6), calls=%async_computation.2 | async-start | bytes 524288 | tf_op jit(solution)/shard_map/all_to_all | solution.py:481
  75.6 6.5 %layer_forward.1 = (bf16[512,256]{1,0:T(8,128)(2,1)S(1)}, bf16[256,512]{1,0:T(8,128)(2,1)S(1)}, bf16[256,512]{1,0:T(8,128)(2,1)S(1)}, f32[512,384]{1,0:T(8,128)S...) custom-call(s32[1]{0:T(128)} %bitcast.index_ref, ...), custom_call_target="tpu_custom_call" | custom-call | tf_op jit(solution)/shard_map/layer_forward/pallas_call | solution.py:436
  82.1 6.6 %all-to-all-done.2 = bf16[64,8,256]{2,1,0:T(8,128)(2,1)S(1)} async-done(((bf16[64,8,256]{2,1,0:T(8,128)(2,1)}), bf16[64,8,256]{2,1,0:T(8,128)(2,1)S(1)}, u32[]{:S(2)}, u32[]{:S(2)}) %all-to-all-start.2) | async-done | bytes 262176 | tf_op jit(solution)/shard_map/all_to_all | solution.py:481
  88.7 9.2 %layer_backward.1 = bf16[512,256]{1,0:T(8,128)(2,1)S(1)} custom-call(bf16[512,512]{1,0:T(8,128)(2,1)S(1)} %bitcast.12, bf16[512,256]{1,0:T(8,128)(2,1)S(1)} %bitcast.14, bf16[512,256]{1,0:T(8,128)(2,1)S(1)} %get-tuple-element.20.value_ref, bf16[256,512]{1,0:T(8,128)(2,1)S(1)} %get-tuple-element.21.query_t_ref, ...), custom_call_target="tpu_custom_call" | custom-call | tf_op jit(solution)/shard_map/layer_backward/pallas_call | solution.py:457
  97.8 17.6 %all_to_all.22 = bf16[64,8,256]{2,1,0:T(8,128)(2,1)S(1)} all-to-all(bf16[64,8,256]{2,1,0:T(8,128)(2,1)S(1)} %bitcast.15), channel_id=1, replica_groups=mesh['blk'=64,'rep'=4] {'blk'}, dimensions={0} | all-to-all | bytes 524288 | tf_op jit(solution)/shard_map/all_to_all | solution.py:481
  115.5 0.9 unpack.1
Async XLA Ops:
  69.9 18.8 %all-to-all-start.2 = ((bf16[64,8,256]{2,1,0:T(8,128)(2,1)}), bf16[64,8,256]{2,1,0:T(8,128)(2,1)S(1)}, u32[]{:S(2)}, u32[]{:S(2)}) async-start(bf16[64,8,256]{2,1,0:T(8,128)(2,1)} %bitcast.6), calls=%async_computation.2 | async-start | bytes 524288 | tf_op jit(solution)/shard_map/all_to_all | solution.py:481

commit v5 on v4

--- a/solution.py
+++ b/solution.py
@@ -184,18 +184,18 @@
     norm_ref[:, D:] = jnp.broadcast_to(inverse, (slots, LANES))
 
 
-def backward_part(x, g, weights, kept, work, wait, before_heads):
+def backward_part(x_ref, g, weights, kept, work, wait, before_heads):
     attend_ref, output_ref, up_ref, down_ref = weights
     value_ref, query_t_ref, key_t_ref, probs_ref, norm_ref, mixed_t_ref = kept
     pre_grad_ref, up_grad_ref, up_grad_t_ref, delta_ref, grads_t_ref = work
     slots = g.shape[0]
     rounded = norm_ref[:, :D].astype(BF)
     wait("up")
+    blocks = [slice(at, at + D) for at in range(0, up_ref.shape[1], D)]
+    slopes = [gelu_slope(mm(rounded, up_ref[:, block])) for block in blocks]
     wait("down")
-    for part in range(up_ref.shape[1] // D):
-        cols = slice(part * D, (part + 1) * D)
-        slope = gelu_slope(mm(rounded, up_ref[:, cols]))
-        pre_grad_ref[:, cols] = (slope * mm_t(g, down_ref[cols, :])).astype(BF)
+    for block, slope in zip(blocks, slopes):
+        pre_grad_ref[:, block] = (slope * mm_t(g, down_ref[block, :])).astype(BF)
     normed_grad = mm_t(pre_grad_ref[...], up_ref[...])
     grad_mid = (
         g.astype(F32) + norm_gradient(normed_grad, norm_ref[:, :D], norm_ref[:, D : D + 1])
@@ -230,34 +230,32 @@
     lax.fori_loop(0, HEADS, one_head, 0, unroll=HEADS)
     wait("attend")
     normed_grads = mm(attend_ref[...], grads_t_ref[...]).T
-    hat, inverse = normalized(x)
+    wait("x")
+    hat, inverse = normalized(x_ref[...].astype(F32))
     branch = norm_gradient(normed_grads, hat, inverse).astype(BF)
     return (grad_mid.astype(F32) + branch.astype(F32)).astype(BF)
 
 
-def whole_layer_kernel(
-    index_ref, xg_ref, owners_hbm, saved_hbm, *rest
-):
-    weights_hbm, (out_ref, dest_ref), rest = rest[:4], rest[4:6], rest[6:]
-    weights, kept, forward_work, backward_work = rest[:4], rest[4:10], rest[10:18], rest[18:23]
-    owners_ref, next_x_ref, sem = rest[23:]
+def prefetch_kernel(owners_hbm, saved_hbm, *rest):
+    weights_hbm, (owners_ref, next_x_ref), weights = rest[1:5], rest[5:7], rest[7:11]
+    copies = fetch(
+        rest[11],
+        [(owners_hbm, owners_ref), (saved_hbm.at[0], next_x_ref)]
+        + [(hbm.at[1], ref) for hbm, ref in zip(weights_hbm, weights)],
+    )
+    for copy in copies:
+        copy.wait()
+
+
+def whole_layer_kernel(index_ref, xg_ref, owners_ref, next_x_ref, *rest):
+    weights, (out_ref, dest_ref), rest = rest[:4], rest[4:6], rest[6:]
+    kept, forward_work, backward_work = rest[:6], rest[6:14], rest[14:19]
     my = index_ref[0]
     slots = out_ref.shape[0]
-    copies = fetch(
-        sem,
-        [(weights_hbm[0].at[1], weights[0]), (owners_hbm, owners_ref)]
-        + [(weights_hbm[i].at[1], weights[i]) for i in (1, 2, 3)]
-        + [(saved_hbm.at[0], next_x_ref)],
-    )
-    order = dict(attend=0, owners=1, output=2, up=3, down=4)
-    waited = set()
+    forward_work[0][...] = key_bias(owners_ref[1], my, slots)
 
     def wait(name):
-        if name in order and name not in waited:
-            waited.add(name)
-            copies[order[name]].wait()
-            if name == "owners":
-                forward_work[0][...] = key_bias(owners_ref[1], my, slots)
+        return None
 
     forward_part(
         xg_ref[:, :D].astype(F32), weights, kept, forward_work, wait, lambda head: None,
@@ -265,20 +263,20 @@
     )
     dest = destination_row(owners_ref.at[0], my, next_x_ref.shape[0])
     dest_ref[...] = jnp.broadcast_to(dest, dest_ref.shape)
-    copies[5].wait()
     out_ref[:, D:] = mm(one_hot(dest, slots), next_x_ref[...]).astype(BF)
     out_ref[:, :D] = backward_part(
-        xg_ref[:, :D].astype(F32), xg_ref[:, D:], weights, kept, backward_work, wait,
+        xg_ref.at[:, pl.ds(0, D)], xg_ref[:, D:], weights, kept, backward_work, wait,
         lambda: None,
     )
 
 
 def forward_kernel(index_ref, rx_ref, owners_hbm, *rest):
-    attend_hbm, output_hbm, up_hbm = rest[:3]
-    value_ref, query_t_ref, key_t_ref, norm_ref, mixed_t_ref, up_ref, probs_out = rest[3:10]
-    attend_ref, output_ref, probs_ref = rest[10:13]
-    work = rest[13:21]
-    owners_ref, in_sem, probs_sem = rest[21:]
+    attend_hbm, output_hbm, up_hbm, down_hbm = rest[:4]
+    value_ref, norm_ref, mixed_t_ref, up_ref, down_ref = rest[4:9]
+    probs_out, x_out, query_out, key_out = rest[9:13]
+    attend_ref, output_ref, probs_ref, query_t_ref, key_t_ref = rest[13:18]
+    work = rest[18:26]
+    owners_ref, in_sem, probs_sem, out_sem = rest[26:]
     my = index_ref[0]
     slots = rx_ref.shape[0]
     copies = fetch(
@@ -288,6 +286,8 @@
             (owners_hbm.at[0], owners_ref),
             (output_hbm.at[0], output_ref),
             (up_hbm.at[0], up_ref),
+            (down_hbm.at[0], down_ref),
+            (rx_ref.at[:, pl.ds(D, D)], x_out),
         ],
     )
     order = dict(attend=0, owners=1, output=2)
@@ -306,44 +306,46 @@
         (value_ref, query_t_ref, key_t_ref, probs_ref, norm_ref, mixed_t_ref),
         work, wait, lambda head: probs_copy(head).start(), 1,
     )
-    copies[3].wait()
+    for copy in copies[3:] + fetch(out_sem, [(query_t_ref, query_out), (key_t_ref, key_out)]):
+        copy.wait()
     for head in range(HEADS):
         probs_copy(head).wait()
 
 
 def backward_kernel(
-    rx_ref, g_ref, value_ref, query_t_ref, key_t_ref, norm_ref, mixed_t_ref, up_ref, probs_hbm,
-    attend_hbm, output_hbm, down_hbm,
+    g_ref, value_ref, norm_ref, mixed_t_ref, up_ref, down_ref, probs_hbm,
+    x_hbm, query_hbm, key_hbm, attend_hbm, output_hbm,
     out_ref,
-    attend_ref, output_ref, down_ref, probs_ref, *rest,
+    attend_ref, output_ref, x_ref, probs_ref, query_t_ref, key_t_ref, *rest,
 ):
     work, (sem, probs_sem) = rest[:5], rest[5:]
-    copies = fetch(
-        sem,
-        [
-            (down_hbm.at[0], down_ref),
-            (output_hbm.at[0], output_ref),
-            (attend_hbm.at[0], attend_ref),
-        ],
-    )
-    order = dict(down=0, output=1, attend=2)
+    pairs = [(output_hbm.at[0], output_ref), (query_hbm, query_t_ref), (key_hbm, key_t_ref)]
+    pairs += [(attend_hbm.at[0], attend_ref), (x_hbm, x_ref)]
+    copies = [pltpu.make_async_copy(a, b, sem.at[i]) for i, (a, b) in enumerate(pairs)]
+    for copy in copies[:3]:
+        copy.start()
+    order = dict(output=0, attend=3, x=4)
 
     def probs_copy(head):
         return pltpu.make_async_copy(probs_hbm.at[head], probs_ref.at[head], probs_sem.at[head])
+
+    for head in range(HEADS):
+        probs_copy(head).start()
+    for copy in copies[3:]:
+        copy.start()
 
     def wait(name):
         if name in order:
             copies[order[name]].wait()
-        if name == "down":
-            for head in range(HEADS):
-                probs_copy(head).start()
 
     def before_heads():
+        copies[1].wait()
+        copies[2].wait()
         for head in range(HEADS):
             probs_copy(head).wait()
 
     out_ref[...] = backward_part(
-        rx_ref[:, D:].astype(F32), g_ref[...], (attend_ref, output_ref, up_ref, down_ref),
+        x_ref, g_ref[...], (attend_ref, output_ref, up_ref, down_ref),
         (value_ref, query_t_ref, key_t_ref, probs_ref, norm_ref, mixed_t_ref),
         work, wait, before_heads,
     )
@@ -408,63 +410,71 @@
     )
 
 
-def whole_layer(my_index, xg, owners, saved_inputs, weights):
-    slots, hidden = xg.shape[0], weights[2].shape[2]
-    points = saved_inputs.shape[1]
+def prefetch(after, owners, saved_inputs, weights):
+    shapes = [(owners.shape, jnp.int32), (saved_inputs.shape[1:], BF)]
+    shapes += [(w.shape[1:], BF) for w in weights]
+    return call(
+        prefetch_kernel,
+        tuple(jax.ShapeDtypeStruct(*k) for k in shapes),
+        [HBM_SPEC] * 2 + [VMEM_SPEC] + [HBM_SPEC] * 4,
+        (VMEM_SPEC,) * 6,
+        [pltpu.SemaphoreType.DMA((6,))],
+        "prefetch",
+    )(owners, saved_inputs, after, *weights)
+
+
+def whole_layer(my_index, xg, owners, next_x, weights):
+    slots, hidden, points = xg.shape[0], weights[2].shape[1], next_x.shape[0]
     return call(
         whole_layer_kernel,
         (jax.ShapeDtypeStruct((slots, 2 * D), BF), jax.ShapeDtypeStruct((8, points), F32)),
-        [SMEM_SPEC, VMEM_SPEC] + [HBM_SPEC] * 6,
+        [SMEM_SPEC] + [VMEM_SPEC] * 7,
         (VMEM_SPEC, VMEM_SPEC),
-        weight_scratch(weights)
-        + [pltpu.VMEM(*k) for k in kept_shapes(slots)]
+        [pltpu.VMEM(*k) for k in kept_shapes(slots)]
         + forward_scratch(slots)
-        + backward_scratch(slots, hidden)
-        + [
-            pltpu.VMEM(owners.shape, jnp.int32),
-            pltpu.VMEM((points, D), BF),
-            pltpu.SemaphoreType.DMA((6,)),
-        ],
+        + backward_scratch(slots, hidden),
         "whole_layer",
-    )(my_index, xg, owners, saved_inputs, *weights)
+    )(my_index, xg, owners, next_x, *weights)
 
 
 def forward(my_index, rx, owners, weights):
     slots = rx.shape[0]
     shapes = kept_shapes(slots)
-    attend, output, up = weights[:3]
+    attend, output, up, down = weights
     return call(
         forward_kernel,
-        tuple(jax.ShapeDtypeStruct(*shapes[i]) for i in (0, 1, 2, 4, 5))
-        + (jax.ShapeDtypeStruct(up.shape[1:], BF), pltpu.HBM(*shapes[3])),
-        [SMEM_SPEC, VMEM_SPEC] + [HBM_SPEC] * 4,
-        (VMEM_SPEC,) * 6 + (HBM_SPEC,),
+        tuple(jax.ShapeDtypeStruct(*shapes[i]) for i in (0, 4, 5))
+        + tuple(jax.ShapeDtypeStruct(w.shape[1:], BF) for w in (up, down))
+        + tuple(pltpu.HBM(*k) for k in (shapes[3], shapes[0], shapes[1], shapes[2])),
+        [SMEM_SPEC, VMEM_SPEC] + [HBM_SPEC] * 5,
+        (VMEM_SPEC,) * 5 + (HBM_SPEC,) * 4,
         weight_scratch((attend, output))
-        + [pltpu.VMEM(*shapes[3])]
+        + [pltpu.VMEM(*shapes[i]) for i in (3, 1, 2)]
         + forward_scratch(slots)
         + [
             pltpu.VMEM(owners.shape[1:], jnp.int32),
-            pltpu.SemaphoreType.DMA((4,)),
+            pltpu.SemaphoreType.DMA((6,)),
             pltpu.SemaphoreType.DMA((HEADS,)),
+            pltpu.SemaphoreType.DMA((2,)),
         ],
         "layer_forward",
-    )(my_index, rx, owners, attend, output, up)
-
-
-def backward(rx, g, kept, weights):
+    )(my_index, rx, owners, *weights)
+
+
+def backward(g, kept, weights):
     slots = g.shape[0]
-    attend, output, up, down = weights
+    attend, output, up, _ = weights
     return call(
         backward_kernel,
         jax.ShapeDtypeStruct((slots, D), BF),
-        [VMEM_SPEC] * 8 + [HBM_SPEC] * 4,
+        [VMEM_SPEC] * 6 + [HBM_SPEC] * 6,
         VMEM_SPEC,
-        weight_scratch((attend, output, down))
-        + [pltpu.VMEM(*kept_shapes(slots)[3])]
+        weight_scratch((attend, output))
+        + [pltpu.VMEM(*kept_shapes(slots)[i]) for i in (0, 3, 1, 2)]
         + backward_scratch(slots, up.shape[2])
-        + [pltpu.SemaphoreType.DMA((3,)), pltpu.SemaphoreType.DMA((HEADS,))],
+        + [pltpu.SemaphoreType.DMA((5,)), pltpu.SemaphoreType.DMA((HEADS,))],
         "layer_backward",
-    )(rx, g, *kept[:6], in_hbm(kept[6]), attend, output, down)
+    )(g, *kept[:5], *(in_hbm(k) for k in kept[5:]), attend, output)
 
 
 def per_device(saved_inputs, output_grads, owner_ids, attend, output, up, down):
@@ -497,14 +507,15 @@
         "route",
     )(my_index, owners, saved_inputs, output_grads)
     xg = exchange(packed)
-    result, dest_zero = whole_layer(my_index, xg, owners, saved_inputs, weights)
+    fetched = prefetch(dest_one, owners, saved_inputs, weights)
+    result, dest_zero = whole_layer(my_index, xg, *fetched[:2], fetched[2:])
     rx = exchange(result)
     packed = call(
         repack_kernel, jax.ShapeDtypeStruct((slots, D), BF), [VMEM_SPEC] * 3, VMEM_SPEC, [], "repack"
     )(dest_one, dest_zero, rx)
     g_zero = exchange(packed)
     kept = forward(my_index, rx, owners, weights)
-    result = backward(rx, g_zero, kept, weights)
+    result = backward(g_zero, kept, weights)
     return call(
         unpack_kernel, jax.ShapeDtypeStruct((points, D), BF), [VMEM_SPEC] * 2, VMEM_SPEC, [], "unpack"
     )(dest_zero, exchange(result))

time: 117 us -> 116 us (level)
  blocking collectives: 71.5 us -> 41 us
  waiting for transfers between devices: 6.59 us -> 22.4 us
  starting transfers between devices: 5.69 us -> 18.8 us
    all_to_all x3 -> x2, blocking collectives: 71.5 us -> 41 us  [exchange(): lax.all_to_all(rows.reshape(devices, 8, width), 'blk', split_axis=0, conc...]
    all_to_all x1 -> x2, waiting for transfers between devices: 6.59 us -> 22.4 us  [exchange(): lax.all_to_all(rows.reshape(devices, 8, width), 'blk', split_axis=0, conc...]
    all_to_all x1 -> x2, starting transfers between devices: 5.69 us -> 18.8 us  [exchange(): lax.all_to_all(rows.reshape(devices, 8, width), 'blk', split_axis=0, conc...]
    pallas_call x1, Pallas kernels: 13.2 us -> 11.2 us  [whole_layer(): call(whole_layer_kernel, (jax.ShapeDtypeStruct((slots, 2 * D), BF), jax.S...]
    pallas_call x0 -> x1, Pallas kernels: none -> 1.55 us  [prefetch(): call(prefetch_kernel, tuple((jax.ShapeDtypeStruct(*k) for k in shapes)),...]
  transfers between devices with their start and end apart: 1 -> 2, of which waited for: 1 -> 2; matrix products, arithmetic and copies ran while one was open for 0% -> 0% of each run, Pallas kernels for 6% -> 7%
where the time goes in v5:
time: 116 us; the launch traced here: 115 us
  blocking collectives  41 us (35%)
  Pallas kernels  33.1 us (29%)
  waiting for transfers between devices  22.4 us (19%)
  starting transfers between devices  18.8 us (16%)
    all_to_all x2, blocking collectives, exchange(): lax.all_to_all(rows.reshape(devices, 8, width), 'blk', split_axis=0, conc...  41 us
    all_to_all x2, waiting for transfers between devices, exchange(): lax.all_to_all(rows.reshape(devices, 8, width), 'blk', split_axis=0, conc...  22.4 us
    all_to_all x2, starting transfers between devices, exchange(): lax.all_to_all(rows.reshape(devices, 8, width), 'blk', split_axis=0, conc...  18.8 us
    pallas_call x1, Pallas kernels, whole_layer(): call(whole_layer_kernel, (jax.ShapeDtypeStruct((slots, 2 * D), BF), jax.S...  11.2 us
    pallas_call x1, Pallas kernels, backward(): call(backward_kernel, jax.ShapeDtypeStruct((slots, D), BF), [VMEM_SPEC] *...  8.9 us
    pallas_call x1, Pallas kernels, forward(): call(forward_kernel, tuple((jax.ShapeDtypeStruct(*shapes[i]) for i in (0,...  6.81 us
    pallas_call x1, Pallas kernels, per_device(): call(route_kernel, (jax.ShapeDtypeStruct((8, points), F32), jax.ShapeDtyp...  2.36 us
  transfers between devices with their start and end apart: 2, of which 2 were waited for; matrix products, arithmetic and copies ran while one was open for 0% of the time, Pallas kernels for 7%

profile of v5, /device:TPU:1, one launch (start us, length us, event | category | flops | bytes accessed | tf_op | source)
XLA Modules:
  0.0 115.4 jit_solution(9208355601654937838)
XLA Ops:
  0.0 2.4 %route.1 = (f32[8,256]{1,0:T(8,128)S(1)}, bf16[512,512]{1,0:T(8,128)(2,1)}) custom-call(s32[1]{0:T(128)} %bitcast.index_ref, s32[2,128,128]{2,1,0:T(8,128)} %bitcast.17, bf16[2,256,256]{2,1,0:T(8,128)(2,1)} %saved_hbm.3, bf16[256,256]{1,0:T(8,128)(2,1)} %g_hbm.1), custom_call_target="tpu_custom_call" | custom-call | tf_op jit(solution)/shard_map/route/pallas_call | solution.py:496
  2.4 13.2 %all-to-all-start = ((bf16[64,8,512]{2,1,0:T(8,128)(2,1)}), bf16[64,8,512]{2,1,0:T(8,128)(2,1)S(1)}, u32[]{:S(2)}, u32[]{:S(2)}) async-start(bf16[64,8,512]{2,1,0:T(8,128)(2,1)} %bitcast.2), calls=%async_computation | async-start | bytes 1048576 | tf_op jit(solution)/shard_map/all_to_all | solution.py:491
  15.5 1.6 %prefetch.1 = (s32[2,128,128]{2,1,0:T(8,128)S(1)}, bf16[256,256]{1,0:T(8,128)(2,1)S(1)}, bf16[256,768]{1,0:T(8,128)(2,1)S(1)}, bf16[256,256]{1,0:T(8,128)(2,1)S(...) custom-call(s32[2,128,128]{2,1,0:T(8,128)} %bitcast.18, bf16[2,256,256]{2,1,0:T(8,128)(2,1)} %saved_hbm.3, ...), custom_call_target="tpu_custom_call" | custom-call | tf_op jit(solution)/shard_map/prefetch/pallas_call | solution.py:416
  17.1 16.1 %all-to-all-done = bf16[64,8,512]{2,1,0:T(8,128)(2,1)S(1)} async-done(((bf16[64,8,512]{2,1,0:T(8,128)(2,1)}), bf16[64,8,512]{2,1,0:T(8,128)(2,1)S(1)}, u32[]{:S(2)}, u32[]{:S(2)}) %all-to-all-start) | async-done | bytes 524320 | tf_op jit(solution)/shard_map/all_to_all | solution.py:491
  33.2 11.2 %whole_layer.1 = (bf16[512,512]{1,0:T(8,128)(2,1)S(1)}, f32[8,256]{1,0:T(8,128)S(1)}) custom-call(s32[1]{0:T(128)} %bitcast.index_ref, bf16[512,512]{1,0:T(8,128)(2,1)S(1)} %bitcast.12, s32[2,128,128]{2,1,0:T(8,128)S(1)} %get-tuple-element.26.owners_ref, bf16[256,256]{1,0:T(8,128)(2,1)S(1)} %get-tuple-element.27.next_x_ref, ...), custom_call_target="tpu_custom_call" | custom-call | tf_op jit(solution)/shard_map/whole_layer/pallas_call | solution.py:428
  44.5 23.4 %all_to_all.20 = bf16[64,8,512]{2,1,0:T(8,128)(2,1)S(1)} all-to-all(bf16[64,8,512]{2,1,0:T(8,128)(2,1)S(1)} %bitcast.16), channel_id=1, replica_groups=mesh['blk'=64,'rep'=4] {'blk'}, dimensions={0} | all-to-all | bytes 1048576 | tf_op jit(solution)/shard_map/all_to_all | solution.py:491
  67.8 1.3 %repack.1 = bf16[512,256]{1,0:T(8,128)(2,1)} custom-call(f32[8,256]{1,0:T(8,128)S(1)} %get-tuple-element.25.rest_0_.dest_one_ref, f32[8,256]{1,0:T(8,128)S(1)} %get-tuple-element.32.dest_zero_ref.dest_ref, bf16[512,512]{1,0:T(8,128)(2,1)S(1)} %bitcast.10), custom_call_target="tpu_custom_call" | custom-call | tf_op jit(solution)/shard_map/repack/pallas_call | solution.py:513
  69.1 5.7 %all-to-all-start.2 = ((bf16[64,8,256]{2,1,0:T(8,128)(2,1)}), bf16[64,8,256]{2,1,0:T(8,128)(2,1)S(1)}, u32[]{:S(2)}, u32[]{:S(2)}) async-start(bf16[64,8,256]{2,1,0:T(8,128)(2,1)} %bitcast.6), calls=%async_computation.2 | async-start | bytes 524288 | tf_op jit(solution)/shard_map/all_to_all | solution.py:491
  74.8 6.8 %layer_forward.1 = (bf16[512,256]{1,0:T(8,128)(2,1)S(1)}, f32[512,384]{1,0:T(8,128)S(1)}, f32[256,512]{1,0:T(8,128)S(1)}, bf16[256,1024]{1,0:T(8,128)(2,1)S(1)},...) custom-call(s32[1]{0:T(128)} %bitcast.index_ref, ...), custom_call_target="tpu_custom_call" | custom-call | tf_op jit(solution)/shard_map/layer_forward/pallas_call | solution.py:444
  81.6 6.3 %all-to-all-done.2 = bf16[64,8,256]{2,1,0:T(8,128)(2,1)S(1)} async-done(((bf16[64,8,256]{2,1,0:T(8,128)(2,1)}), bf16[64,8,256]{2,1,0:T(8,128)(2,1)S(1)}, u32[]{:S(2)}, u32[]{:S(2)}) %all-to-all-start.2) | async-done | bytes 262176 | tf_op jit(solution)/shard_map/all_to_all | solution.py:491
  87.9 8.9 %layer_backward.1 = bf16[512,256]{1,0:T(8,128)(2,1)S(1)} custom-call(bf16[512,256]{1,0:T(8,128)(2,1)S(1)} %bitcast.13, bf16[512,256]{1,0:T(8,128)(2,1)S(1)} %get-tuple-element.34.value_ref, f32[512,384]{1,0:T(8,128)S(1)} %get-tuple-element.35.norm_ref, f32[256,512]{1,0:T(8,128)S(1)} %get-tuple-element.36.mixed_t_ref, ...), custom_call_target="tpu_custom_call" | custom-call | tf_op jit(solution)/shard_map/layer_backward/pallas_call | solution.py:467
  96.8 17.6 %all_to_all.21 = bf16[64,8,256]{2,1,0:T(8,128)(2,1)S(1)} all-to-all(bf16[64,8,256]{2,1,0:T(8,128)(2,1)S(1)} %bitcast.14), channel_id=1, replica_groups=mesh['blk'=64,'rep'=4] {'blk'}, dimensions={0} | all-to-all | bytes 524288 | tf_op jit(solution)/shard_map/all_to_all | solution.py:491
  114.4 0.9 unpack.1
Async XLA Ops:
  2.4 30.9 %all-to-all-start = ((bf16[64,8,512]{2,1,0:T(8,128)(2,1)}), bf16[64,8,512]{2,1,0:T(8,128)(2,1)S(1)}, u32[]{:S(2)}, u32[]{:S(2)}) async-start(bf16[64,8,512]{2,1,0:T(8,128)(2,1)} %bitcast.2), calls=%async_computation | async-start | bytes 1048576 | tf_op jit(solution)/shard_map/all_to_all | solution.py:491
  69.1 18.8 %all-to-all-start.2 = ((bf16[64,8,256]{2,1,0:T(8,128)(2,1)}), bf16[64,8,256]{2,1,0:T(8,128)(2,1)S(1)}, u32[]{:S(2)}, u32[]{:S(2)}) async-start(bf16[64,8,256]{2,1,0:T(8,128)(2,1)} %bitcast.6), calls=%async_computation.2 | async-start | bytes 524288 | tf_op jit(solution)/shard_map/all_to_all | solution.py:491

commit v6 on v5

--- a/solution.py
+++ b/solution.py
@@ -70,9 +70,10 @@
 
 
 def route_kernel(
-    index_ref, owners_hbm, saved_hbm, g_hbm, dest_ref, out_ref, owners_ref, x_ref, g_ref, sem
+    index_ref, owners_hbm, saved_hbm, g_hbm, dest_ref, out_hbm,
+    owners_ref, x_ref, g_ref, packed_x_ref, packed_g_ref, sem, out_sem,
 ):
-    slots, points = out_ref.shape[0], g_hbm.shape[0]
+    slots, points = out_hbm.shape[0], g_hbm.shape[0]
     owners_in, x_in, g_in = fetch(
         sem, [(owners_hbm.at[1], owners_ref), (saved_hbm.at[1], x_ref), (g_hbm, g_ref)]
     )
@@ -81,14 +82,30 @@
     dest_ref[...] = jnp.broadcast_to(dest, dest_ref.shape)
     hot = one_hot(dest, slots)
     x_in.wait()
-    out_ref[:, :D] = mm(hot, x_ref[...]).astype(BF)
+    packed_x_ref[...] = mm(hot, x_ref[...]).astype(BF)
+    x_out = pltpu.make_async_copy(packed_x_ref, out_hbm.at[:, pl.ds(0, D)], out_sem.at[0])
+    x_out.start()
     g_in.wait()
-    out_ref[:, D:] = mm(hot, g_ref[...]).astype(BF)
-
-
-def repack_kernel(dest_one_ref, dest_zero_ref, rows_ref, out_ref):
+    packed_g_ref[...] = mm(hot, g_ref[...]).astype(BF)
+    g_out = pltpu.make_async_copy(packed_g_ref, out_hbm.at[:, pl.ds(D, D)], out_sem.at[1])
+    g_out.start()
+    x_out.wait()
+    g_out.wait()
+
+
+def repack_kernel(dest_one_ref, dest_zero_ref, rows_ref, out_hbm, packed_ref, sem):
     gradient = unpack(dest_one_ref[0:1, :], rows_ref[:, :D])
-    out_ref[...] = mm(one_hot(dest_zero_ref[0:1, :], out_ref.shape[0]), gradient).astype(BF)
+    slots = packed_ref.shape[0]
+    hot = one_hot(dest_zero_ref[0:1, :], slots)
+    copies = []
+    for part in range(2):
+        rows = pl.ds(part * (slots // 2), slots // 2)
+        at = slice(part * (slots // 2), (part + 1) * (slots // 2))
+        packed_ref[at, :] = mm(hot[at], gradient).astype(BF)
+        copies.append(pltpu.make_async_copy(packed_ref.at[rows], out_hbm.at[rows], sem.at[part]))
+        copies[part].start()
+    for copy in copies:
+        copy.wait()
 
 
 def unpack_kernel(dest_ref, rows_ref, out_ref):
@@ -272,11 +289,11 @@
 
 def forward_kernel(index_ref, rx_ref, owners_hbm, *rest):
     attend_hbm, output_hbm, up_hbm, down_hbm = rest[:4]
-    value_ref, norm_ref, mixed_t_ref, up_ref, down_ref = rest[4:9]
-    probs_out, x_out, query_out, key_out = rest[9:13]
-    attend_ref, output_ref, probs_ref, query_t_ref, key_t_ref = rest[13:18]
-    work = rest[18:26]
-    owners_ref, in_sem, probs_sem, out_sem = rest[26:]
+    norm_ref, mixed_t_ref, attend_ref, output_ref, up_ref, down_ref = rest[4:10]
+    probs_out, x_out, value_out, query_out, key_out = rest[10:15]
+    probs_ref, value_ref, query_t_ref, key_t_ref = rest[15:19]
+    work = rest[19:27]
+    owners_ref, in_sem, probs_sem, out_sem = rest[27:]
     my = index_ref[0]
     slots = rx_ref.shape[0]
     copies = fetch(
@@ -306,48 +323,34 @@
         (value_ref, query_t_ref, key_t_ref, probs_ref, norm_ref, mixed_t_ref),
         work, wait, lambda head: probs_copy(head).start(), 1,
     )
-    for copy in copies[3:] + fetch(out_sem, [(query_t_ref, query_out), (key_t_ref, key_out)]):
+    for copy in copies[3:] + fetch(
+        out_sem, [(value_ref, value_out), (query_t_ref, query_out), (key_t_ref, key_out)]
+    ):
         copy.wait()
     for head in range(HEADS):
         probs_copy(head).wait()
 
 
 def backward_kernel(
-    g_ref, value_ref, norm_ref, mixed_t_ref, up_ref, down_ref, probs_hbm,
-    x_hbm, query_hbm, key_hbm, attend_hbm, output_hbm,
+    g_ref, norm_ref, mixed_t_ref, attend_ref, output_ref, up_ref, down_ref,
+    probs_hbm, x_hbm, value_hbm, query_hbm, key_hbm,
     out_ref,
-    attend_ref, output_ref, x_ref, probs_ref, query_t_ref, key_t_ref, *rest,
+    x_ref, probs_ref, value_ref, query_t_ref, key_t_ref, *rest,
 ):
-    work, (sem, probs_sem) = rest[:5], rest[5:]
-    pairs = [(output_hbm.at[0], output_ref), (query_hbm, query_t_ref), (key_hbm, key_t_ref)]
-    pairs += [(attend_hbm.at[0], attend_ref), (x_hbm, x_ref)]
-    copies = [pltpu.make_async_copy(a, b, sem.at[i]) for i, (a, b) in enumerate(pairs)]
-    for copy in copies[:3]:
-        copy.start()
-    order = dict(output=0, attend=3, x=4)
-
-    def probs_copy(head):
-        return pltpu.make_async_copy(probs_hbm.at[head], probs_ref.at[head], probs_sem.at[head])
-
-    for head in range(HEADS):
-        probs_copy(head).start()
-    for copy in copies[3:]:
-        copy.start()
-
-    def wait(name):
-        if name in order:
-            copies[order[name]].wait()
+    work, sem = rest[:5], rest[5]
+    pairs = [(value_hbm, value_ref), (query_hbm, query_t_ref), (key_hbm, key_t_ref)]
+    pairs += [(x_hbm, x_ref)]
+    pairs += [(probs_hbm.at[head], probs_ref.at[head]) for head in range(HEADS)]
+    copies = fetch(sem, pairs)
 
     def before_heads():
-        copies[1].wait()
-        copies[2].wait()
-        for head in range(HEADS):
-            probs_copy(head).wait()
+        for copy in copies:
+            copy.wait()
 
     out_ref[...] = backward_part(
         x_ref, g_ref[...], (attend_ref, output_ref, up_ref, down_ref),
         (value_ref, query_t_ref, key_t_ref, probs_ref, norm_ref, mixed_t_ref),
-        work, wait, before_heads,
+        work, lambda name: None, before_heads,
     )
 
 
@@ -369,10 +372,6 @@
         ((slots, D + LANES), F32),
         ((D, slots), F32),
     ]
-
-
-def weight_scratch(weights):
-    return [pltpu.VMEM(w.shape[1:], BF) for w in weights]
 
 
 def forward_scratch(slots):
@@ -440,41 +439,37 @@
 def forward(my_index, rx, owners, weights):
     slots = rx.shape[0]
     shapes = kept_shapes(slots)
-    attend, output, up, down = weights
     return call(
         forward_kernel,
-        tuple(jax.ShapeDtypeStruct(*shapes[i]) for i in (0, 4, 5))
-        + tuple(jax.ShapeDtypeStruct(w.shape[1:], BF) for w in (up, down))
-        + tuple(pltpu.HBM(*k) for k in (shapes[3], shapes[0], shapes[1], shapes[2])),
+        tuple(jax.ShapeDtypeStruct(*shapes[i]) for i in (4, 5))
+        + tuple(jax.ShapeDtypeStruct(w.shape[1:], BF) for w in weights)
+        + tuple(pltpu.HBM(*k) for k in (shapes[3], shapes[0], shapes[0], shapes[1], shapes[2])),
         [SMEM_SPEC, VMEM_SPEC] + [HBM_SPEC] * 5,
-        (VMEM_SPEC,) * 5 + (HBM_SPEC,) * 4,
-        weight_scratch((attend, output))
-        + [pltpu.VMEM(*shapes[i]) for i in (3, 1, 2)]
+        (VMEM_SPEC,) * 6 + (HBM_SPEC,) * 5,
+        [pltpu.VMEM(*shapes[i]) for i in (3, 0, 1, 2)]
         + forward_scratch(slots)
         + [
             pltpu.VMEM(owners.shape[1:], jnp.int32),
             pltpu.SemaphoreType.DMA((6,)),
             pltpu.SemaphoreType.DMA((HEADS,)),
-            pltpu.SemaphoreType.DMA((2,)),
+            pltpu.SemaphoreType.DMA((3,)),
         ],
         "layer_forward",
     )(my_index, rx, owners, *weights)
 
 
-def backward(g, kept, weights):
+def backward(g, kept, hidden):
     slots = g.shape[0]
-    attend, output, up, _ = weights
     return call(
         backward_kernel,
         jax.ShapeDtypeStruct((slots, D), BF),
-        [VMEM_SPEC] * 6 + [HBM_SPEC] * 6,
+        [VMEM_SPEC] * 7 + [HBM_SPEC] * 5,
         VMEM_SPEC,
-        weight_scratch((attend, output))
-        + [pltpu.VMEM(*kept_shapes(slots)[i]) for i in (0, 3, 1, 2)]
-        + backward_scratch(slots, up.shape[2])
-        + [pltpu.SemaphoreType.DMA((5,)), pltpu.SemaphoreType.DMA((HEADS,))],
+        [pltpu.VMEM(*kept_shapes(slots)[i]) for i in (0, 3, 0, 1, 2)]
+        + backward_scratch(slots, hidden)
+        + [pltpu.SemaphoreType.DMA((4 + HEADS,))],
         "layer_backward",
-    )(g, *kept[:5], *(in_hbm(k) for k in kept[5:]), attend, output)
+    )(g, *kept[:6], *(in_hbm(k) for k in kept[6:]))
 
 
 def per_device(saved_inputs, output_grads, owner_ids, attend, output, up, down):
@@ -495,14 +490,17 @@
 
     dest_one, packed = call(
         route_kernel,
-        (jax.ShapeDtypeStruct((8, points), F32), jax.ShapeDtypeStruct((slots, 2 * D), BF)),
+        (jax.ShapeDtypeStruct((8, points), F32), pltpu.HBM((slots, 2 * D), BF)),
         [SMEM_SPEC] + [HBM_SPEC] * 3,
-        (VMEM_SPEC, VMEM_SPEC),
+        (VMEM_SPEC, HBM_SPEC),
         [
             pltpu.VMEM(owners.shape[1:], jnp.int32),
             pltpu.VMEM((points, D), BF),
             pltpu.VMEM((points, D), BF),
+            pltpu.VMEM((slots, D), BF),
+            pltpu.VMEM((slots, D), BF),
             pltpu.SemaphoreType.DMA((3,)),
+            pltpu.SemaphoreType.DMA((2,)),
         ],
         "route",
     )(my_index, owners, saved_inputs, output_grads)
@@ -511,11 +509,16 @@
     result, dest_zero = whole_layer(my_index, xg, *fetched[:2], fetched[2:])
     rx = exchange(result)
     packed = call(
-        repack_kernel, jax.ShapeDtypeStruct((slots, D), BF), [VMEM_SPEC] * 3, VMEM_SPEC, [], "repack"
+        repack_kernel,
+        pltpu.HBM((slots, D), BF),
+        [VMEM_SPEC] * 3,
+        HBM_SPEC,
+        [pltpu.VMEM((slots, D), BF), pltpu.SemaphoreType.DMA((2,))],
+        "repack",
     )(dest_one, dest_zero, rx)
     g_zero = exchange(packed)
     kept = forward(my_index, rx, owners, weights)
-    result = backward(g_zero, kept, weights)
+    result = backward(g_zero, kept, up.shape[2])
     return call(
         unpack_kernel, jax.ShapeDtypeStruct((points, D), BF), [VMEM_SPEC] * 2, VMEM_SPEC, [], "unpack"
     )(dest_zero, exchange(result))

time: 116 us -> 117 us (level)
  local copies, waits for them, and re-layouts: 0 us -> 1.55 us
    unnamed x0 -> x4, local copies, waits for them, and re-layouts: none -> 1.55 us
where the time goes in v6:
time: 117 us; the launch traced here: 116 us
  blocking collectives  41.1 us (35%)
  Pallas kernels  33 us (28%)
  waiting for transfers between devices  21.6 us (18%)
  starting transfers between devices  18.9 us (16%)
  local copies, waits for them, and re-layouts  1.55 us (1%)
    all_to_all x2, blocking collectives, exchange(): lax.all_to_all(rows.reshape(devices, 8, width), 'blk', split_axis=0, conc...  41.1 us
    all_to_all x2, waiting for transfers between devices, exchange(): lax.all_to_all(rows.reshape(devices, 8, width), 'blk', split_axis=0, conc...  21.6 us
    all_to_all x2, starting transfers between devices, exchange(): lax.all_to_all(rows.reshape(devices, 8, width), 'blk', split_axis=0, conc...  18.9 us
    pallas_call x1, Pallas kernels, whole_layer(): call(whole_layer_kernel, (jax.ShapeDtypeStruct((slots, 2 * D), BF), jax.S...  11.3 us
    pallas_call x1, Pallas kernels, backward(): call(backward_kernel, jax.ShapeDtypeStruct((slots, D), BF), [VMEM_SPEC] *...  8.73 us
    pallas_call x1, Pallas kernels, forward(): call(forward_kernel, tuple((jax.ShapeDtypeStruct(*shapes[i]) for i in (4,...  6.98 us
  transfers between devices with their start and end apart: 2, of which 2 were waited for; matrix products, arithmetic and copies ran while one was open for 0% of the time, Pallas kernels for 7%

profile of v6, /device:TPU:1, one launch (start us, length us, event | category | flops | bytes accessed | tf_op | source)
XLA Modules:
  0.0 116.1 jit_solution(2089588419599686530)
XLA Ops:
  0.0 2.3 %route.1 = (f32[8,256]{1,0:T(8,128)S(1)}, bf16[512,512]{1,0:T(8,128)(2,1)}) custom-call(s32[1]{0:T(128)} %bitcast.index_ref, s32[2,128,128]{2,1,0:T(8,128)} %bitcast.17, bf16[2,256,256]{2,1,0:T(8,128)(2,1)} %saved_hbm.3, bf16[256,256]{1,0:T(8,128)(2,1)} %g_hbm.1), custom_call_target="tpu_custom_call" | custom-call | tf_op jit(solution)/shard_map/route/pallas_call | solution.py:491
  2.3 13.2 %all-to-all-start = ((bf16[64,8,512]{2,1,0:T(8,128)(2,1)}), bf16[64,8,512]{2,1,0:T(8,128)(2,1)S(1)}, u32[]{:S(2)}, u32[]{:S(2)}) async-start(bf16[64,8,512]{2,1,0:T(8,128)(2,1)} %bitcast.21), calls=%async_computation | async-start | bytes 1048576 | tf_op jit(solution)/shard_map/all_to_all | solution.py:486
  15.5 1.6 %prefetch.1 = (s32[2,128,128]{2,1,0:T(8,128)S(1)}, bf16[256,256]{1,0:T(8,128)(2,1)S(1)}, bf16[256,768]{1,0:T(8,128)(2,1)S(1)}, bf16[256,256]{1,0:T(8,128)(2,1)S(...) custom-call(s32[2,128,128]{2,1,0:T(8,128)} %bitcast.18, bf16[2,256,256]{2,1,0:T(8,128)(2,1)} %saved_hbm.3, ...), custom_call_target="tpu_custom_call" | custom-call | tf_op jit(solution)/shard_map/prefetch/pallas_call | solution.py:415
  17.0 16.1 %all-to-all-done = bf16[64,8,512]{2,1,0:T(8,128)(2,1)S(1)} async-done(((bf16[64,8,512]{2,1,0:T(8,128)(2,1)}), bf16[64,8,512]{2,1,0:T(8,128)(2,1)S(1)}, u32[]{:S(2)}, u32[]{:S(2)}) %all-to-all-start) | async-done | bytes 524320 | tf_op jit(solution)/shard_map/all_to_all | solution.py:486
  33.1 11.3 %whole_layer.1 = (bf16[512,512]{1,0:T(8,128)(2,1)S(1)}, f32[8,256]{1,0:T(8,128)S(1)}) custom-call(s32[1]{0:T(128)} %bitcast.index_ref, bf16[512,512]{1,0:T(8,128)(2,1)S(1)} %bitcast.12, s32[2,128,128]{2,1,0:T(8,128)S(1)} %get-tuple-element.28.owners_ref, bf16[256,256]{1,0:T(8,128)(2,1)S(1)} %get-tuple-element.29.next_x_ref, ...), custom_call_target="tpu_custom_call" | custom-call | tf_op jit(solution)/shard_map/whole_layer/pallas_call | solution.py:427
  44.4 23.4 %all_to_all.20 = bf16[64,8,512]{2,1,0:T(8,128)(2,1)S(1)} all-to-all(bf16[64,8,512]{2,1,0:T(8,128)(2,1)S(1)} %bitcast.16), channel_id=1, replica_groups=mesh['blk'=64,'rep'=4] {'blk'}, dimensions={0} | all-to-all | bytes 1048576 | tf_op jit(solution)/shard_map/all_to_all | solution.py:486
  67.8 1.2 %repack.1 = bf16[512,256]{1,0:T(8,128)(2,1)} custom-call(f32[8,256]{1,0:T(8,128)S(1)} %get-tuple-element.27.rest_0_.dest_one_ref, f32[8,256]{1,0:T(8,128)S(1)} %get-tuple-element.34.dest_zero_ref.dest_ref, bf16[512,512]{1,0:T(8,128)(2,1)S(1)} %bitcast.10), custom_call_target="tpu_custom_call" | custom-call | tf_op jit(solution)/shard_map/repack/pallas_call | solution.py:511
  69.0 5.7 %all-to-all-start.2 = ((bf16[64,8,256]{2,1,0:T(8,128)(2,1)}), bf16[64,8,256]{2,1,0:T(8,128)(2,1)S(1)}, u32[]{:S(2)}, u32[]{:S(2)}) async-start(bf16[64,8,256]{2,1,0:T(8,128)(2,1)} %bitcast.20), calls=%async_computation.2 | async-start | bytes 524288 | tf_op jit(solution)/shard_map/all_to_all | solution.py:486
  74.7 7.0 %layer_forward.1 = (f32[512,384]{1,0:T(8,128)S(1)}, f32[256,512]{1,0:T(8,128)S(1)}, bf16[256,768]{1,0:T(8,128)(2,1)S(1)}, bf16[256,256]{1,0:T(8,128)(2,1)S(1)}, ...) custom-call(s32[1]{0:T(128)} %bitcast.index_ref, ...), custom_call_target="tpu_custom_call" | custom-call | tf_op jit(solution)/shard_map/layer_forward/pallas_call | solution.py:442
  81.7 0.0 copy-start
  81.7 0.6 copy-done
  82.4 5.4 %all-to-all-done.2 = bf16[64,8,256]{2,1,0:T(8,128)(2,1)S(1)} async-done(((bf16[64,8,256]{2,1,0:T(8,128)(2,1)}), bf16[64,8,256]{2,1,0:T(8,128)(2,1)S(1)}, u32[]{:S(2)}, u32[]{:S(2)}) %all-to-all-start.2) | async-done | bytes 262176 | tf_op jit(solution)/shard_map/all_to_all | solution.py:486
  87.8 0.0 copy-start.1
  87.8 0.9 copy-done.1
  88.7 8.7 %layer_backward.1 = bf16[512,256]{1,0:T(8,128)(2,1)S(1)} custom-call(bf16[512,256]{1,0:T(8,128)(2,1)S(1)} %bitcast.13, f32[512,384]{1,0:T(8,128)S(1)} %get-tuple-element.36.norm_ref, f32[256,512]{1,0:T(8,128)S(1)} %get-tuple-element.37.mixed_t_ref, bf16[256,768]{1,0:T(8,128)(2,1)S(1)} %get-tuple-element.38.attend_ref, bf16[256,256]{1,0:T(8,128)(2,1)S(1)} %copy-done.1, ...), custom_call_target="tpu_custom_call" | custom-call | tf_op jit(solution)/shard_map/layer_backward/pallas_call | solution.py:463
  97.4 17.8 %all_to_all.21 = bf16[64,8,256]{2,1,0:T(8,128)(2,1)S(1)} all-to-all(bf16[64,8,256]{2,1,0:T(8,128)(2,1)S(1)} %bitcast.14), channel_id=1, replica_groups=mesh['blk'=64,'rep'=4] {'blk'}, dimensions={0} | all-to-all | bytes 524288 | tf_op jit(solution)/shard_map/all_to_all | solution.py:486
  115.2 0.9 unpack.1
Async XLA Ops:
  2.3 30.9 %all-to-all-start = ((bf16[64,8,512]{2,1,0:T(8,128)(2,1)}), bf16[64,8,512]{2,1,0:T(8,128)(2,1)S(1)}, u32[]{:S(2)}, u32[]{:S(2)}) async-start(bf16[64,8,512]{2,1,0:T(8,128)(2,1)} %bitcast.21), calls=%async_computation | async-start | bytes 1048576 | tf_op jit(solution)/shard_map/all_to_all | solution.py:486
  69.0 18.8 %all-to-all-start.2 = ((bf16[64,8,256]{2,1,0:T(8,128)(2,1)}), bf16[64,8,256]{2,1,0:T(8,128)(2,1)S(1)}, u32[]{:S(2)}, u32[]{:S(2)}) async-start(bf16[64,8,256]{2,1,0:T(8,128)(2,1)} %bitcast.20), calls=%async_computation.2 | async-start | bytes 524288 | tf_op jit(solution)/shard_map/all_to_all | solution.py:486
  81.7 0.7 copy-start
  87.8 0.9 copy-start.1

commit v7 on v6

--- a/solution.py
+++ b/solution.py
@@ -289,9 +289,9 @@
 
 def forward_kernel(index_ref, rx_ref, owners_hbm, *rest):
     attend_hbm, output_hbm, up_hbm, down_hbm = rest[:4]
-    norm_ref, mixed_t_ref, attend_ref, output_ref, up_ref, down_ref = rest[4:10]
-    probs_out, x_out, value_out, query_out, key_out = rest[10:15]
-    probs_ref, value_ref, query_t_ref, key_t_ref = rest[15:19]
+    norm_ref, mixed_t_ref, output_ref, up_ref, down_ref = rest[4:9]
+    probs_out, x_out, value_out, query_out, key_out = rest[9:14]
+    attend_ref, probs_ref, value_ref, query_t_ref, key_t_ref = rest[14:19]
     work = rest[19:27]
     owners_ref, in_sem, probs_sem, out_sem = rest[27:]
     my = index_ref[0]
@@ -332,15 +332,16 @@
 
 
 def backward_kernel(
-    g_ref, norm_ref, mixed_t_ref, attend_ref, output_ref, up_ref, down_ref,
-    probs_hbm, x_hbm, value_hbm, query_hbm, key_hbm,
+    g_ref, norm_ref, mixed_t_ref, output_ref, up_ref, down_ref,
+    probs_hbm, x_hbm, value_hbm, query_hbm, key_hbm, attend_hbm,
     out_ref,
-    x_ref, probs_ref, value_ref, query_t_ref, key_t_ref, *rest,
+    attend_ref, x_ref, probs_ref, value_ref, query_t_ref, key_t_ref, *rest,
 ):
     work, sem = rest[:5], rest[5]
     pairs = [(value_hbm, value_ref), (query_hbm, query_t_ref), (key_hbm, key_t_ref)]
     pairs += [(x_hbm, x_ref)]
     pairs += [(probs_hbm.at[head], probs_ref.at[head]) for head in range(HEADS)]
+    pairs.append((attend_hbm.at[0], attend_ref))
     copies = fetch(sem, pairs)
 
     def before_heads():
@@ -442,11 +443,12 @@
     return call(
         forward_kernel,
         tuple(jax.ShapeDtypeStruct(*shapes[i]) for i in (4, 5))
-        + tuple(jax.ShapeDtypeStruct(w.shape[1:], BF) for w in weights)
+        + tuple(jax.ShapeDtypeStruct(w.shape[1:], BF) for w in weights[1:])
         + tuple(pltpu.HBM(*k) for k in (shapes[3], shapes[0], shapes[0], shapes[1], shapes[2])),
         [SMEM_SPEC, VMEM_SPEC] + [HBM_SPEC] * 5,
-        (VMEM_SPEC,) * 6 + (HBM_SPEC,) * 5,
-        [pltpu.VMEM(*shapes[i]) for i in (3, 0, 1, 2)]
+        (VMEM_SPEC,) * 5 + (HBM_SPEC,) * 5,
+        [pltpu.VMEM(weights[0].shape[1:], BF)]
+        + [pltpu.VMEM(*shapes[i]) for i in (3, 0, 1, 2)]
         + forward_scratch(slots)
         + [
             pltpu.VMEM(owners.shape[1:], jnp.int32),
@@ -458,18 +460,19 @@
     )(my_index, rx, owners, *weights)
 
 
-def backward(g, kept, hidden):
-    slots = g.shape[0]
+def backward(g, kept, weights):
+    slots, hidden = g.shape[0], weights[2].shape[2]
     return call(
         backward_kernel,
         jax.ShapeDtypeStruct((slots, D), BF),
-        [VMEM_SPEC] * 7 + [HBM_SPEC] * 5,
+        [VMEM_SPEC] * 6 + [HBM_SPEC] * 6,
         VMEM_SPEC,
-        [pltpu.VMEM(*kept_shapes(slots)[i]) for i in (0, 3, 0, 1, 2)]
+        [pltpu.VMEM(weights[0].shape[1:], BF)]
+        + [pltpu.VMEM(*kept_shapes(slots)[i]) for i in (0, 3, 0, 1, 2)]
         + backward_scratch(slots, hidden)
-        + [pltpu.SemaphoreType.DMA((4 + HEADS,))],
+        + [pltpu.SemaphoreType.DMA((5 + HEADS,))],
         "layer_backward",
-    )(g, *kept[:6], *(in_hbm(k) for k in kept[6:]))
+    )(g, *kept[:5], *(in_hbm(k) for k in kept[5:]), weights[0])
 
 
 def per_device(saved_inputs, output_grads, owner_ids, attend, output, up, down):
@@ -518,7 +521,7 @@
     )(dest_one, dest_zero, rx)
     g_zero = exchange(packed)
     kept = forward(my_index, rx, owners, weights)
-    result = backward(g_zero, kept, up.shape[2])
+    result = backward(g_zero, kept, weights)
     return call(
         unpack_kernel, jax.ShapeDtypeStruct((points, D), BF), [VMEM_SPEC] * 2, VMEM_SPEC, [], "unpack"
     )(dest_zero, exchange(result))

time: 117 us -> 116 us (level)
  local copies, waits for them, and re-layouts: 1.55 us -> 0 us
    unnamed x4 -> x0, local copies, waits for them, and re-layouts: 1.55 us -> none
where the time goes in v7:
time: 116 us; the launch traced here: 115 us
  blocking collectives  41 us (35%)
  Pallas kernels  33.1 us (29%)
  waiting for transfers between devices  22.2 us (19%)
  starting transfers between devices  18.9 us (16%)
    all_to_all x2, blocking collectives, exchange(): lax.all_to_all(rows.reshape(devices, 8, width), 'blk', split_axis=0, conc...  41 us
    all_to_all x2, waiting for transfers between devices, exchange(): lax.all_to_all(rows.reshape(devices, 8, width), 'blk', split_axis=0, conc...  22.2 us
    all_to_all x2, starting transfers between devices, exchange(): lax.all_to_all(rows.reshape(devices, 8, width), 'blk', split_axis=0, conc...  18.9 us
    pallas_call x1, Pallas kernels, whole_layer(): call(whole_layer_kernel, (jax.ShapeDtypeStruct((slots, 2 * D), BF), jax.S...  11.3 us
    pallas_call x1, Pallas kernels, backward(): call(backward_kernel, jax.ShapeDtypeStruct((slots, D), BF), [VMEM_SPEC] *...  8.84 us
    pallas_call x1, Pallas kernels, forward(): call(forward_kernel, tuple((jax.ShapeDtypeStruct(*shapes[i]) for i in (4,...  6.96 us
  transfers between devices with their start and end apart: 2, of which 2 were waited for; matrix products, arithmetic and copies ran while one was open for 0% of the time, Pallas kernels for 7%

profile of v7, /device:TPU:1, one launch (start us, length us, event | category | flops | bytes accessed | tf_op | source)
XLA Modules:
  0.0 115.2 jit_solution(13753231457392593292)
XLA Ops:
  0.0 2.3 %route.1 = (f32[8,256]{1,0:T(8,128)S(1)}, bf16[512,512]{1,0:T(8,128)(2,1)}) custom-call(s32[1]{0:T(128)} %bitcast.index_ref, s32[2,128,128]{2,1,0:T(8,128)} %bitcast.17, bf16[2,256,256]{2,1,0:T(8,128)(2,1)} %saved_hbm.3, bf16[256,256]{1,0:T(8,128)(2,1)} %g_hbm.1), custom_call_target="tpu_custom_call" | custom-call | tf_op jit(solution)/shard_map/route/pallas_call | solution.py:494
  2.3 13.2 %all-to-all-start = ((bf16[64,8,512]{2,1,0:T(8,128)(2,1)}), bf16[64,8,512]{2,1,0:T(8,128)(2,1)S(1)}, u32[]{:S(2)}, u32[]{:S(2)}) async-start(bf16[64,8,512]{2,1,0:T(8,128)(2,1)} %bitcast.21), calls=%async_computation | async-start | bytes 1048576 | tf_op jit(solution)/shard_map/all_to_all | solution.py:489
  15.5 1.6 %prefetch.1 = (s32[2,128,128]{2,1,0:T(8,128)S(1)}, bf16[256,256]{1,0:T(8,128)(2,1)S(1)}, bf16[256,768]{1,0:T(8,128)(2,1)S(1)}, bf16[256,256]{1,0:T(8,128)(2,1)S(...) custom-call(s32[2,128,128]{2,1,0:T(8,128)} %bitcast.18, bf16[2,256,256]{2,1,0:T(8,128)(2,1)} %saved_hbm.3, ...), custom_call_target="tpu_custom_call" | custom-call | tf_op jit(solution)/shard_map/prefetch/pallas_call | solution.py:416
  17.0 16.1 %all-to-all-done = bf16[64,8,512]{2,1,0:T(8,128)(2,1)S(1)} async-done(((bf16[64,8,512]{2,1,0:T(8,128)(2,1)}), bf16[64,8,512]{2,1,0:T(8,128)(2,1)S(1)}, u32[]{:S(2)}, u32[]{:S(2)}) %all-to-all-start) | async-done | bytes 524320 | tf_op jit(solution)/shard_map/all_to_all | solution.py:489
  33.1 11.3 %whole_layer.1 = (bf16[512,512]{1,0:T(8,128)(2,1)S(1)}, f32[8,256]{1,0:T(8,128)S(1)}) custom-call(s32[1]{0:T(128)} %bitcast.index_ref, bf16[512,512]{1,0:T(8,128)(2,1)S(1)} %bitcast.12, s32[2,128,128]{2,1,0:T(8,128)S(1)} %get-tuple-element.27.owners_ref, bf16[256,256]{1,0:T(8,128)(2,1)S(1)} %get-tuple-element.28.next_x_ref, ...), custom_call_target="tpu_custom_call" | custom-call | tf_op jit(solution)/shard_map/whole_layer/pallas_call | solution.py:428
  44.4 23.4 %all_to_all.20 = bf16[64,8,512]{2,1,0:T(8,128)(2,1)S(1)} all-to-all(bf16[64,8,512]{2,1,0:T(8,128)(2,1)S(1)} %bitcast.16), channel_id=1, replica_groups=mesh['blk'=64,'rep'=4] {'blk'}, dimensions={0} | all-to-all | bytes 1048576 | tf_op jit(solution)/shard_map/all_to_all | solution.py:489
  67.8 1.2 %repack.1 = bf16[512,256]{1,0:T(8,128)(2,1)} custom-call(f32[8,256]{1,0:T(8,128)S(1)} %get-tuple-element.26.rest_0_.dest_one_ref, f32[8,256]{1,0:T(8,128)S(1)} %get-tuple-element.33.dest_zero_ref.dest_ref, bf16[512,512]{1,0:T(8,128)(2,1)S(1)} %bitcast.10), custom_call_target="tpu_custom_call" | custom-call | tf_op jit(solution)/shard_map/repack/pallas_call | solution.py:514
  69.0 5.7 %all-to-all-start.2 = ((bf16[64,8,256]{2,1,0:T(8,128)(2,1)}), bf16[64,8,256]{2,1,0:T(8,128)(2,1)S(1)}, u32[]{:S(2)}, u32[]{:S(2)}) async-start(bf16[64,8,256]{2,1,0:T(8,128)(2,1)} %bitcast.20), calls=%async_computation.2 | async-start | bytes 524288 | tf_op jit(solution)/shard_map/all_to_all | solution.py:489
  74.7 7.0 %layer_forward.1 = (f32[512,384]{1,0:T(8,128)S(1)}, f32[256,512]{1,0:T(8,128)S(1)}, bf16[256,256]{1,0:T(8,128)(2,1)S(1)}, bf16[256,1024]{1,0:T(8,128)(2,1)S(1)},...) custom-call(s32[1]{0:T(128)} %bitcast.index_ref, ...), custom_call_target="tpu_custom_call" | custom-call | tf_op jit(solution)/shard_map/layer_forward/pallas_call | solution.py:443
  81.7 6.1 %all-to-all-done.2 = bf16[64,8,256]{2,1,0:T(8,128)(2,1)S(1)} async-done(((bf16[64,8,256]{2,1,0:T(8,128)(2,1)}), bf16[64,8,256]{2,1,0:T(8,128)(2,1)S(1)}, u32[]{:S(2)}, u32[]{:S(2)}) %all-to-all-start.2) | async-done | bytes 262176 | tf_op jit(solution)/shard_map/all_to_all | solution.py:489
  87.8 8.8 %layer_backward.1 = bf16[512,256]{1,0:T(8,128)(2,1)S(1)} custom-call(bf16[512,256]{1,0:T(8,128)(2,1)S(1)} %bitcast.13, f32[512,384]{1,0:T(8,128)S(1)} %get-tuple-element.35.norm_ref, f32[256,512]{1,0:T(8,128)S(1)} %get-tuple-element.36.mixed_t_ref, bf16[256,256]{1,0:T(8,128)(2,1)S(1)} %get-tuple-element.37.output_ref, ...), custom_call_target="tpu_custom_call" | custom-call | tf_op jit(solution)/shard_map/layer_backward/pallas_call | solution.py:465
  96.6 17.7 %all_to_all.21 = bf16[64,8,256]{2,1,0:T(8,128)(2,1)S(1)} all-to-all(bf16[64,8,256]{2,1,0:T(8,128)(2,1)S(1)} %bitcast.14), channel_id=1, replica_groups=mesh['blk'=64,'rep'=4] {'blk'}, dimensions={0} | all-to-all | bytes 524288 | tf_op jit(solution)/shard_map/all_to_all | solution.py:489
  114.3 0.9 unpack.1
Async XLA Ops:
  2.3 30.9 %all-to-all-start = ((bf16[64,8,512]{2,1,0:T(8,128)(2,1)}), bf16[64,8,512]{2,1,0:T(8,128)(2,1)S(1)}, u32[]{:S(2)}, u32[]{:S(2)}) async-start(bf16[64,8,512]{2,1,0:T(8,128)(2,1)} %bitcast.21), calls=%async_computation | async-start | bytes 1048576 | tf_op jit(solution)/shard_map/all_to_all | solution.py:489
  69.0 18.8 %all-to-all-start.2 = ((bf16[64,8,256]{2,1,0:T(8,128)(2,1)}), bf16[64,8,256]{2,1,0:T(8,128)(2,1)S(1)}, u32[]{:S(2)}, u32[]{:S(2)}) async-start(bf16[64,8,256]{2,1,0:T(8,128)(2,1)} %bitcast.20), calls=%async_computation.2 | async-start | bytes 524288 | tf_op jit(solution)/shard_map/all_to_all | solution.py:489

commit v8 on v5

--- a/solution.py
+++ b/solution.py
@@ -70,20 +70,27 @@
 
 
 def route_kernel(
-    index_ref, owners_hbm, saved_hbm, g_hbm, dest_ref, out_ref, owners_ref, x_ref, g_ref, sem
+    index_ref, owners_hbm, saved_hbm, g_hbm, *rest
 ):
+    weights_hbm, (dest_ref, out_ref, all_owners_ref, next_x_ref), rest = rest[:4], rest[4:8], rest[8:]
+    weights, (x_ref, g_ref, sem) = rest[:4], rest[4:]
     slots, points = out_ref.shape[0], g_hbm.shape[0]
-    owners_in, x_in, g_in = fetch(
-        sem, [(owners_hbm.at[1], owners_ref), (saved_hbm.at[1], x_ref), (g_hbm, g_ref)]
+    owners_in, x_in, g_in, *others = fetch(
+        sem,
+        [(owners_hbm, all_owners_ref), (saved_hbm.at[1], x_ref), (g_hbm, g_ref)]
+        + [(saved_hbm.at[0], next_x_ref)]
+        + [(hbm.at[1], ref) for hbm, ref in zip(weights_hbm, weights)],
     )
     owners_in.wait()
-    dest = destination_row(owners_ref, index_ref[0], points)
+    dest = destination_row(all_owners_ref.at[1], index_ref[0], points)
     dest_ref[...] = jnp.broadcast_to(dest, dest_ref.shape)
     hot = one_hot(dest, slots)
     x_in.wait()
     out_ref[:, :D] = mm(hot, x_ref[...]).astype(BF)
     g_in.wait()
     out_ref[:, D:] = mm(hot, g_ref[...]).astype(BF)
+    for copy in others:
+        copy.wait()
 
 
 def repack_kernel(dest_one_ref, dest_zero_ref, rows_ref, out_ref):
@@ -236,17 +243,6 @@
     return (grad_mid.astype(F32) + branch.astype(F32)).astype(BF)
 
 
-def prefetch_kernel(owners_hbm, saved_hbm, *rest):
-    weights_hbm, (owners_ref, next_x_ref), weights = rest[1:5], rest[5:7], rest[7:11]
-    copies = fetch(
-        rest[11],
-        [(owners_hbm, owners_ref), (saved_hbm.at[0], next_x_ref)]
-        + [(hbm.at[1], ref) for hbm, ref in zip(weights_hbm, weights)],
-    )
-    for copy in copies:
-        copy.wait()
-
-
 def whole_layer_kernel(index_ref, xg_ref, owners_ref, next_x_ref, *rest):
     weights, (out_ref, dest_ref), rest = rest[:4], rest[4:6], rest[6:]
     kept, forward_work, backward_work = rest[:6], rest[6:14], rest[14:19]
@@ -408,19 +404,6 @@
         name=name,
         compiler_params=pltpu.CompilerParams(vmem_limit_bytes=40 << 20),
     )
-
-
-def prefetch(after, owners, saved_inputs, weights):
-    shapes = [(owners.shape, jnp.int32), (saved_inputs.shape[1:], BF)]
-    shapes += [(w.shape[1:], BF) for w in weights]
-    return call(
-        prefetch_kernel,
-        tuple(jax.ShapeDtypeStruct(*k) for k in shapes),
-        [HBM_SPEC] * 2 + [VMEM_SPEC] + [HBM_SPEC] * 4,
-        (VMEM_SPEC,) * 6,
-        [pltpu.SemaphoreType.DMA((6,))],
-        "prefetch",
-    )(owners, saved_inputs, after, *weights)
 
 
 def whole_layer(my_index, xg, owners, next_x, weights):
@@ -493,21 +476,22 @@
         )
         return moved.reshape(slots, width)
 
-    dest_one, packed = call(
+    fetched_shapes = [(owners.shape, jnp.int32), ((points, D), BF)]
+    fetched_shapes += [(w.shape[1:], BF) for w in weights]
+    dest_one, packed, *fetched = call(
         route_kernel,
-        (jax.ShapeDtypeStruct((8, points), F32), jax.ShapeDtypeStruct((slots, 2 * D), BF)),
-        [SMEM_SPEC] + [HBM_SPEC] * 3,
-        (VMEM_SPEC, VMEM_SPEC),
+        (jax.ShapeDtypeStruct((8, points), F32), jax.ShapeDtypeStruct((slots, 2 * D), BF))
+        + tuple(jax.ShapeDtypeStruct(*k) for k in fetched_shapes),
+        [SMEM_SPEC] + [HBM_SPEC] * 7,
+        (VMEM_SPEC,) * 8,
         [
-            pltpu.VMEM(owners.shape[1:], jnp.int32),
             pltpu.VMEM((points, D), BF),
             pltpu.VMEM((points, D), BF),
-            pltpu.SemaphoreType.DMA((3,)),
+            pltpu.SemaphoreType.DMA((8,)),
         ],
         "route",
-    )(my_index, owners, saved_inputs, output_grads)
+    )(my_index, owners, saved_inputs, output_grads, *weights)
     xg = exchange(packed)
-    fetched = prefetch(dest_one, owners, saved_inputs, weights)
     result, dest_zero = whole_layer(my_index, xg, *fetched[:2], fetched[2:])
     rx = exchange(result)
     packed = call(

time: 116 us -> 115 us (level)
  blocking collectives: 41 us -> 71.6 us
  waiting for transfers between devices: 22.4 us -> 6.24 us
  starting transfers between devices: 18.8 us -> 5.69 us
  Pallas kernels: 33.1 us -> 30.9 us
    all_to_all x2 -> x3, blocking collectives: 41 us -> 71.6 us  [exchange(): lax.all_to_all(rows.reshape(devices, 8, width), 'blk', split_axis=0, conc...]
    all_to_all x2 -> x1, waiting for transfers between devices: 22.4 us -> 6.24 us  [exchange(): lax.all_to_all(rows.reshape(devices, 8, width), 'blk', split_axis=0, conc...]
    all_to_all x2 -> x1, starting transfers between devices: 18.8 us -> 5.69 us  [exchange(): lax.all_to_all(rows.reshape(devices, 8, width), 'blk', split_axis=0, conc...]
    pallas_call x1 -> x0, Pallas kernels: 1.55 us -> none  [prefetch(): call(prefetch_kernel, tuple((jax.ShapeDtypeStruct(*k) for k in shapes)),...]
  transfers between devices with their start and end apart: 2 -> 1, of which waited for: 2 -> 1; matrix products, arithmetic and copies ran while one was open for 0% -> 0% of each run, Pallas kernels for 7% -> 6%
where the time goes in v8:
time: 115 us
  blocking collectives  71.6 us (62%)
  Pallas kernels  30.9 us (27%)
  waiting for transfers between devices  6.24 us (5%)
  starting transfers between devices  5.69 us (5%)
    all_to_all x3, blocking collectives, exchange(): lax.all_to_all(rows.reshape(devices, 8, width), 'blk', split_axis=0, conc...  71.6 us
    pallas_call x1, Pallas kernels, whole_layer(): call(whole_layer_kernel, (jax.ShapeDtypeStruct((slots, 2 * D), BF), jax.S...  11.3 us
    pallas_call x1, Pallas kernels, backward(): call(backward_kernel, jax.ShapeDtypeStruct((slots, D), BF), [VMEM_SPEC] *...  8.9 us
    pallas_call x1, Pallas kernels, forward(): call(forward_kernel, tuple((jax.ShapeDtypeStruct(*shapes[i]) for i in (0,...  6.83 us
    all_to_all x1, waiting for transfers between devices, exchange(): lax.all_to_all(rows.reshape(devices, 8, width), 'blk', split_axis=0, conc...  6.24 us
    all_to_all x1, starting transfers between devices, exchange(): lax.all_to_all(rows.reshape(devices, 8, width), 'blk', split_axis=0, conc...  5.69 us
  transfers between devices with their start and end apart: 1, of which 1 were waited for; matrix products, arithmetic and copies ran while one was open for 0% of the time, Pallas kernels for 6%

profile of v8, /device:TPU:1, one launch (start us, length us, event | category | flops | bytes accessed | tf_op | source)
XLA Modules:
  0.0 114.5 jit_solution(13078845443167379600)
XLA Ops:
  0.0 1.7 %route.1 = (f32[8,256]{1,0:T(8,128)S(1)}, bf16[512,512]{1,0:T(8,128)(2,1)S(1)}, s32[2,128,128]{2,1,0:T(8,128)S(1)}, bf16[256,256]{1,0:T(8,128)(2,1)S(1)}, bf16[2...) custom-call(s32[1]{0:T(128)} %bitcast.index_ref, ...), custom_call_target="tpu_custom_call" | custom-call | tf_op jit(solution)/shard_map/route/pallas_call | solution.py:481
  1.7 30.6 %all_to_all.20 = bf16[64,8,512]{2,1,0:T(8,128)(2,1)S(1)} all-to-all(bf16[64,8,512]{2,1,0:T(8,128)(2,1)S(1)} %bitcast.17), channel_id=1, replica_groups=mesh['blk'=64,'rep'=4] {'blk'}, dimensions={0} | all-to-all | bytes 1048576 | tf_op jit(solution)/shard_map/all_to_all | solution.py:474
  32.3 11.3 %whole_layer.1 = (bf16[512,512]{1,0:T(8,128)(2,1)S(1)}, f32[8,256]{1,0:T(8,128)S(1)}) custom-call(s32[1]{0:T(128)} %bitcast.index_ref, bf16[512,512]{1,0:T(8,128)(2,1)S(1)} %bitcast.12, s32[2,128,128]{2,1,0:T(8,128)S(1)} %get-tuple-element.25.owners_ref, bf16[256,256]{1,0:T(8,128)(2,1)S(1)} %get-tuple-element.26.next_x_ref, ...), custom_call_target="tpu_custom_call" | custom-call | tf_op jit(solution)/shard_map/whole_layer/pallas_call | solution.py:411
  43.6 23.4 %all_to_all.21 = bf16[64,8,512]{2,1,0:T(8,128)(2,1)S(1)} all-to-all(bf16[64,8,512]{2,1,0:T(8,128)(2,1)S(1)} %bitcast.16), channel_id=1, replica_groups=mesh['blk'=64,'rep'=4] {'blk'}, dimensions={0} | all-to-all | bytes 1048576 | tf_op jit(solution)/shard_map/all_to_all | solution.py:474
  67.0 1.3 %repack.1 = bf16[512,256]{1,0:T(8,128)(2,1)} custom-call(f32[8,256]{1,0:T(8,128)S(1)} %get-tuple-element.32.dest_one_ref, f32[8,256]{1,0:T(8,128)S(1)} %get-tuple-element.31.dest_zero_ref.dest_ref, bf16[512,512]{1,0:T(8,128)(2,1)S(1)} %bitcast.10), custom_call_target="tpu_custom_call" | custom-call | tf_op jit(solution)/shard_map/repack/pallas_call | solution.py:497
  68.3 5.7 %all-to-all-start.2 = ((bf16[64,8,256]{2,1,0:T(8,128)(2,1)}), bf16[64,8,256]{2,1,0:T(8,128)(2,1)S(1)}, u32[]{:S(2)}, u32[]{:S(2)}) async-start(bf16[64,8,256]{2,1,0:T(8,128)(2,1)} %bitcast.6), calls=%async_computation.2 | async-start | bytes 524288 | tf_op jit(solution)/shard_map/all_to_all | solution.py:474
  74.0 6.8 %layer_forward.1 = (bf16[512,256]{1,0:T(8,128)(2,1)S(1)}, f32[512,384]{1,0:T(8,128)S(1)}, f32[256,512]{1,0:T(8,128)S(1)}, bf16[256,1024]{1,0:T(8,128)(2,1)S(1)},...) custom-call(s32[1]{0:T(128)} %bitcast.index_ref, ...), custom_call_target="tpu_custom_call" | custom-call | tf_op jit(solution)/shard_map/layer_forward/pallas_call | solution.py:427
  80.8 6.2 %all-to-all-done.2 = bf16[64,8,256]{2,1,0:T(8,128)(2,1)S(1)} async-done(((bf16[64,8,256]{2,1,0:T(8,128)(2,1)}), bf16[64,8,256]{2,1,0:T(8,128)(2,1)S(1)}, u32[]{:S(2)}, u32[]{:S(2)}) %all-to-all-start.2) | async-done | bytes 262176 | tf_op jit(solution)/shard_map/all_to_all | solution.py:474
  87.0 8.9 %layer_backward.1 = bf16[512,256]{1,0:T(8,128)(2,1)S(1)} custom-call(bf16[512,256]{1,0:T(8,128)(2,1)S(1)} %bitcast.13, bf16[512,256]{1,0:T(8,128)(2,1)S(1)} %get-tuple-element.34.value_ref, f32[512,384]{1,0:T(8,128)S(1)} %get-tuple-element.35.norm_ref, f32[256,512]{1,0:T(8,128)S(1)} %get-tuple-element.36.mixed_t_ref, ...), custom_call_target="tpu_custom_call" | custom-call | tf_op jit(solution)/shard_map/layer_backward/pallas_call | solution.py:450
  95.9 17.6 %all_to_all.22 = bf16[64,8,256]{2,1,0:T(8,128)(2,1)S(1)} all-to-all(bf16[64,8,256]{2,1,0:T(8,128)(2,1)S(1)} %bitcast.14), channel_id=1, replica_groups=mesh['blk'=64,'rep'=4] {'blk'}, dimensions={0} | all-to-all | bytes 524288 | tf_op jit(solution)/shard_map/all_to_all | solution.py:474
  113.6 0.9 unpack.1
Async XLA Ops:
  68.3 18.8 %all-to-all-start.2 = ((bf16[64,8,256]{2,1,0:T(8,128)(2,1)}), bf16[64,8,256]{2,1,0:T(8,128)(2,1)S(1)}, u32[]{:S(2)}, u32[]{:S(2)}) async-start(bf16[64,8,256]{2,1,0:T(8,128)(2,1)} %bitcast.6), calls=%async_computation.2 | async-start | bytes 524288 | tf_op jit(solution)/shard_map/all_to_all | solution.py:474

commit v9 on v8

--- a/solution.py
+++ b/solution.py
@@ -93,9 +93,19 @@
         copy.wait()
 
 
-def repack_kernel(dest_one_ref, dest_zero_ref, rows_ref, out_ref):
+def repack_kernel(dest_one_ref, dest_zero_ref, rows_ref, out_hbm, packed_ref, sem):
     gradient = unpack(dest_one_ref[0:1, :], rows_ref[:, :D])
-    out_ref[...] = mm(one_hot(dest_zero_ref[0:1, :], out_ref.shape[0]), gradient).astype(BF)
+    slots = packed_ref.shape[0]
+    hot = one_hot(dest_zero_ref[0:1, :], slots)
+    copies = []
+    for part in range(2):
+        rows = pl.ds(part * (slots // 2), slots // 2)
+        at = slice(part * (slots // 2), (part + 1) * (slots // 2))
+        packed_ref[at, :] = mm(hot[at], gradient).astype(BF)
+        copies.append(pltpu.make_async_copy(packed_ref.at[rows], out_hbm.at[rows], sem.at[part]))
+        copies[part].start()
+    for copy in copies:
+        copy.wait()
 
 
 def unpack_kernel(dest_ref, rows_ref, out_ref):
@@ -495,7 +505,12 @@
     result, dest_zero = whole_layer(my_index, xg, *fetched[:2], fetched[2:])
     rx = exchange(result)
     packed = call(
-        repack_kernel, jax.ShapeDtypeStruct((slots, D), BF), [VMEM_SPEC] * 3, VMEM_SPEC, [], "repack"
+        repack_kernel,
+        pltpu.HBM((slots, D), BF),
+        [VMEM_SPEC] * 3,
+        HBM_SPEC,
+        [pltpu.VMEM((slots, D), BF), pltpu.SemaphoreType.DMA((2,))],
+        "repack",
     )(dest_one, dest_zero, rx)
     g_zero = exchange(packed)
     kept = forward(my_index, rx, owners, weights)

time: 115 us -> 115 us (level)
  no operation moved by 1% of the time
where the time goes in v9:
time: 115 us
  blocking collectives  71.6 us (62%)
  Pallas kernels  30.9 us (27%)
  waiting for transfers between devices  6.24 us (5%)
  starting transfers between devices  5.7 us (5%)
    all_to_all x3, blocking collectives, exchange(): lax.all_to_all(rows.reshape(devices, 8, width), 'blk', split_axis=0, conc...  71.6 us
    pallas_call x1, Pallas kernels, whole_layer(): call(whole_layer_kernel, (jax.ShapeDtypeStruct((slots, 2 * D), BF), jax.S...  11.3 us
    pallas_call x1, Pallas kernels, backward(): call(backward_kernel, jax.ShapeDtypeStruct((slots, D), BF), [VMEM_SPEC] *...  8.94 us
    pallas_call x1, Pallas kernels, forward(): call(forward_kernel, tuple((jax.ShapeDtypeStruct(*shapes[i]) for i in (0,...  6.83 us
    all_to_all x1, waiting for transfers between devices, exchange(): lax.all_to_all(rows.reshape(devices, 8, width), 'blk', split_axis=0, conc...  6.24 us
    all_to_all x1, starting transfers between devices, exchange(): lax.all_to_all(rows.reshape(devices, 8, width), 'blk', split_axis=0, conc...  5.7 us
  transfers between devices with their start and end apart: 1, of which 1 were waited for; matrix products, arithmetic and copies ran while one was open for 0% of the time, Pallas kernels for 6%

profile of v9, /device:TPU:1, one launch (start us, length us, event | category | flops | bytes accessed | tf_op | source)
XLA Modules:
  0.0 114.6 jit_solution(6692587846970461751)
XLA Ops:
  0.0 1.7 %route.1 = (f32[8,256]{1,0:T(8,128)S(1)}, bf16[512,512]{1,0:T(8,128)(2,1)S(1)}, s32[2,128,128]{2,1,0:T(8,128)S(1)}, bf16[256,256]{1,0:T(8,128)(2,1)S(1)}, bf16[2...) custom-call(s32[1]{0:T(128)} %bitcast.index_ref, ...), custom_call_target="tpu_custom_call" | custom-call | tf_op jit(solution)/shard_map/route/pallas_call | solution.py:491
  1.7 30.6 %all_to_all.20 = bf16[64,8,512]{2,1,0:T(8,128)(2,1)S(1)} all-to-all(bf16[64,8,512]{2,1,0:T(8,128)(2,1)S(1)} %bitcast.17), channel_id=1, replica_groups=mesh['blk'=64,'rep'=4] {'blk'}, dimensions={0} | all-to-all | bytes 1048576 | tf_op jit(solution)/shard_map/all_to_all | solution.py:484
  32.3 11.3 %whole_layer.1 = (bf16[512,512]{1,0:T(8,128)(2,1)S(1)}, f32[8,256]{1,0:T(8,128)S(1)}) custom-call(s32[1]{0:T(128)} %bitcast.index_ref, bf16[512,512]{1,0:T(8,128)(2,1)S(1)} %bitcast.12, s32[2,128,128]{2,1,0:T(8,128)S(1)} %get-tuple-element.25.owners_ref, bf16[256,256]{1,0:T(8,128)(2,1)S(1)} %get-tuple-element.26.next_x_ref, ...), custom_call_target="tpu_custom_call" | custom-call | tf_op jit(solution)/shard_map/whole_layer/pallas_call | solution.py:421
  43.7 23.4 %all_to_all.21 = bf16[64,8,512]{2,1,0:T(8,128)(2,1)S(1)} all-to-all(bf16[64,8,512]{2,1,0:T(8,128)(2,1)S(1)} %bitcast.16), channel_id=1, replica_groups=mesh['blk'=64,'rep'=4] {'blk'}, dimensions={0} | all-to-all | bytes 1048576 | tf_op jit(solution)/shard_map/all_to_all | solution.py:484
  67.0 1.2 %repack.1 = bf16[512,256]{1,0:T(8,128)(2,1)} custom-call(f32[8,256]{1,0:T(8,128)S(1)} %get-tuple-element.32.dest_one_ref, f32[8,256]{1,0:T(8,128)S(1)} %get-tuple-element.31.dest_zero_ref.dest_ref, bf16[512,512]{1,0:T(8,128)(2,1)S(1)} %bitcast.10), custom_call_target="tpu_custom_call" | custom-call | tf_op jit(solution)/shard_map/repack/pallas_call | solution.py:507
  68.3 5.7 %all-to-all-start.2 = ((bf16[64,8,256]{2,1,0:T(8,128)(2,1)}), bf16[64,8,256]{2,1,0:T(8,128)(2,1)S(1)}, u32[]{:S(2)}, u32[]{:S(2)}) async-start(bf16[64,8,256]{2,1,0:T(8,128)(2,1)} %bitcast.18), calls=%async_computation.2 | async-start | bytes 524288 | tf_op jit(solution)/shard_map/all_to_all | solution.py:484
  74.0 6.8 %layer_forward.1 = (bf16[512,256]{1,0:T(8,128)(2,1)S(1)}, f32[512,384]{1,0:T(8,128)S(1)}, f32[256,512]{1,0:T(8,128)S(1)}, bf16[256,1024]{1,0:T(8,128)(2,1)S(1)},...) custom-call(s32[1]{0:T(128)} %bitcast.index_ref, ...), custom_call_target="tpu_custom_call" | custom-call | tf_op jit(solution)/shard_map/layer_forward/pallas_call | solution.py:437
  80.8 6.2 %all-to-all-done.2 = bf16[64,8,256]{2,1,0:T(8,128)(2,1)S(1)} async-done(((bf16[64,8,256]{2,1,0:T(8,128)(2,1)}), bf16[64,8,256]{2,1,0:T(8,128)(2,1)S(1)}, u32[]{:S(2)}, u32[]{:S(2)}) %all-to-all-start.2) | async-done | bytes 262176 | tf_op jit(solution)/shard_map/all_to_all | solution.py:484
  87.0 8.9 %layer_backward.1 = bf16[512,256]{1,0:T(8,128)(2,1)S(1)} custom-call(bf16[512,256]{1,0:T(8,128)(2,1)S(1)} %bitcast.13, bf16[512,256]{1,0:T(8,128)(2,1)S(1)} %get-tuple-element.34.value_ref, f32[512,384]{1,0:T(8,128)S(1)} %get-tuple-element.35.norm_ref, f32[256,512]{1,0:T(8,128)S(1)} %get-tuple-element.36.mixed_t_ref, ...), custom_call_target="tpu_custom_call" | custom-call | tf_op jit(solution)/shard_map/layer_backward/pallas_call | solution.py:460
  96.0 17.7 %all_to_all.22 = bf16[64,8,256]{2,1,0:T(8,128)(2,1)S(1)} all-to-all(bf16[64,8,256]{2,1,0:T(8,128)(2,1)S(1)} %bitcast.14), channel_id=1, replica_groups=mesh['blk'=64,'rep'=4] {'blk'}, dimensions={0} | all-to-all | bytes 524288 | tf_op jit(solution)/shard_map/all_to_all | solution.py:484
  113.6 0.9 unpack.1
Async XLA Ops:
  68.3 18.8 %all-to-all-start.2 = ((bf16[64,8,256]{2,1,0:T(8,128)(2,1)}), bf16[64,8,256]{2,1,0:T(8,128)(2,1)S(1)}, u32[]{:S(2)}, u32[]{:S(2)}) async-start(bf16[64,8,256]{2,1,0:T(8,128)(2,1)} %bitcast.18), calls=%async_computation.2 | async-start | bytes 524288 | tf_op jit(solution)/shard_map/all_to_all | solution.py:484
